TPU v7x, 128 devices: a whole 4x4x4 slice. The times are simulated.
128 devices in a mesh: nodes: 16 (over x_hi, y, core), feat: 8 (over x_lo, z).
Axes of the slice: x: 4 (x_hi: 2, x_lo: 2; x = x_hi * 2 + x_lo), y: 4, z: 4, core: 2. Of those that a mesh axis runs over, the one named last changes fastest.
Arguments:
- feats: bfloat16 [131072, 128], P('nodes', 'feat'), may hold values from -6 to 6
- tiles: bfloat16 [16, 16, 32, 128, 128], P('nodes'), may hold values from -0.25 to 0.25
- dst_block: int32 [16, 16, 32], P('nodes'), may hold values from 0 to 63
- src_block: int32 [16, 16, 32], P('nodes'), may hold values from 0 to 63
- tile_counts: int32 [16, 16], P('nodes'), may hold values from 1 to 32, as said below
- norm: float32 [131072], P('nodes'), may hold values from 0.3 to 3
- weight: bfloat16 [128, 256], P('feat'), may hold values from -0.5 to 0.5
- bias: float32 [256], P('feat'), may hold values from -3 to 3
- cotangent: bfloat16 [131072, 256], P('nodes', 'feat'), may hold values from -6 to 6
Outputs:
- hidden: bfloat16 [131072, 256], P('nodes', 'feat')
- grad_weight: float32 [128, 256], P('feat')
- grad_bias: float32 [256], P('feat')
- grad_feats: float32 [131072, 128], P('nodes', 'feat')
Inputs may be any that keep to these rules, and one draw needn't show every extreme that they name: Slots at or past tile_counts[o, p] hold no tile; one source slab has 32 tiles from every owner slab in every draw.
All inputs are finite; a program needn't handle non-finite values.
Results may differ from a plain program's by a relative error of at most 0.0075.
Values may be sent and summed in bfloat16 or wider, within the bound.
No kernel may reach another device: no remote copies, remote signals or barrier semaphores. Data moves between devices by JAX's collectives and lax.ppermute only.
A program may use at most 128 MiB of HBM per device.

v0:
```python
import jax
import jax.numpy as jnp
from jax import lax
from jax.sharding import PartitionSpec as P


def silu_slope(pre):
    sigma = jax.nn.sigmoid(pre)
    return sigma * (1.0 + pre * (1.0 - sigma))


def on_device(feats, tiles, dst_block, src_block, tile_counts, norm, weight, bias, cotangent):
    highest = lax.Precision.HIGHEST
    rows_dev = feats.shape[0]
    tile_size = tiles.shape[-1]
    block_count = rows_dev // tile_size
    slot_count = tiles.shape[2]
    feat_local = feats.shape[1]
    own_tiles = tiles[0]
    own_dst = dst_block[0]
    own_src = src_block[0]
    own_counts = tile_counts[0]
    block_ids = jnp.arange(block_count, dtype=jnp.int32)
    slot_ids = jnp.arange(slot_count, dtype=jnp.int32)
    usable_slots = (slot_ids[None, :] < own_counts[:, None]).astype(jnp.float32)
    scaled = (norm[:, None] * feats.astype(jnp.float32)).astype(jnp.bfloat16)
    start_sum = jnp.zeros((block_count, tile_size, feat_local), jnp.float32)
    piece = lax.all_gather(scaled, "nodes", axis=0, tiled=True)
    shards = piece.reshape(piece.shape[0] // rows_dev, block_count, tile_size, feat_local)

    def add_one(position, inner):
        shard = lax.dynamic_index_in_dim(shards, position, 0, keepdims=False)
        tile_set = lax.dynamic_index_in_dim(own_tiles, position, 0, keepdims=False)
        sources = lax.dynamic_index_in_dim(own_src, position, 0, keepdims=False)
        targets = lax.dynamic_index_in_dim(own_dst, position, 0, keepdims=False)
        usable = lax.dynamic_index_in_dim(usable_slots, position, 0, keepdims=False)
        picked = shard[sources]
        product = jnp.einsum("cij,cjf->cif", tile_set, picked, preferred_element_type=jnp.float32)
        placing = (targets[:, None] == block_ids[None, :]).astype(jnp.float32) * usable[:, None]
        return inner + jnp.einsum("cb,cif->bif", placing, product, precision=highest)

    summed = lax.fori_loop(0, shards.shape[0], add_one, start_sum)
    aggregated = (norm[:, None] * summed.reshape(rows_dev, feat_local)).astype(jnp.bfloat16)
    partial_pre = jnp.dot(aggregated, weight, preferred_element_type=jnp.float32)
    pre = lax.psum_scatter(partial_pre, "feat", scatter_dimension=1, tiled=True) + bias
    hidden = jax.nn.silu(pre).astype(jnp.bfloat16)
    grad_pre = (cotangent.astype(jnp.float32) * silu_slope(pre)).astype(jnp.bfloat16)
    piece = lax.all_gather(grad_pre, "feat", axis=1, tiled=True)
    projected = lax.dot_general(
        piece, weight, (((1,), (1,)), ((), ())), preferred_element_type=jnp.float32
    )
    block = lax.dot_general(
        aggregated, piece, (((0,), (0,)), ((), ())), preferred_element_type=jnp.float32
    )
    projected, weight_part = (projected, block)
    scale = (rows_dev * lax.axis_size("nodes")) ** (-0.5)
    bias_part = jnp.sum(grad_pre, axis=0, dtype=jnp.float32)
    weight_sum, bias_sum = lax.psum((weight_part, bias_part), "nodes")
    grad_weight = weight_sum * scale
    grad_bias = bias_sum * scale
    back_scaled = (norm[:, None] * projected).astype(jnp.bfloat16)
    back_blocks = back_scaled.reshape(block_count, tile_size, feat_local)
    picked_back = back_blocks[own_dst]
    partial_back = (
        jnp.einsum("pcij,pcif->pcjf", own_tiles, picked_back, preferred_element_type=jnp.float32)
        * usable_slots[:, :, None, None]
    )
    sources = own_src
    placing = (sources[..., None] == block_ids).astype(jnp.float32)
    returned = lax.psum_scatter(
        jnp.einsum("pcb,pcjf->pbjf", placing, partial_back, precision=highest).reshape(
            rows_dev * lax.axis_size("nodes"), feat_local
        ),
        "nodes",
        scatter_dimension=0,
        tiled=True,
    )
    grad_feats = norm[:, None] * returned
    return (hidden, grad_weight, grad_bias, grad_feats)


def solution(mesh):
    return jax.shard_map(
        on_device,
        mesh=mesh,
        in_specs=(
            P("nodes", "feat"),
            P("nodes", None, None, None, None),
            P("nodes", None, None),
            P("nodes", None, None),
            P("nodes", None),
            P("nodes"),
            P("feat", None),
            P("feat"),
            P("nodes", "feat"),
        ),
        out_specs=(P("nodes", "feat"), P("feat", None), P("feat"), P("nodes", "feat")),
        check_vma=False,
    )
```

profile of v0, /device:TPU:0, one launch (start us, length us, event | category | flops | bytes accessed | tf_op | source)
XLA Modules:
  0.0 432.4 jit_solution(2135381942234439921)
XLA Ops:
  9.7 59.0 %all-gather.3.cloned.1.call-done = bf16[131072,16]{0,1:T(8,128)(2,1)} async-done(((bf16[8192,16]{0,1:T(8,128)(2,1)}), bf16[131072,16]{0,1:T(8,128)(2,1)}) %all-gather.3.cloned.1.call-update) | async-done | bytes 4194320 | tf_op jit(solution)/shard_map/all_gather | solution.py:28
  68.8 4.9 %copy.24 = bf16[2,8,1024,128]{3,2,1,0:T(8,128)(2,1)} copy(bf16[2,8,1024,128]{3,1,2,0:T(8,128)(2,1)} %bitcast.97) | data formatting | bytes 8388608
  73.7 72.4 %while.14 = (s32[]{:T(128)}, f32[64,128,16]{1,0,2:T(8,128)S(1)}, s32[16,32]{1,0:T(8,128)S(1)}, f32[16,32]{1,0:T(8,128)S(1)}, bf16[16,32,128,128]{3,2,1,0:T(8,128...) while((s32[]{:T(128)}, f32[64,128,16]{1,0,2:T(8,128)S(1)}, ...), condition=%wide.region_1.2_spmd.clone, body=%wide.region_0.1_spmd.clone.sunk | while | flops 67376224 | bytes 4068739 | solution.py:42
  75.6 1.9 fusion.54
  80.1 1.9 fusion.54
  84.6 1.9 fusion.54
  89.1 1.9 fusion.54
  93.7 1.9 fusion.54
  98.2 1.9 fusion.54
  102.7 1.9 fusion.54
  107.2 1.9 fusion.54
  111.8 1.9 fusion.54
  116.3 1.9 fusion.54
  120.8 1.9 fusion.54
  125.3 1.9 fusion.54
  129.9 1.9 fusion.54
  134.4 1.9 fusion.54
  138.9 1.9 fusion.54
  143.4 1.9 fusion.54
  146.1 4.5 %fusion.28 = f32[8192,256]{0,1:T(8,128)} fusion(bf16[16,256]{1,0:T(8,128)(2,1)S(1)} %copy-done, f32[2,8,64,128]{3,2,1,0:T(8,128)S(1)} %bitcast.94, f32[8192]{0:T(1024)S(1)} %copy-done.2), kind=kOutput, calls=%fused_computation.48 | convolution fusion | flops 67371008 | bytes 8953856 | tf_op jit(solution)/shard_map/dot_general | solution.py:44
  150.7 90.9 %reduce-scatter.3.cloned.1.call-done = f32[8192,32]{0,1:T(8,128)} async-done(((f32[8192,256]{0,1:T(8,128)}), f32[8192,32]{0,1:T(8,128)}) %reduce-scatter.3.cloned.1.call-update) | async-done | bytes 1048592 | tf_op jit(solution)/shard_map/reduce_scatter | solution.py:45
  241.6 2.9 convert_reduce_fusion
  244.7 51.5 %all-gather.5.cloned.1.call-done = bf16[8192,256]{0,1:T(8,128)(2,1)} async-done(((bf16[8192,32]{0,1:T(8,128)(2,1)}), bf16[8192,256]{0,1:T(8,128)(2,1)}) %all-gather.5.cloned.1.call-update) | async-done | bytes 4194320 | tf_op jit(solution)/shard_map/all_gather | solution.py:48
  296.1 2.8 fusion.21
  299.0 2.0 gather_fusion.1
  301.1 8.4 %fusion.31 = f32[16,32,16,128]{3,2,1,0:T(8,128)S(1)} fusion(bf16[16,32,128,16]{2,3,1,0:T(8,128)(2,1)S(1)} %bitcast.88, bf16[1,16,32,128,128]{4,3,2,1,0:T(8,128)(2,1)} %bitcast.91), kind=kOutput, calls=%fused_computation.55 | convolution fusion | flops 268435456 | bytes 23068672 | tf_op jit(solution)/shard_map/pcij,pcif->pcjf/dot_general | solution.py:65
  309.5 5.0 %fusion.18 = f32[16,64,128,16]{2,1,0,3:T(8,128)S(1)} fusion(s32[16,32]{1,0:T(8,128)S(1)} %get-tuple-element.291, f32[16,32,16,128]{3,2,1,0:T(8,128)S(1)} %fusion.31, f32[16,32]{1,0:T(8,128)S(1)} %get-tuple-element.290), kind=kOutput, calls=%fused_computation.30 | convolution fusion | flops 806387712 | bytes 12587008 | tf_op jit(solution)/shard_map/pcb,pcjf->pbjf/dot_general | solution.py:71
  314.6 8.1 %copy.43 = f32[2,8,1024,128]{3,1,2,0:T(8,128)} copy(f32[2,8,1024,128]{3,2,1,0:T(8,128)S(1)} %bitcast.93) | data formatting | bytes 16777216
  322.7 3.4 fusion.26
  326.1 69.7 %all-reduce = (f32[16,256]{1,0:T(8,128)S(1)}, f32[32]{0:T(128)S(1)}) all-reduce(f32[16,256]{1,0:T(8,128)S(1)} %fusion.26, f32[32]{0:T(128)S(1)} %get-tuple-element.200), channel_id=1, replica_groups=mesh['nodes'=16,'feat'=8] {'nodes'}, use_global_device_ids=true, to_apply=%region_3.4 | all-reduce | flops 4128 | bytes 33024 | tf_op jit(solution)/shard_map/psum | solution.py:58
  397.0 27.0 %reduce-scatter.5.cloned.1.call-done = f32[8192,16]{0,1:T(8,128)} async-done(((f32[131072,16]{0,1:T(8,128)}), f32[8192,16]{0,1:T(8,128)}) %reduce-scatter.5.cloned.1.call-update) | async-done | bytes 524304 | tf_op jit(solution)/shard_map/reduce_scatter | solution.py:70
  423.9 1.9 broadcast_multiply_fusion
  (159 shorter events, 45.5 us)
Async XLA Ops:
  7.2 139.0 %copy-start = (bf16[16,256]{1,0:T(8,128)(2,1)S(1)}, bf16[16,256]{1,0:T(8,128)(2,1)}, u32[]{:S(2)}) copy-start(bf16[16,256]{1,0:T(8,128)(2,1)} %param.17) | copy-start | bytes 24580
  7.2 61.6 %all-gather.3.cloned.1.call-start = ((), (), s32[]{:S(2)}) async-start(), calls=%async_computation.2 | async-start | bytes 4456448 | tf_op jit(solution)/shard_map/all_gather | solution.py:28
  9.0 232.7 %reduce-scatter.3.cloned.1.call-start = ((), (), s32[]{:S(2)}) async-start(), calls=%async_computation.3 | async-start | bytes 9437184 | tf_op jit(solution)/shard_map/reduce_scatter | solution.py:45
  68.8 4.9 %copy-start.4 = (s32[1,16,32]{2,1,0:T(8,128)S(1)}, s32[1,16,32]{2,1,0:T(8,128)}, u32[]{:S(2)}) copy-start(s32[1,16,32]{2,1,0:T(8,128)} %param.14) | copy-start | bytes 6148
  68.8 4.9 %copy-start.5 = (s32[1,16,32]{2,1,0:T(8,128)S(1)}, s32[1,16,32]{2,1,0:T(8,128)}, u32[]{:S(2)}) copy-start(s32[1,16,32]{2,1,0:T(8,128)} %param.13) | copy-start | bytes 6148
  73.7 72.4 %copy-start.2 = (f32[8192]{0:T(1024)S(1)}, f32[8192]{0:T(1024)}, u32[]{:S(2)}) copy-start(f32[8192]{0:T(1024)} %param.16) | copy-start | bytes 98308
  150.7 91.0 %copy-start.3 = (bf16[8192,32]{0,1:T(8,128)(2,1)S(1)}, bf16[8192,32]{0,1:T(8,128)(2,1)}, u32[]{:S(2)}) copy-start(bf16[8192,32]{0,1:T(8,128)(2,1)} %param.19) | copy-start | bytes 1572868
  150.7 91.0 %copy-start.6 = (f32[32]{0:T(128)S(1)}, f32[32]{0:T(128)}, u32[]{:S(2)}) copy-start(f32[32]{0:T(128)} %param.18) | copy-start | bytes 388
  150.7 145.5 %all-gather.5.cloned.1.call-start = ((), (), s32[]{:S(2)}) async-start(), calls=%async_computation.4 | async-start | bytes 4718592 | tf_op jit(solution)/shard_map/all_gather | solution.py:48
  244.5 179.4 %reduce-scatter.5.cloned.1.call-start = ((), (), s32[]{:S(2)}) async-start(), calls=%async_computation.5 | async-start | bytes 8912896 | tf_op jit(solution)/shard_map/reduce_scatter | solution.py:70
  322.7 103.1 %copy-start.1 = (bf16[16,256]{1,0:T(8,128)(2,1)S(1)}, bf16[16,256]{1,0:T(8,128)(2,1)}, u32[]{:S(2)}) copy-start(bf16[16,256]{1,0:T(8,128)(2,1)} %param.17) | copy-start | bytes 24580
Sparse Core Ops, SparseCore 0:
  11.1 57.6 all-gather.2
  150.8 90.7 reduce-scatter.2
  244.7 51.4 all-gather.4
  322.8 101.0 reduce-scatter.4
where the time goes:
time: 434 us; the launch traced here: 432 us
  waiting for transfers between devices  228 us (53%)
  blocking collectives  69.7 us (16%)
  matrix products  67 us (15%)
  local copies, waits for them, and re-layouts  43.6 us (10%)
  between operations  13.9 us (3%)
  other arithmetic  8.61 us (2%)
    reduce_scatter x1, waiting for transfers between devices, on_device(): lax.psum_scatter(partial_pre, 'feat', scatter_dimension=1, tiled=True)  90.9 us
    psum x1, blocking collectives, on_device(): weight_sum, bias_sum = lax.psum((weight_part, bias_part), 'nodes')  69.7 us
    all_gather x1, waiting for transfers between devices, on_device(): piece = lax.all_gather(scaled, 'nodes', axis=0, tiled=True)  59 us
    all_gather x1, waiting for transfers between devices, on_device(): piece = lax.all_gather(grad_pre, 'feat', axis=1, tiled=True)  51.5 us
    dot_general x16, matrix products, add_one(): jnp.einsum('cij,cjf->cif', tile_set, picked, preferred_element_type=jnp.f...  29.8 us
    reduce_scatter x1, waiting for transfers between devices, on_device(): lax.psum_scatter(jnp.einsum('pcb,pcjf->pbjf', placing, partial_back, prec...  27 us
    dynamic_slice x32, local copies, waits for them, and re-layouts, add_one(): shard = lax.dynamic_index_in_dim(shards, position, 0, keepdims=False)  18.5 us
    unnamed x16, local copies, waits for them, and re-layouts  13 us
  transfers between devices with their start and end apart: 4, of which 4 were waited for; matrix products, arithmetic and copies ran while one was open for 1% of the time, Pallas kernels for 0%

commit v1 on v0

v1 whole, which is shorter than its diff:
```python
import functools

import jax
import jax.numpy as jnp
from jax import lax
from jax.experimental import pallas as pl
from jax.experimental.pallas import tpu as pltpu
from jax.sharding import PartitionSpec as P

LANES = 128
UNROLL = 8
BF16 = jnp.bfloat16
F32 = jnp.float32


def vmem(*shape):
    return pl.BlockSpec(memory_space=pltpu.VMEM)


def smem():
    return pl.BlockSpec(memory_space=pltpu.SMEM)


def hbm():
    return pl.BlockSpec(memory_space=pl.ANY)


def prepare_kernel(feats, norm, cotangent, weight, bias, scaled, payload):
    blocks = scaled.shape[0]
    peers, slots = payload.shape[0], payload.shape[1]
    per_peer = blocks // peers
    for b in range(blocks):
        lanes = pl.ds(b * LANES, LANES)
        scaled[b] = (norm[pl.ds(b, 1), :] * feats[:, lanes].astype(F32)).astype(BF16)
        payload[b // per_peer, b % per_peer] = cotangent[:, lanes]
    w = jnp.concatenate([weight[:, :LANES], weight[:, LANES:]], axis=0)
    rest = bias[...]
    parts = []
    for _ in range(3):
        part = rest.astype(BF16)
        rest = rest - part.astype(F32)
        parts.append(part.astype(F32))
    row = lax.broadcasted_iota(jnp.int32, (payload.shape[2], LANES), 0)
    packed = jnp.where(row == 0, parts[0], jnp.where(row == 1, parts[1], jnp.where(row == 2, parts[2], 0.0)))
    packed = packed.astype(BF16)
    for g in range(peers):
        payload[g, per_peer] = w
        payload[g, per_peer + 1] = packed


def start_tiles(slabs, counts, tiles, buffer, sems, pieces):
    slots = tiles.shape[1]
    for k in range(pieces):
        slab = slabs[k]
        count = counts[slab]
        for chunk in range(slots // UNROLL):
            @pl.when(chunk * UNROLL < count)
            def _():
                pltpu.make_async_copy(
                    tiles.at[slab, pl.ds(chunk * UNROLL, UNROLL)],
                    buffer.at[k, pl.ds(chunk * UNROLL, UNROLL)],
                    sems.at[k, chunk],
                ).start()


def over_tiles(k, slab, count, tiles, buffer, sems, source_of, target_of, dims, accumulator):
    def step(chunk, carry):
        first = chunk * UNROLL
        pltpu.make_async_copy(
            tiles.at[slab, pl.ds(first, UNROLL)], buffer.at[k, pl.ds(first, UNROLL)], sems.at[k, chunk]
        ).wait()
        products = []
        for j in range(UNROLL):
            c = first + j
            r = lax.dot_general(source_of(c), buffer[k, c], (dims, ((), ())), preferred_element_type=F32)
            products.append(jnp.where(c < count, r, 0.0))
        for j in range(UNROLL):
            t = target_of(first + j)
            accumulator[t] = accumulator[t] + products[j]
        return carry

    lax.fori_loop(0, (count + UNROLL - 1) // UNROLL, step, 0)


def forward_kernel(pieces, first, last, slabs, counts, src, dst, *refs):
    refs = list(refs)
    xs = [refs.pop(0) for _ in range(pieces)]
    tiles = refs.pop(0)
    start = None if first else refs.pop(0)
    norm = refs.pop(0) if last else None
    out, buffer, sems = refs[0], refs[1], refs[2]
    acc = refs[3] if last else out
    start_tiles(slabs, counts, tiles, buffer, sems, pieces)
    for b in range(acc.shape[0]):
        acc[b] = jnp.zeros(acc.shape[1:], F32) if first else start[b]
    for k in range(pieces):
        slab = slabs[k]
        over_tiles(
            k, slab, counts[slab], tiles, buffer, sems,
            lambda c, slab=slab, k=k: xs[k][src[slab, c]],
            lambda c, slab=slab: dst[slab, c],
            ((1,), (1,)), acc,
        )
    if last:
        per_peer = out.shape[1]
        for b in range(acc.shape[0]):
            out[b // per_peer, b % per_peer] = (norm[pl.ds(b, 1), :] * acc[b]).astype(BF16)


def forward_call(xs, slabs, counts, src, dst, tiles, start, norm, peers):
    pieces = len(xs)
    first, last = start is None, norm is not None
    shape = xs[0].shape
    args = [slabs, counts, src, dst, *xs, tiles]
    specs = [smem()] * 4 + [vmem()] * pieces + [hbm()]
    if not first:
        args.append(start)
        specs.append(vmem())
    scratch = [
        pltpu.VMEM((pieces, *tiles.shape[1:]), BF16),
        pltpu.SemaphoreType.DMA((pieces, tiles.shape[1] // UNROLL)),
    ]
    if last:
        args.append(norm)
        specs.append(vmem())
        scratch.append(pltpu.VMEM(shape, F32))
        out = jax.ShapeDtypeStruct((peers, shape[0] // peers, *shape[1:]), BF16)
    else:
        out = jax.ShapeDtypeStruct(shape, F32)
    return pl.pallas_call(
        functools.partial(forward_kernel, pieces, first, last),
        out_shape=out, in_specs=specs, out_specs=vmem(), scratch_shapes=scratch,
        name="forward_tiles",
    )(*args)


def backward_kernel(pieces, added, kept, slabs, counts, src, dst, *refs):
    refs = list(refs)
    ys = refs.pop(0)
    tiles = refs.pop(0)
    adds = [refs.pop(0) for _ in range(pieces)] if added else None
    outs = [refs.pop(0) for _ in range(pieces)]
    buffer, sems, acc = refs
    per_peer = ys.shape[1]
    blocks = acc.shape[0]
    start_tiles(slabs, counts, tiles, buffer, sems, pieces)
    for k in range(pieces):
        slab = slabs[k]
        for b in range(blocks):
            acc[b] = adds[k][b].astype(F32) if added else jnp.zeros(acc.shape[1:], F32)

        def source_of(c, slab=slab):
            d = dst[slab, c]
            return ys[d // per_peer, d % per_peer]

        over_tiles(
            k, slab, counts[slab], tiles, buffer, sems, source_of,
            lambda c, slab=slab: src[slab, c], ((1,), (0,)), acc,
        )
        for b in range(blocks):
            outs[k][b] = acc[b].astype(outs[k].dtype)


def backward_call(ys, slabs, counts, src, dst, tiles, adds, kept, pieces):
    blocks = ys.shape[0] * ys.shape[1]
    shape = (blocks, *ys.shape[2:])
    added = adds is not None
    args = [slabs, counts, src, dst, ys, tiles] + (list(adds) if added else [])
    specs = [smem()] * 4 + [vmem(), hbm()] + [vmem()] * (pieces if added else 0)
    outs = [jax.ShapeDtypeStruct(shape, F32 if k == kept else BF16) for k in range(pieces)]
    return pl.pallas_call(
        functools.partial(backward_kernel, pieces, added, kept),
        out_shape=outs, in_specs=specs, out_specs=[vmem()] * pieces,
        scratch_shapes=[
            pltpu.VMEM((pieces, *tiles.shape[1:]), BF16),
            pltpu.SemaphoreType.DMA((pieces, tiles.shape[1] // UNROLL)),
            pltpu.VMEM(shape, F32),
        ],
        name="backward_tiles",
    )(*args)


def dense_kernel(place, agg, received, norm, hidden, back, grads):
    peers, blocks, feat_local = agg.shape[0], agg.shape[1], agg.shape[2]
    hid_local = hidden.shape[2]
    halves = received.shape[2] // feat_local
    weight = jnp.concatenate(
        [
            jnp.concatenate([received[g, blocks, pl.ds(h * feat_local, feat_local), :] for h in range(halves)], axis=1)
            for g in range(peers)
        ],
        axis=0,
    )
    bias_rows = []
    for g in range(peers):
        parts = received[g, blocks + 1].astype(F32)
        bias_rows.append((parts[0:1] + parts[1:2] + parts[2:3])[:, :hid_local])
    bias = jnp.concatenate(bias_rows, axis=1)
    bias = jnp.transpose(jnp.broadcast_to(bias, (8, bias.shape[1])))[:, 0:1]
    grad = jnp.zeros(grads.shape, F32)
    for b in range(blocks):
        agg_b = jnp.concatenate([agg[g, b] for g in range(peers)], axis=0)
        cot_b = jnp.concatenate([received[g, b] for g in range(peers)], axis=0).astype(F32)
        pre = lax.dot_general(weight, agg_b, (((0,), (0,)), ((), ())), preferred_element_type=F32) + bias
        sig = 1.0 / (1.0 + jnp.exp(-pre))
        hid = (pre * sig).astype(BF16)
        grad_pre = (cot_b * sig * (1.0 + pre * (1.0 - sig))).astype(BF16)
        back_b = jnp.dot(weight, grad_pre, preferred_element_type=F32)
        back_b = (norm[pl.ds(place[0] * blocks + b, 1), :] * back_b).astype(BF16)
        left = jnp.concatenate([agg_b, jnp.ones((8, LANES), BF16)], axis=0)
        grad = grad + lax.dot_general(left, grad_pre, (((1,), (1,)), ((), ())), preferred_element_type=F32)
        for g in range(peers):
            hidden[g, b] = hid[g * hid_local:(g + 1) * hid_local]
            back[g, b] = back_b[g * feat_local:(g + 1) * feat_local]
    grads[...] = grad


def finish_kernel(kept, norm, *refs):
    out = refs[-1]
    for b in range(kept.shape[0]):
        total = kept[b]
        for r in refs[:-1]:
            total = total + r[b].astype(F32)
        out[:, pl.ds(b * LANES, LANES)] = norm[pl.ds(b, 1), :] * total


def on_device(feats, tiles, dst_block, src_block, tile_counts, norm, weight, bias, cotangent):
    rows, feat_local = feats.shape
    tile = tiles.shape[-1]
    blocks = rows // tile
    hid = weight.shape[1]
    hid_local = cotangent.shape[1]
    peers = lax.axis_size("feat")
    slabs = lax.axis_size("nodes")
    per_peer = blocks // peers
    own_tiles, own_dst, own_src, own_counts = tiles[0], dst_block[0], src_block[0], tile_counts[0]
    norm_blocks = norm.reshape(blocks, tile)
    me = lax.axis_index("nodes")
    me_x, me_y, me_c = me // 8, (me // 2) % 4, me % 2
    place = lax.axis_index("feat").astype(jnp.int32).reshape(1)

    def slab_at(dx, dy, dc):
        return ((me_x + dx) % 2) * 8 + ((me_y + dy) % 4) * 2 + (me_c + dc) % 2

    def move(value, dx, dy, dc):
        pairs = []
        for i in range(slabs):
            x, y, c = i // 8, (i // 2) % 4, i % 2
            pairs.append((i, ((x + dx) % 2) * 8 + ((y + dy) % 4) * 2 + (c + dc) % 2))
        return lax.ppermute(value, "nodes", pairs)

    scaled, payload = pl.pallas_call(
        prepare_kernel,
        out_shape=(
            jax.ShapeDtypeStruct((blocks, feat_local, LANES), BF16),
            jax.ShapeDtypeStruct((peers, per_peer + 2, hid_local, LANES), BF16),
        ),
        name="prepare",
    )(
        feats.T, norm_blocks, cotangent.T, weight,
        jnp.pad(bias.reshape(1, hid_local), ((0, 0), (0, LANES - hid_local))),
    )
    hops = [(0, 0), (0, 1), (0, 3), (1, 0), (1, 1), (1, 3), (0, 2), (1, 2)]
    pieces = {}
    for dx, dy in hops:
        pieces[dx, dy] = scaled if (dx, dy) == (0, 0) else move(scaled, dx, dy, 0)
    received = lax.all_to_all(payload, "feat", 0, 0)
    start = None
    groups = [hops[:1], hops[1:4], hops[4:6], hops[6:]]
    for g, group in enumerate(groups):
        xs, ids = [], []
        for dx, dy in group:
            for dc in (0, 1):
                value = pieces[dx, dy]
                xs.append(move(value, 0, 0, 1) if dc else value)
                ids.append(slab_at(-dx, -dy, dc))
        start = forward_call(
            xs, jnp.stack(ids).astype(jnp.int32), own_counts, own_src, own_dst, own_tiles, start,
            norm_blocks if g == len(groups) - 1 else None, peers,
        )
    agg = lax.all_to_all(start, "feat", 0, 0)
    hidden, back, grads = pl.pallas_call(
        dense_kernel,
        out_shape=(
            jax.ShapeDtypeStruct((peers, per_peer, hid_local, LANES), BF16),
            jax.ShapeDtypeStruct((peers, per_peer, feat_local, LANES), BF16),
            jax.ShapeDtypeStruct((peers * feat_local + 8, hid), F32),
        ),
        in_specs=[smem(), vmem(), vmem(), vmem()],
        name="dense",
    )(place, agg, received, norm_blocks)
    back = lax.all_to_all(back, "feat", 0, 0)

    order = [(1, 2), (0, 2), (1, 1), (1, 3), (0, 1), (0, 3), (1, 0), (0, 0)]
    halves = [order[:4], order[4:]]
    swapped = []
    for half in halves:
        ids = jnp.stack([slab_at(dx, dy, 1) for dx, dy in half]).astype(jnp.int32)
        parts = backward_call(back, ids, own_counts, own_src, own_dst, own_tiles, None, None, len(half))
        swapped.append([move(p, 0, 0, 1) for p in parts])
    arrived, kept = [], None
    for half, adds in zip(halves, swapped):
        ids = jnp.stack([slab_at(dx, dy, 0) for dx, dy in half]).astype(jnp.int32)
        stay = half.index((0, 0)) if (0, 0) in half else None
        parts = backward_call(back, ids, own_counts, own_src, own_dst, own_tiles, adds, stay, len(half))
        for (dx, dy), p in zip(half, parts):
            if (dx, dy) == (0, 0):
                kept = p
            else:
                arrived.append(move(p, dx, dy, 0))

    hidden = lax.all_to_all(hidden, "feat", 0, 0)
    hidden = hidden.reshape(blocks, hid_local, LANES).transpose(1, 0, 2).reshape(hid_local, rows).T
    weight_part = grads[: peers * feat_local].reshape(peers, feat_local, hid)
    bias_part = jnp.broadcast_to(grads[peers * feat_local:], (peers, 8, hid))
    summed = jnp.sum(lax.all_to_all(jnp.concatenate([weight_part, bias_part], axis=1), "feat", 0, 0), axis=0)
    for i in range(4):
        pairs = []
        for n in range(slabs):
            x, y, c = n // 8, (n // 2) % 4, n % 2
            c, y, x = (c ^ 1, y, x) if i == 0 else (c, y ^ 1, x) if i == 1 else (c, 3 - y, x) if i == 2 else (c, y, x ^ 1)
            pairs.append((n, x * 8 + y * 2 + c))
        summed = summed + lax.ppermute(summed, "nodes", pairs)
    summed = summed * (rows * slabs) ** (-0.5)
    grad_weight = summed[:feat_local]
    grad_bias = lax.dynamic_slice(summed[feat_local], (place[0] * hid_local,), (hid_local,))

    grad_feats = pl.pallas_call(
        finish_kernel,
        out_shape=jax.ShapeDtypeStruct((feat_local, rows), F32),
        name="finish",
    )(kept, norm_blocks, *arrived).T
    return hidden, grad_weight, grad_bias, grad_feats


def solution(mesh):
    return jax.shard_map(
        on_device,
        mesh=mesh,
        in_specs=(
            P("nodes", "feat"),
            P("nodes", None, None, None, None),
            P("nodes", None, None),
            P("nodes", None, None),
            P("nodes", None),
            P("nodes"),
            P("feat", None),
            P("feat"),
            P("nodes", "feat"),
        ),
        out_specs=(P("nodes", "feat"), P("feat", None), P("feat"), P("nodes", "feat")),
        check_vma=False,
    )
```

time: 434 us -> 167 us (0.38)
  waiting for transfers between devices: 228 us -> 26.7 us
  matrix products: 67 us -> 0 us
  starting transfers between devices: 0.16 us -> 65.7 us
  blocking collectives: 69.7 us -> 9.81 us
  Pallas kernels: 0 us -> 47.7 us
  local copies, waits for them, and re-layouts: 43.6 us -> 9 us
  between operations: 13.9 us -> 1.25 us
    reduce_scatter x2 -> x0, waiting for transfers between devices: 118 us -> none  [the longest x1 90.9 us: on_device(): lax.psum_scatter(partial_pre, 'feat', scatter_dimension=1, tiled=True)]
    all_gather x2 -> x0, waiting for transfers between devices: 110 us -> none  [the longest x1 59 us: on_device(): piece = lax.all_gather(scaled, 'nodes', axis=0, tiled=True)]
    psum x1 -> x0, blocking collectives: 69.7 us -> none  [on_device(): weight_sum, bias_sum = lax.psum((weight_part, bias_part), 'nodes')]
    dot_general x37 -> x0, matrix products: 67 us -> none  [the longest x16 29.8 us: add_one(): jnp.einsum('cij,cjf->cif', tile_set, picked, preferred_element_type=jnp.f...]
    pallas_call x0 -> x11, Pallas kernels: none -> 47.7 us  [the longest x4 20.3 us: forward_call(): pl.pallas_call(functools.partial(forward_kernel, pieces, first, last), ou...]
    ppermute x0 -> x34, starting transfers between devices: none -> 47.3 us  [the longest x30 45.4 us: move(): return lax.ppermute(value, 'nodes', pairs)]
    all_to_all x0 -> x4, starting transfers between devices: none -> 18.4 us  [the longest x1 6.15 us: on_device(): agg = lax.all_to_all(start, 'feat', 0, 0)]
    dynamic_slice x32 -> x1, local copies, waits for them, and re-layouts: 18.5 us -> 0.58 us  [on_device(): lax.dynamic_slice(summed[feat_local], (place[0] * hid_local,), (hid_local,))]
  transfers between devices with their start and end apart: 4 -> 38, of which waited for: 4 -> 7; matrix products, arithmetic and copies ran while one was open for 1% -> 4% of each run, Pallas kernels for 0% -> 24%
where the time goes in v1:
time: 167 us; the launch traced here: 165 us
  starting transfers between devices  65.7 us (39%)
  Pallas kernels  47.7 us (29%)
  waiting for transfers between devices  26.7 us (16%)
  blocking collectives  9.81 us (6%)
  local copies, waits for them, and re-layouts  9 us (5%)
  other arithmetic  4.43 us (3%)
    ppermute x30, starting transfers between devices, move(): return lax.ppermute(value, 'nodes', pairs)  45.4 us
    pallas_call x4, Pallas kernels, forward_call(): pl.pallas_call(functools.partial(forward_kernel, pieces, first, last), ou...  20.3 us
    pallas_call x4, Pallas kernels, backward_call(): pl.pallas_call(functools.partial(backward_kernel, pieces, added, kept), o...  19 us
    ppermute x30, waiting for transfers between devices, move(): return lax.ppermute(value, 'nodes', pairs)  12.5 us
    all_to_all x1, blocking collectives, on_device(): lax.all_to_all(jnp.concatenate([weight_part, bias_part], axis=1), 'feat',...  9.81 us
    all_to_all x1, waiting for transfers between devices, on_device(): agg = lax.all_to_all(start, 'feat', 0, 0)  7.8 us
    all_to_all x1, waiting for transfers between devices, on_device(): back = lax.all_to_all(back, 'feat', 0, 0)  6.34 us
    all_to_all x1, starting transfers between devices, on_device(): agg = lax.all_to_all(start, 'feat', 0, 0)  6.15 us
  transfers between devices with their start and end apart: 38, of which 7 were waited for; matrix products, arithmetic and copies ran while one was open for 4% of the time, Pallas kernels for 24%

profile of v1, /device:TPU:0, one launch (start us, length us, event | category | flops | bytes accessed | tf_op | source)
XLA Modules:
  0.0 164.5 jit_solution(6974497137825032232)
XLA Ops:
  1.8 2.2 %prepare.1 = (bf16[64,16,128]{2,1,0:T(8,128)(2,1)}, bf16[8,10,32,128]{3,2,1,0:T(8,128)(2,1)}) custom-call(bf16[16,8192]{1,0:T(8,128)(2,1)} %bitcast.86, f32[64,128]{1,0:T(8,128)} %bitcast.78, bf16[32,8192]{1,0:T(8,128)(2,1)} %bitcast.83, bf16[16,256]{1,0:T(8,128)(2,1)} %weight.1, f32[1,128]{1,0:T(1,128)} %pad.4.bias), custom_call_target="tpu_custom_call" | custom-call | tf_op jit(solution)/shard_map/prepare/pallas_call | solution.py:252
  4.0 3.1 %collective-permute-start.12 = (bf16[64,16,128]{2,1,0:T(8,128)(2,1)}, bf16[64,16,128]{2,1,0:T(8,128)(2,1)S(1)}, u32[]{:S(2)}, u32[]{:S(2)}) collective-permute-start(bf16[64,16,128]{2,1,0:T(8,128)(2,1)} %get-tuple-element.25.refs_0_), channel_id=1, source_target_pairs={{0,64},{8,72},{16,80},{24,88},{32,96},{40,104},{48,112},{56,120},{... | collective-permute-start | bytes 786440 | tf_op jit(solution)/shard_map/ppermute | solution.py:250
  7.1 3.0 %collective-permute-start.10 = (bf16[64,16,128]{2,1,0:T(8,128)(2,1)}, bf16[64,16,128]{2,1,0:T(8,128)(2,1)S(1)}, u32[]{:S(2)}, u32[]{:S(2)}) collective-permute-start(bf16[64,16,128]{2,1,0:T(8,128)(2,1)} %get-tuple-element.25.refs_0_), channel_id=1, source_target_pairs={{0,48},{8,56},{16,0},{24,8},{32,16},{40,24},{48,32},{56,40},{64,11... | collective-permute-start | bytes 786440 | tf_op jit(solution)/shard_map/ppermute | solution.py:250
  10.2 3.2 %collective-permute-start.6 = (bf16[64,16,128]{2,1,0:T(8,128)(2,1)}, bf16[64,16,128]{2,1,0:T(8,128)(2,1)S(1)}, u32[]{:S(2)}, u32[]{:S(2)}) collective-permute-start(bf16[64,16,128]{2,1,0:T(8,128)(2,1)} %get-tuple-element.25.refs_0_), channel_id=1, source_target_pairs={{0,112},{8,120},{16,64},{24,72},{32,80},{40,88},{48,96},{56,104},{... | collective-permute-start | bytes 786440 | tf_op jit(solution)/shard_map/ppermute | solution.py:250
  14.6 6.0 %collective-permute-start.2 = (bf16[64,16,128]{2,1,0:T(8,128)(2,1)}, bf16[64,16,128]{2,1,0:T(8,128)(2,1)S(1)}, u32[]{:S(2)}, u32[]{:S(2)}) collective-permute-start(bf16[64,16,128]{2,1,0:T(8,128)(2,1)} %get-tuple-element.25.refs_0_), channel_id=1, source_target_pairs={{0,96},{8,104},{16,112},{24,120},{32,64},{40,72},{48,80},{56,88},{... | collective-permute-start | bytes 786440 | tf_op jit(solution)/shard_map/ppermute | solution.py:250
  21.1 3.6 %collective-permute-start = (bf16[64,16,128]{2,1,0:T(8,128)(2,1)}, bf16[64,16,128]{2,1,0:T(8,128)(2,1)S(1)}, u32[]{:S(2)}, u32[]{:S(2)}) collective-permute-start(bf16[64,16,128]{2,1,0:T(8,128)(2,1)} %get-tuple-element.25.refs_0_), channel_id=1, source_target_pairs={{0,32},{8,40},{16,48},{24,56},{32,0},{40,8},{48,16},{56,24},{64,96... | collective-permute-start | bytes 786440 | tf_op jit(solution)/shard_map/ppermute | solution.py:250
  25.1 5.3 %all-to-all-start.1 = ((bf16[8,10,32,128]{3,2,1,0:T(8,128)(2,1)}), bf16[8,10,32,128]{3,2,1,0:T(8,128)(2,1)S(1)}, u32[]{:S(2)}, u32[]{:S(2)}) async-start(bf16[8,10,32,128]{3,2,1,0:T(8,128)(2,1)} %get-tuple-element.26), calls=%async_computation.1 | async-start | bytes 1310720 | tf_op jit(solution)/shard_map/all_to_all | solution.py:267
  30.6 3.6 %collective-permute-done.2.refs_2_ = bf16[64,16,128]{2,1,0:T(8,128)(2,1)S(1)} collective-permute-done((bf16[64,16,128]{2,1,0:T(8,128)(2,1)}, bf16[64,16,128]{2,1,0:T(8,128)(2,1)S(1)}, u32[]{:S(2)}, u32[]{:S(2)}) %collective-permute-start.2) | collective-permute-done | bytes 262176 | tf_op jit(solution)/shard_map/ppermute | solution.py:250
  34.2 5.5 %collective-permute-done.refs_0_ = bf16[64,16,128]{2,1,0:T(8,128)(2,1)S(1)} collective-permute-done((bf16[64,16,128]{2,1,0:T(8,128)(2,1)}, bf16[64,16,128]{2,1,0:T(8,128)(2,1)S(1)}, u32[]{:S(2)}, u32[]{:S(2)}) %collective-permute-start) | collective-permute-done | bytes 262176 | tf_op jit(solution)/shard_map/ppermute | solution.py:250
  42.8 3.4 %forward_tiles.4.refs_7_ = f32[64,16,128]{2,1,0:T(8,128)} custom-call(s32[2]{0:T(128)} %pad_add_fusion.2.slabs, s32[16]{0:T(128)} %bitcast.87, s32[16,32]{1,0:T(8,128)} %bitcast.62, s32[16,32]{1,0:T(8,128)} %bitcast.70, bf16[64,16,128]{2,1,0:T(8,128)(2,1)} %get-tuple-element.25.refs_0_, bf16[64,16,128]{2,1,0:T(8,128)(2,1)} %copy-done.29, ...), custom_call_target="tpu_custom_call" | custom-call | tf_op jit(solution)/shard_map/forward_tiles/pallas_call | solution.py:130
  46.2 6.6 %forward_tiles.5.refs_5_ = f32[64,16,128]{2,1,0:T(8,128)} custom-call(s32[6]{0:T(128)} %stack.132.slabs, s32[16]{0:T(128)} %bitcast.88, s32[16,32]{1,0:T(8,128)} %bitcast.63, s32[16,32]{1,0:T(8,128)} %bitcast.71, bf16[64,16,128]{2,1,0:T(8,128)(2,1)} %copy-done.9, bf16[64,16,128]{2,1,0:T(8,128)(2,1)} %collective-permute-done.9.refs_1_, ...), custom_call_target="tpu_custom_call" | custom-call | tf_op jit(solution)/shard_map/forward_tiles/pallas_call | solution.py:130
  53.6 5.8 %forward_tiles.6.refs_5_ = f32[64,16,128]{2,1,0:T(8,128)} custom-call(s32[4]{0:T(128)} %pad_add_fusion.1.slabs, s32[16]{0:T(128)} %bitcast.89, s32[16,32]{1,0:T(8,128)} %bitcast.64, s32[16,32]{1,0:T(8,128)} %bitcast.72, bf16[64,16,128]{2,1,0:T(8,128)(2,1)} %copy-done.7, bf16[64,16,128]{2,1,0:T(8,128)(2,1)} %collective-permute-done.5.refs_1_, ...), custom_call_target="tpu_custom_call" | custom-call | tf_op jit(solution)/shard_map/forward_tiles/pallas_call | solution.py:130
  60.1 4.5 %forward_tiles.7 = bf16[8,8,16,128]{3,2,1,0:T(8,128)(2,1)} custom-call(s32[4]{0:T(128)} %pad_add_fusion.slabs, s32[16]{0:T(128)} %bitcast.90, s32[16,32]{1,0:T(8,128)} %bitcast.65, s32[16,32]{1,0:T(8,128)} %bitcast.73, bf16[64,16,128]{2,1,0:T(8,128)(2,1)} %copy-done.8, bf16[64,16,128]{2,1,0:T(8,128)(2,1)} %collective-permute-done.1.refs_1_, ...), custom_call_target="tpu_custom_call" | custom-call | tf_op jit(solution)/shard_map/forward_tiles/pallas_call | solution.py:130
  64.6 6.2 %all-to-all-start = ((bf16[8,8,16,128]{3,2,1,0:T(8,128)(2,1)}), bf16[8,8,16,128]{3,2,1,0:T(8,128)(2,1)S(1)}, u32[]{:S(2)}, u32[]{:S(2)}) async-start(bf16[8,8,16,128]{3,2,1,0:T(8,128)(2,1)} %forward_tiles.7), calls=%async_computation | async-start | bytes 524288 | tf_op jit(solution)/shard_map/all_to_all | solution.py:281
  70.8 7.8 %all-to-all-done.agg = bf16[8,8,16,128]{3,2,1,0:T(8,128)(2,1)S(1)} async-done(((bf16[8,8,16,128]{3,2,1,0:T(8,128)(2,1)}), bf16[8,8,16,128]{3,2,1,0:T(8,128)(2,1)S(1)}, u32[]{:S(2)}, u32[]{:S(2)}) %all-to-all-start) | async-done | bytes 262176 | tf_op jit(solution)/shard_map/all_to_all | solution.py:281
  79.3 3.5 %dense.1 = (bf16[8,8,32,128]{3,2,1,0:T(8,128)(2,1)}, bf16[8,8,16,128]{3,2,1,0:T(8,128)(2,1)}, f32[136,256]{1,0:T(8,128)}) custom-call(s32[1]{0:T(128)} %bitcast.place, bf16[8,8,16,128]{3,2,1,0:T(8,128)(2,1)} %copy-done.2, bf16[8,10,32,128]{3,2,1,0:T(8,128)(2,1)} %copy-done.1, f32[64,128]{1,0:T(8,128)} %bitcast.80), custom_call_target="tpu_custom_call" | custom-call | tf_op jit(solution)/shard_map/dense/pallas_call | solution.py:282
  84.4 9.8 %all_to_all.25 = f32[8,24,256]{2,1,0:T(8,128)S(1)} all-to-all(f32[8,24,256]{2,1,0:T(8,128)S(1)} %pad_maximum_fusion), channel_id=1, replica_groups=mesh['nodes'=16,'feat'=8] {'feat'}, dimensions={0} | all-to-all | bytes 393216 | tf_op jit(solution)/shard_map/all_to_all | solution.py:316
  94.2 3.4 %all-to-all-start.4 = ((bf16[8,8,16,128]{3,2,1,0:T(8,128)(2,1)}), bf16[8,8,16,128]{3,2,1,0:T(8,128)(2,1)S(1)}, u32[]{:S(2)}, u32[]{:S(2)}) async-start(bf16[8,8,16,128]{3,2,1,0:T(8,128)(2,1)} %get-tuple-element.29), calls=%async_computation.4 | async-start | bytes 524288 | tf_op jit(solution)/shard_map/all_to_all | solution.py:292
  98.5 6.3 %all-to-all-done.4.refs_0_ = bf16[8,8,16,128]{3,2,1,0:T(8,128)(2,1)S(1)} async-done(((bf16[8,8,16,128]{3,2,1,0:T(8,128)(2,1)}), bf16[8,8,16,128]{3,2,1,0:T(8,128)(2,1)S(1)}, u32[]{:S(2)}, u32[]{:S(2)}) %all-to-all-start.4) | async-done | bytes 262176 | tf_op jit(solution)/shard_map/all_to_all | solution.py:292
  105.5 4.7 %backward_tiles.6 = (bf16[64,16,128]{2,1,0:T(8,128)(2,1)}, bf16[64,16,128]{2,1,0:T(8,128)(2,1)}, bf16[64,16,128]{2,1,0:T(8,128)(2,1)}, bf16[64,16,128]{2,1,0:T(8,128)(2,1)}) custom-call(s32[4]{0:T(128)} %pad_add_fusion.6.slabs, s32[16]{0:T(128)} %bitcast.91, s32[16,32]{1,0:T(8,128)} %bitcast.66, s32[16,32]{1,0:T(8,128)} %bitcast.74, ...), custom_call_target="tpu_custom_call" | custom-call | tf_op jit(solution)/shard_map/backward_tiles/pallas_call | solution.py:171
  112.1 4.5 %backward_tiles.4 = (bf16[64,16,128]{2,1,0:T(8,128)(2,1)}, bf16[64,16,128]{2,1,0:T(8,128)(2,1)}, bf16[64,16,128]{2,1,0:T(8,128)(2,1)}, bf16[64,16,128]{2,1,0:T(8,128)(2,1)}) custom-call(s32[4]{0:T(128)} %pad_add_fusion.4.slabs, s32[16]{0:T(128)} %bitcast.92, s32[16,32]{1,0:T(8,128)} %bitcast.67, s32[16,32]{1,0:T(8,128)} %bitcast.75, ...), custom_call_target="tpu_custom_call" | custom-call | tf_op jit(solution)/shard_map/backward_tiles/pallas_call | solution.py:171
  120.0 4.9 %backward_tiles.7 = (bf16[64,16,128]{2,1,0:T(8,128)(2,1)}, bf16[64,16,128]{2,1,0:T(8,128)(2,1)}, bf16[64,16,128]{2,1,0:T(8,128)(2,1)}, bf16[64,16,128]{2,1,0:T(8,128)(2,1)}) custom-call(s32[4]{0:T(128)} %pad_add_fusion.5.slabs, s32[16]{0:T(128)} %bitcast.93, s32[16,32]{1,0:T(8,128)} %bitcast.68, s32[16,32]{1,0:T(8,128)} %bitcast.76, ...), custom_call_target="tpu_custom_call" | custom-call | tf_op jit(solution)/shard_map/backward_tiles/pallas_call | solution.py:171
  124.9 6.7 %collective-permute-start.27 = (bf16[64,16,128]{2,1,0:T(8,128)(2,1)}, bf16[64,16,128]{2,1,0:T(8,128)(2,1)S(1)}, u32[]{:S(2)}, u32[]{:S(2)}) collective-permute-start(bf16[64,16,128]{2,1,0:T(8,128)(2,1)} %get-tuple-element.39), channel_id=1, source_target_pairs={{0,96},{8,104},{16,112},{24,120},{32,64},{40,72},{48,80},{56,88},{... | collective-permute-start | bytes 786440 | tf_op jit(solution)/shard_map/ppermute | solution.py:250
  131.6 2.2 %collective-permute-start.28 = (bf16[64,16,128]{2,1,0:T(8,128)(2,1)}, bf16[64,16,128]{2,1,0:T(8,128)(2,1)S(1)}, u32[]{:S(2)}, u32[]{:S(2)}) collective-permute-start(bf16[64,16,128]{2,1,0:T(8,128)(2,1)} %get-tuple-element.40), channel_id=1, source_target_pairs={{0,32},{8,40},{16,48},{24,56},{32,0},{40,8},{48,16},{56,24},{64,96... | collective-permute-start | bytes 786440 | tf_op jit(solution)/shard_map/ppermute | solution.py:250
  133.8 3.5 %all-to-all-start.2 = ((bf16[8,8,32,128]{3,2,1,0:T(8,128)(2,1)}), bf16[8,8,32,128]{3,2,1,0:T(8,128)(2,1)S(1)}, u32[]{:S(2)}, u32[]{:S(2)}) async-start(bf16[8,8,32,128]{3,2,1,0:T(8,128)(2,1)} %get-tuple-element.27), calls=%async_computation.2 | async-start | bytes 1048576 | tf_op jit(solution)/shard_map/all_to_all | solution.py:312
  138.1 3.2 %collective-permute-start.29 = (bf16[64,16,128]{2,1,0:T(8,128)(2,1)}, bf16[64,16,128]{2,1,0:T(8,128)(2,1)S(1)}, u32[]{:S(2)}, u32[]{:S(2)}) collective-permute-start(bf16[64,16,128]{2,1,0:T(8,128)(2,1)} %get-tuple-element.41), channel_id=1, source_target_pairs={{0,80},{8,88},{16,96},{24,104},{32,112},{40,120},{48,64},{56,72},{... | collective-permute-start | bytes 786440 | tf_op jit(solution)/shard_map/ppermute | solution.py:250
  141.4 2.7 %collective-permute-start.30 = (bf16[64,16,128]{2,1,0:T(8,128)(2,1)}, bf16[64,16,128]{2,1,0:T(8,128)(2,1)S(1)}, u32[]{:S(2)}, u32[]{:S(2)}) collective-permute-start(bf16[64,16,128]{2,1,0:T(8,128)(2,1)} %get-tuple-element.42), channel_id=1, source_target_pairs={{0,112},{8,120},{16,64},{24,72},{32,80},{40,88},{48,96},{56,104},{... | collective-permute-start | bytes 786440 | tf_op jit(solution)/shard_map/ppermute | solution.py:250
  144.1 5.0 %backward_tiles.5 = (bf16[64,16,128]{2,1,0:T(8,128)(2,1)}, bf16[64,16,128]{2,1,0:T(8,128)(2,1)}, bf16[64,16,128]{2,1,0:T(8,128)(2,1)}, f32[64,16,128]{2,1,0:T(8,128)}) custom-call(s32[4]{0:T(128)} %pad_add_fusion.3.slabs, s32[16]{0:T(128)} %bitcast.94, s32[16,32]{1,0:T(8,128)} %bitcast.69, s32[16,32]{1,0:T(8,128)} %bitcast.77, ...), custom_call_target="tpu_custom_call" | custom-call | tf_op jit(solution)/shard_map/backward_tiles/pallas_call | solution.py:171
  149.2 3.2 %collective-permute-start.32 = (bf16[64,16,128]{2,1,0:T(8,128)(2,1)}, bf16[64,16,128]{2,1,0:T(8,128)(2,1)S(1)}, u32[]{:S(2)}, u32[]{:S(2)}) collective-permute-start(bf16[64,16,128]{2,1,0:T(8,128)(2,1)} %get-tuple-element.44), channel_id=1, source_target_pairs={{0,48},{8,56},{16,0},{24,8},{32,16},{40,24},{48,32},{56,40},{64,11... | collective-permute-start | bytes 786440 | tf_op jit(solution)/shard_map/ppermute | solution.py:250
  152.4 3.7 %collective-permute-start.33 = (bf16[64,16,128]{2,1,0:T(8,128)(2,1)}, bf16[64,16,128]{2,1,0:T(8,128)(2,1)S(1)}, u32[]{:S(2)}, u32[]{:S(2)}) collective-permute-start(bf16[64,16,128]{2,1,0:T(8,128)(2,1)} %get-tuple-element.45), channel_id=1, source_target_pairs={{0,64},{8,72},{16,80},{24,88},{32,96},{40,104},{48,112},{56,120},{... | collective-permute-start | bytes 786440 | tf_op jit(solution)/shard_map/ppermute | solution.py:250
  158.3 2.3 %collective-permute-done.32.refs_5_ = bf16[64,16,128]{2,1,0:T(8,128)(2,1)S(1)} collective-permute-done((bf16[64,16,128]{2,1,0:T(8,128)(2,1)}, bf16[64,16,128]{2,1,0:T(8,128)(2,1)S(1)}, u32[]{:S(2)}, u32[]{:S(2)}) %collective-permute-start.32) | collective-permute-done | bytes 262176 | tf_op jit(solution)/shard_map/ppermute | solution.py:250
  161.9 2.7 %finish.1 = f32[16,8192]{1,0:T(8,128)} custom-call(f32[64,16,128]{2,1,0:T(8,128)} %get-tuple-element.34.kept, f32[64,128]{1,0:T(8,128)} %bitcast.81, bf16[64,16,128]{2,1,0:T(8,128)(2,1)} %copy-done.22, bf16[64,16,128]{2,1,0:T(8,128)(2,1)} %copy-done.23, bf16[64,16,128]{2,1,0:T(8,128)(2,1)} %copy-done.24, bf16[64,16,128]{2,1,0:T(8,128)(2,1)} %copy-done.25, ...), custom_call_target="tpu_custom_call" | custom-call | tf_op jit(solution)/shard_map/finish/pallas_call | solution.py:328
  (138 shorter events, 21.1 us)
Async XLA Ops:
  4.0 9.3 %collective-permute-start.14 = (bf16[64,16,128]{2,1,0:T(8,128)(2,1)}, bf16[64,16,128]{2,1,0:T(8,128)(2,1)S(1)}, u32[]{:S(2)}, u32[]{:S(2)}) collective-permute-start(bf16[64,16,128]{2,1,0:T(8,128)(2,1)} %get-tuple-element.25.refs_0_), channel_id=1, source_target_pairs={{0,8},{8,0},{16,24},{24,16},{32,40},{40,32},{48,56},{56,48},{64,72... | collective-permute-start | bytes 786440 | tf_op jit(solution)/shard_map/ppermute | solution.py:250
  4.0 10.6 %collective-permute-start.12 = (bf16[64,16,128]{2,1,0:T(8,128)(2,1)}, bf16[64,16,128]{2,1,0:T(8,128)(2,1)S(1)}, u32[]{:S(2)}, u32[]{:S(2)}) collective-permute-start(bf16[64,16,128]{2,1,0:T(8,128)(2,1)} %get-tuple-element.25.refs_0_), channel_id=1, source_target_pairs={{0,64},{8,72},{16,80},{24,88},{32,96},{40,104},{48,112},{56,120},{... | collective-permute-start | bytes 786440 | tf_op jit(solution)/shard_map/ppermute | solution.py:250
  7.1 13.9 %collective-permute-start.10 = (bf16[64,16,128]{2,1,0:T(8,128)(2,1)}, bf16[64,16,128]{2,1,0:T(8,128)(2,1)S(1)}, u32[]{:S(2)}, u32[]{:S(2)}) collective-permute-start(bf16[64,16,128]{2,1,0:T(8,128)(2,1)} %get-tuple-element.25.refs_0_), channel_id=1, source_target_pairs={{0,48},{8,56},{16,0},{24,8},{32,16},{40,24},{48,32},{56,40},{64,11... | collective-permute-start | bytes 786440 | tf_op jit(solution)/shard_map/ppermute | solution.py:250
  10.2 14.5 %collective-permute-start.8 = (bf16[64,16,128]{2,1,0:T(8,128)(2,1)}, bf16[64,16,128]{2,1,0:T(8,128)(2,1)S(1)}, u32[]{:S(2)}, u32[]{:S(2)}) collective-permute-start(bf16[64,16,128]{2,1,0:T(8,128)(2,1)} %get-tuple-element.25.refs_0_), channel_id=1, source_target_pairs={{0,16},{8,24},{16,32},{24,40},{32,48},{40,56},{48,0},{56,8},{64,80... | collective-permute-start | bytes 786440 | tf_op jit(solution)/shard_map/ppermute | solution.py:250
  10.2 14.5 %collective-permute-start.6 = (bf16[64,16,128]{2,1,0:T(8,128)(2,1)}, bf16[64,16,128]{2,1,0:T(8,128)(2,1)S(1)}, u32[]{:S(2)}, u32[]{:S(2)}) collective-permute-start(bf16[64,16,128]{2,1,0:T(8,128)(2,1)} %get-tuple-element.25.refs_0_), channel_id=1, source_target_pairs={{0,112},{8,120},{16,64},{24,72},{32,80},{40,88},{48,96},{56,104},{... | collective-permute-start | bytes 786440 | tf_op jit(solution)/shard_map/ppermute | solution.py:250
  13.3 17.1 %collective-permute-start.4 = (bf16[64,16,128]{2,1,0:T(8,128)(2,1)}, bf16[64,16,128]{2,1,0:T(8,128)(2,1)S(1)}, u32[]{:S(2)}, u32[]{:S(2)}) collective-permute-start(bf16[64,16,128]{2,1,0:T(8,128)(2,1)} %get-tuple-element.25.refs_0_), channel_id=1, source_target_pairs={{0,80},{8,88},{16,96},{24,104},{32,112},{40,120},{48,64},{56,72},{... | collective-permute-start | bytes 786440 | tf_op jit(solution)/shard_map/ppermute | solution.py:250
  14.6 19.6 %collective-permute-start.2 = (bf16[64,16,128]{2,1,0:T(8,128)(2,1)}, bf16[64,16,128]{2,1,0:T(8,128)(2,1)S(1)}, u32[]{:S(2)}, u32[]{:S(2)}) collective-permute-start(bf16[64,16,128]{2,1,0:T(8,128)(2,1)} %get-tuple-element.25.refs_0_), channel_id=1, source_target_pairs={{0,96},{8,104},{16,112},{24,120},{32,64},{40,72},{48,80},{56,88},{... | collective-permute-start | bytes 786440 | tf_op jit(solution)/shard_map/ppermute | solution.py:250
  21.1 18.6 %collective-permute-start = (bf16[64,16,128]{2,1,0:T(8,128)(2,1)}, bf16[64,16,128]{2,1,0:T(8,128)(2,1)S(1)}, u32[]{:S(2)}, u32[]{:S(2)}) collective-permute-start(bf16[64,16,128]{2,1,0:T(8,128)(2,1)} %get-tuple-element.25.refs_0_), channel_id=1, source_target_pairs={{0,32},{8,40},{16,48},{24,56},{32,0},{40,8},{48,16},{56,24},{64,96... | collective-permute-start | bytes 786440 | tf_op jit(solution)/shard_map/ppermute | solution.py:250
  24.6 15.1 %collective-permute-start.13 = (bf16[64,16,128]{2,1,0:T(8,128)(2,1)S(1)}, bf16[64,16,128]{2,1,0:T(8,128)(2,1)S(1)}, u32[]{:S(2)}, u32[]{:S(2)}) collective-permute-start(bf16[64,16,128]{2,1,0:T(8,128)(2,1)S(1)} %collective-permute-done.12.refs_4_), channel_id=1, source_target_pairs={{0,8},{8,0},{16,24},{24,16},{32,40},{40,32},{48,56},{56,48},{64,72... | collective-permute-start | bytes 786440 | tf_op jit(solution)/shard_map/ppermute | solution.py:250
  24.6 15.6 %collective-permute-start.11 = (bf16[64,16,128]{2,1,0:T(8,128)(2,1)S(1)}, bf16[64,16,128]{2,1,0:T(8,128)(2,1)S(1)}, u32[]{:S(2)}, u32[]{:S(2)}) collective-permute-start(bf16[64,16,128]{2,1,0:T(8,128)(2,1)S(1)} %collective-permute-done.10.refs_2_), channel_id=1, source_target_pairs={{0,8},{8,0},{16,24},{24,16},{32,40},{40,32},{48,56},{56,48},{64,72... | collective-permute-start | bytes 786440 | tf_op jit(solution)/shard_map/ppermute | solution.py:250
  25.1 39.5 %all-to-all-start.1 = ((bf16[8,10,32,128]{3,2,1,0:T(8,128)(2,1)}), bf16[8,10,32,128]{3,2,1,0:T(8,128)(2,1)S(1)}, u32[]{:S(2)}, u32[]{:S(2)}) async-start(bf16[8,10,32,128]{3,2,1,0:T(8,128)(2,1)} %get-tuple-element.26), calls=%async_computation.1 | async-start | bytes 1310720 | tf_op jit(solution)/shard_map/all_to_all | solution.py:267
  30.5 15.7 %collective-permute-start.9 = (bf16[64,16,128]{2,1,0:T(8,128)(2,1)S(1)}, bf16[64,16,128]{2,1,0:T(8,128)(2,1)}, u32[]{:S(2)}, u32[]{:S(2)}) collective-permute-start(bf16[64,16,128]{2,1,0:T(8,128)(2,1)S(1)} %collective-permute-done.8.refs_0_), channel_id=1, source_target_pairs={{0,8},{8,0},{16,24},{24,16},{32,40},{40,32},{48,56},{56,48},{64,72... | collective-permute-start | bytes 786440 | tf_op jit(solution)/shard_map/ppermute | solution.py:250
  34.2 18.7 %collective-permute-start.7 = (bf16[64,16,128]{2,1,0:T(8,128)(2,1)S(1)}, bf16[64,16,128]{2,1,0:T(8,128)(2,1)S(1)}, u32[]{:S(2)}, u32[]{:S(2)}) collective-permute-start(bf16[64,16,128]{2,1,0:T(8,128)(2,1)S(1)} %collective-permute-done.6.refs_2_), channel_id=1, source_target_pairs={{0,8},{8,0},{16,24},{24,16},{32,40},{40,32},{48,56},{56,48},{64,72... | collective-permute-start | bytes 786440 | tf_op jit(solution)/shard_map/ppermute | solution.py:250
  39.7 13.2 %collective-permute-start.5 = (bf16[64,16,128]{2,1,0:T(8,128)(2,1)S(1)}, bf16[64,16,128]{2,1,0:T(8,128)(2,1)}, u32[]{:S(2)}, u32[]{:S(2)}) collective-permute-start(bf16[64,16,128]{2,1,0:T(8,128)(2,1)S(1)} %collective-permute-done.4.refs_0_), channel_id=1, source_target_pairs={{0,8},{8,0},{16,24},{24,16},{32,40},{40,32},{48,56},{56,48},{64,72... | collective-permute-start | bytes 786440 | tf_op jit(solution)/shard_map/ppermute | solution.py:250
  39.7 19.7 %collective-permute-start.3 = (bf16[64,16,128]{2,1,0:T(8,128)(2,1)S(1)}, bf16[64,16,128]{2,1,0:T(8,128)(2,1)S(1)}, u32[]{:S(2)}, u32[]{:S(2)}) collective-permute-start(bf16[64,16,128]{2,1,0:T(8,128)(2,1)S(1)} %collective-permute-done.2.refs_2_), channel_id=1, source_target_pairs={{0,8},{8,0},{16,24},{24,16},{32,40},{40,32},{48,56},{56,48},{64,72... | collective-permute-start | bytes 786440 | tf_op jit(solution)/shard_map/ppermute | solution.py:250
  40.2 19.2 %collective-permute-start.1 = (bf16[64,16,128]{2,1,0:T(8,128)(2,1)S(1)}, bf16[64,16,128]{2,1,0:T(8,128)(2,1)}, u32[]{:S(2)}, u32[]{:S(2)}) collective-permute-start(bf16[64,16,128]{2,1,0:T(8,128)(2,1)S(1)} %collective-permute-done.refs_0_), channel_id=1, source_target_pairs={{0,8},{8,0},{16,24},{24,16},{32,40},{40,32},{48,56},{56,48},{64,72... | collective-permute-start | bytes 786440 | tf_op jit(solution)/shard_map/ppermute | solution.py:250
  64.6 14.0 %all-to-all-start = ((bf16[8,8,16,128]{3,2,1,0:T(8,128)(2,1)}), bf16[8,8,16,128]{3,2,1,0:T(8,128)(2,1)S(1)}, u32[]{:S(2)}, u32[]{:S(2)}) async-start(bf16[8,8,16,128]{3,2,1,0:T(8,128)(2,1)} %forward_tiles.7), calls=%async_computation | async-start | bytes 524288 | tf_op jit(solution)/shard_map/all_to_all | solution.py:281
  94.2 10.6 %all-to-all-start.4 = ((bf16[8,8,16,128]{3,2,1,0:T(8,128)(2,1)}), bf16[8,8,16,128]{3,2,1,0:T(8,128)(2,1)S(1)}, u32[]{:S(2)}, u32[]{:S(2)}) async-start(bf16[8,8,16,128]{3,2,1,0:T(8,128)(2,1)} %get-tuple-element.29), calls=%async_computation.4 | async-start | bytes 524288 | tf_op jit(solution)/shard_map/all_to_all | solution.py:292
  97.8 13.6 %collective-permute-start.15 = (f32[24,256]{1,0:T(8,128)S(1)}, f32[24,256]{1,0:T(8,128)S(1)}, u32[]{:S(2)}, u32[]{:S(2)}) collective-permute-start(f32[24,256]{1,0:T(8,128)S(1)} %reduce_sum.9), channel_id=1, source_target_pairs={{0,8},{8,0},{16,24},{24,16},{32,40},{40,32},{48,56},{56,48},{64,72... | collective-permute-start | bytes 73736 | tf_op jit(solution)/shard_map/ppermute | solution.py:323
  116.6 15.0 %collective-permute-start.19 = (bf16[64,16,128]{2,1,0:T(8,128)(2,1)}, bf16[64,16,128]{2,1,0:T(8,128)(2,1)S(1)}, u32[]{:S(2)}, u32[]{:S(2)}) collective-permute-start(bf16[64,16,128]{2,1,0:T(8,128)(2,1)} %get-tuple-element.30), channel_id=1, source_target_pairs={{0,8},{8,0},{16,24},{24,16},{32,40},{40,32},{48,56},{56,48},{64,72... | collective-permute-start | bytes 786440 | tf_op jit(solution)/shard_map/ppermute | solution.py:250
  116.8 20.6 %collective-permute-start.20 = (bf16[64,16,128]{2,1,0:T(8,128)(2,1)}, bf16[64,16,128]{2,1,0:T(8,128)(2,1)S(1)}, u32[]{:S(2)}, u32[]{:S(2)}) collective-permute-start(bf16[64,16,128]{2,1,0:T(8,128)(2,1)} %get-tuple-element.31), channel_id=1, source_target_pairs={{0,8},{8,0},{16,24},{24,16},{32,40},{40,32},{48,56},{56,48},{64,72... | collective-permute-start | bytes 786440 | tf_op jit(solution)/shard_map/ppermute | solution.py:250
  118.9 19.2 %collective-permute-start.21 = (bf16[64,16,128]{2,1,0:T(8,128)(2,1)}, bf16[64,16,128]{2,1,0:T(8,128)(2,1)S(1)}, u32[]{:S(2)}, u32[]{:S(2)}) collective-permute-start(bf16[64,16,128]{2,1,0:T(8,128)(2,1)} %get-tuple-element.32), channel_id=1, source_target_pairs={{0,8},{8,0},{16,24},{24,16},{32,40},{40,32},{48,56},{56,48},{64,72... | collective-permute-start | bytes 786440 | tf_op jit(solution)/shard_map/ppermute | solution.py:250
  118.9 22.5 %collective-permute-start.22 = (bf16[64,16,128]{2,1,0:T(8,128)(2,1)}, bf16[64,16,128]{2,1,0:T(8,128)(2,1)S(1)}, u32[]{:S(2)}, u32[]{:S(2)}) collective-permute-start(bf16[64,16,128]{2,1,0:T(8,128)(2,1)} %get-tuple-element.33), channel_id=1, source_target_pairs={{0,8},{8,0},{16,24},{24,16},{32,40},{40,32},{48,56},{56,48},{64,72... | collective-permute-start | bytes 786440 | tf_op jit(solution)/shard_map/ppermute | solution.py:250
  124.9 24.3 %collective-permute-start.27 = (bf16[64,16,128]{2,1,0:T(8,128)(2,1)}, bf16[64,16,128]{2,1,0:T(8,128)(2,1)S(1)}, u32[]{:S(2)}, u32[]{:S(2)}) collective-permute-start(bf16[64,16,128]{2,1,0:T(8,128)(2,1)} %get-tuple-element.39), channel_id=1, source_target_pairs={{0,96},{8,104},{16,112},{24,120},{32,64},{40,72},{48,80},{56,88},{... | collective-permute-start | bytes 786440 | tf_op jit(solution)/shard_map/ppermute | solution.py:250
  131.6 20.8 %collective-permute-start.28 = (bf16[64,16,128]{2,1,0:T(8,128)(2,1)}, bf16[64,16,128]{2,1,0:T(8,128)(2,1)S(1)}, u32[]{:S(2)}, u32[]{:S(2)}) collective-permute-start(bf16[64,16,128]{2,1,0:T(8,128)(2,1)} %get-tuple-element.40), channel_id=1, source_target_pairs={{0,32},{8,40},{16,48},{24,56},{32,0},{40,8},{48,16},{56,24},{64,96... | collective-permute-start | bytes 786440 | tf_op jit(solution)/shard_map/ppermute | solution.py:250
  133.8 23.5 %all-to-all-start.2 = ((bf16[8,8,32,128]{3,2,1,0:T(8,128)(2,1)}), bf16[8,8,32,128]{3,2,1,0:T(8,128)(2,1)S(1)}, u32[]{:S(2)}, u32[]{:S(2)}) async-start(bf16[8,8,32,128]{3,2,1,0:T(8,128)(2,1)} %get-tuple-element.27), calls=%async_computation.2 | async-start | bytes 1048576 | tf_op jit(solution)/shard_map/all_to_all | solution.py:312
  137.4 11.7 %collective-permute-start.18 = (f32[24,256]{1,0:T(8,128)S(1)}, f32[24,256]{1,0:T(8,128)S(1)}, u32[]{:S(2)}, u32[]{:S(2)}) collective-permute-start(f32[24,256]{1,0:T(8,128)S(1)} %add.415), channel_id=1, source_target_pairs={{0,64},{8,72},{16,80},{24,88},{32,96},{40,104},{48,112},{56,120},{... | collective-permute-start | bytes 73736 | tf_op jit(solution)/shard_map/ppermute | solution.py:323
  138.1 20.1 %collective-permute-start.29 = (bf16[64,16,128]{2,1,0:T(8,128)(2,1)}, bf16[64,16,128]{2,1,0:T(8,128)(2,1)S(1)}, u32[]{:S(2)}, u32[]{:S(2)}) collective-permute-start(bf16[64,16,128]{2,1,0:T(8,128)(2,1)} %get-tuple-element.41), channel_id=1, source_target_pairs={{0,80},{8,88},{16,96},{24,104},{32,112},{40,120},{48,64},{56,72},{... | collective-permute-start | bytes 786440 | tf_op jit(solution)/shard_map/ppermute | solution.py:250
  141.4 16.9 %collective-permute-start.30 = (bf16[64,16,128]{2,1,0:T(8,128)(2,1)}, bf16[64,16,128]{2,1,0:T(8,128)(2,1)S(1)}, u32[]{:S(2)}, u32[]{:S(2)}) collective-permute-start(bf16[64,16,128]{2,1,0:T(8,128)(2,1)} %get-tuple-element.42), channel_id=1, source_target_pairs={{0,112},{8,120},{16,64},{24,72},{32,80},{40,88},{48,96},{56,104},{... | collective-permute-start | bytes 786440 | tf_op jit(solution)/shard_map/ppermute | solution.py:250
  149.1 9.2 %collective-permute-start.31 = (bf16[64,16,128]{2,1,0:T(8,128)(2,1)}, bf16[64,16,128]{2,1,0:T(8,128)(2,1)S(1)}, u32[]{:S(2)}, u32[]{:S(2)}) collective-permute-start(bf16[64,16,128]{2,1,0:T(8,128)(2,1)} %get-tuple-element.43), channel_id=1, source_target_pairs={{0,16},{8,24},{16,32},{24,40},{32,48},{40,56},{48,0},{56,8},{64,80... | collective-permute-start | bytes 786440 | tf_op jit(solution)/shard_map/ppermute | solution.py:250
  149.2 11.4 %collective-permute-start.32 = (bf16[64,16,128]{2,1,0:T(8,128)(2,1)}, bf16[64,16,128]{2,1,0:T(8,128)(2,1)S(1)}, u32[]{:S(2)}, u32[]{:S(2)}) collective-permute-start(bf16[64,16,128]{2,1,0:T(8,128)(2,1)} %get-tuple-element.44), channel_id=1, source_target_pairs={{0,48},{8,56},{16,0},{24,8},{32,16},{40,24},{48,32},{56,40},{64,11... | collective-permute-start | bytes 786440 | tf_op jit(solution)/shard_map/ppermute | solution.py:250
  152.4 8.8 %collective-permute-start.33 = (bf16[64,16,128]{2,1,0:T(8,128)(2,1)}, bf16[64,16,128]{2,1,0:T(8,128)(2,1)S(1)}, u32[]{:S(2)}, u32[]{:S(2)}) collective-permute-start(bf16[64,16,128]{2,1,0:T(8,128)(2,1)} %get-tuple-element.45), channel_id=1, source_target_pairs={{0,64},{8,72},{16,80},{24,88},{32,96},{40,104},{48,112},{56,120},{... | collective-permute-start | bytes 786440 | tf_op jit(solution)/shard_map/ppermute | solution.py:250
  (36 other events, 311.3 us)

commit v2 on v1

v2 whole, which is shorter than its diff:
```python
import functools

import jax
import jax.numpy as jnp
from jax import lax
from jax.experimental import pallas as pl
from jax.experimental.pallas import tpu as pltpu
from jax.sharding import PartitionSpec as P

LANES = 128
UNROLL = 8
BF16 = jnp.bfloat16
F32 = jnp.float32
META_COUNTS, META_ME = 16, 17


def spec(space):
    return pl.BlockSpec(memory_space=space)


ANY, VMEM, SMEM = pl.ANY, pltpu.VMEM, pltpu.SMEM


def params():
    return pltpu.CompilerParams(vmem_limit_bytes=16 << 20)


def scale_kernel(feats, norm, scaled):
    for b in range(scaled.shape[0]):
        scaled[b] = (norm[pl.ds(b, 1), :] * feats[:, pl.ds(b * LANES, LANES)].astype(F32)).astype(BF16)


def payload_kernel(cotangent, weight, bias, payload):
    peers, per_peer = payload.shape[0], payload.shape[1] - 2
    for b in range(peers * per_peer):
        payload[b // per_peer, b % per_peer] = cotangent[:, pl.ds(b * LANES, LANES)]
    w = jnp.concatenate([weight[:, :LANES], weight[:, LANES:]], axis=0)
    rest = jnp.concatenate([bias[...]] * (LANES // bias.shape[1]), axis=1)
    parts = []
    for _ in range(3):
        part = rest.astype(BF16).astype(F32)
        rest = rest - part
        parts.append(part)
    row = lax.broadcasted_iota(jnp.int32, (payload.shape[2], LANES), 0)
    packed = jnp.where(row == 0, parts[0], jnp.where(row == 1, parts[1], jnp.where(row == 2, parts[2], 0.0)))
    packed = packed.astype(BF16)
    for g in range(peers):
        payload[g, per_peer] = w
        payload[g, per_peer + 1] = packed


def slab_id(meta, hop):
    me = meta[META_ME, 0]
    dx, dy, dc = hop
    return ((((me >> 3) + dx) & 1) << 3) + ((((me >> 1) + dy) & 3) << 1) + ((me + dc) & 1)


def start_tiles(k, slab, count, tiles, buffer, sems):
    for chunk in range(tiles.shape[1] // UNROLL):
        @pl.when(chunk * UNROLL < count)
        def _():
            pltpu.make_async_copy(
                tiles.at[slab, pl.ds(chunk * UNROLL, UNROLL)],
                buffer.at[k, pl.ds(chunk * UNROLL, UNROLL)],
                sems.at[k, chunk],
            ).start()


def over_tiles(k, slab, count, meta, tiles, buffer, sems, source_of, target_of, dims, accumulator):
    def step(chunk, carry):
        first = chunk * UNROLL
        pltpu.make_async_copy(
            tiles.at[slab, pl.ds(first, UNROLL)], buffer.at[k, pl.ds(first, UNROLL)], sems.at[k, chunk]
        ).wait()
        products, targets = [], []
        for j in range(UNROLL):
            c = first + j
            entry = meta[slab, c]
            r = lax.dot_general(source_of(entry), buffer[k, c], (dims, ((), ())), preferred_element_type=F32)
            products.append(jnp.where(c < count, r, 0.0))
            targets.append(target_of(entry))
        for t, r in zip(targets, products):
            accumulator[t] = accumulator[t] + r
        return carry

    lax.fori_loop(0, (count + UNROLL - 1) // UNROLL, step, 0)


def cost(pieces, tiles):
    used = pieces * tiles.shape[1] // 2
    tile = tiles.shape[2]
    return pl.CostEstimate(
        flops=2 * used * 16 * tile * tile, transcendentals=0, bytes_accessed=used * tile * tile * 4
    )


def forward_kernel(hops, first, last, meta, *refs):
    refs = list(refs)
    pieces = len(hops)
    xs = [refs.pop(0) for _ in range(pieces)]
    tiles = refs.pop(0)
    start = None if first else refs.pop(0)
    norm = refs.pop(0) if last else None
    out, buffer, sems, x_buffer, x_sems, acc = refs
    loads = []
    for k in range(pieces):
        slab = slab_id(meta, hops[k])
        load = pltpu.make_async_copy(xs[k], x_buffer.at[k], x_sems.at[k])
        load.start()
        loads.append(load)
        if k == 0 and not first:
            seed = pltpu.make_async_copy(start, acc, x_sems.at[pieces])
            seed.start()
        start_tiles(k, slab, meta[META_COUNTS, slab], tiles, buffer, sems)
    if first:
        for b in range(acc.shape[0]):
            acc[b] = jnp.zeros(acc.shape[1:], F32)
    else:
        seed.wait()
    for k in range(pieces):
        slab = slab_id(meta, hops[k])
        loads[k].wait()
        over_tiles(
            k, slab, meta[META_COUNTS, slab], meta, tiles, buffer, sems,
            lambda entry, k=k: x_buffer[k, entry & 63], lambda entry: entry >> 6, ((1,), (1,)), acc,
        )
    if last:
        per_peer = out.shape[1]
        for b in range(acc.shape[0]):
            out[b // per_peer, b % per_peer] = (norm[pl.ds(b, 1), :] * acc[b]).astype(BF16)
    else:
        save = pltpu.make_async_copy(acc, out, x_sems.at[pieces + 1])
        save.start()
        save.wait()


def forward_call(hops, xs, meta, tiles, start, norm, peers):
    pieces = len(xs)
    first, last = start is None, norm is not None
    shape = xs[0].shape
    args = [meta, *xs, tiles]
    specs = [spec(SMEM)] + [spec(ANY)] * (pieces + 1)
    if not first:
        args.append(start)
        specs.append(spec(ANY))
    if last:
        args.append(norm)
        specs.append(spec(VMEM))
        out = jax.ShapeDtypeStruct((peers, shape[0] // peers, *shape[1:]), BF16)
    else:
        out = jax.ShapeDtypeStruct(shape, F32)
    return pl.pallas_call(
        functools.partial(forward_kernel, hops, first, last),
        out_shape=out, in_specs=specs, out_specs=spec(VMEM) if last else spec(ANY),
        scratch_shapes=[
            VMEM((pieces, *tiles.shape[1:]), BF16),
            pltpu.SemaphoreType.DMA((pieces, tiles.shape[1] // UNROLL)),
            VMEM((pieces, *shape), BF16),
            pltpu.SemaphoreType.DMA((pieces + 2,)),
            VMEM(shape, F32),
        ],
        compiler_params=params(), cost_estimate=cost(pieces, tiles), name="forward_tiles",
    )(*args)


def backward_kernel(hops, added, meta, *refs):
    refs = list(refs)
    pieces = len(hops)
    ys = refs.pop(0)
    tiles = refs.pop(0)
    adds = [refs.pop(0) for _ in range(pieces)] if added else None
    outs = [refs.pop(0) for _ in range(pieces)]
    buffer, sems, y_buffer, y_sem, acc, save_sems = refs[:6]
    if added:
        add_buffer, add_sems = refs[6:]
    load = pltpu.make_async_copy(ys, y_buffer, y_sem.at[0])
    load.start()
    seeds = []
    for k in range(pieces):
        slab = slab_id(meta, hops[k])
        start_tiles(k, slab, meta[META_COUNTS, slab], tiles, buffer, sems)
        if added:
            seed = pltpu.make_async_copy(adds[k], add_buffer.at[k], add_sems.at[k])
            seed.start()
            seeds.append(seed)
    per_peer = ys.shape[1]
    blocks = acc.shape[1]
    saves = []
    for k in range(pieces):
        slab = slab_id(meta, hops[k])
        if added:
            seeds[k].wait()
        for b in range(blocks):
            acc[k, b] = add_buffer[k, b].astype(F32) if added else jnp.zeros(acc.shape[2:], F32)
        if k == 0:
            load.wait()

        def source_of(entry):
            d = entry >> 6
            return y_buffer[d // per_peer, d % per_peer]

        over_tiles(
            k, slab, meta[META_COUNTS, slab], meta, tiles, buffer, sems, source_of,
            lambda entry: entry & 63, ((1,), (0,)), acc.at[k],
        )
        if outs[k].dtype == F32:
            save = pltpu.make_async_copy(acc.at[k], outs[k], save_sems.at[k])
        else:
            held = buffer.at[k, pl.ds(0, acc.shape[1] * acc.shape[2] // LANES)]
            rows = acc.shape[2]
            per_tile = LANES // rows
            for b in range(blocks):
                held[b // per_tile, pl.ds((b % per_tile) * rows, rows), :] = acc[k, b].astype(BF16)
            save = pltpu.make_async_copy(held, outs[k], save_sems.at[k])
        save.start()
        saves.append(save)
    for save in saves:
        save.wait()


def backward_call(hops, ys, meta, tiles, adds, kept):
    pieces = len(hops)
    rows = ys.shape[2]
    blocks = ys.shape[0] * ys.shape[1]
    added = adds is not None
    args = [meta, ys, tiles] + (list(adds) if added else [])
    specs = [spec(SMEM), spec(ANY), spec(ANY)] + [spec(ANY)] * (pieces if added else 0)
    packed = (blocks * rows // LANES, LANES, LANES)
    outs = [
        jax.ShapeDtypeStruct((blocks, rows, LANES), F32) if k == kept else jax.ShapeDtypeStruct(packed, BF16)
        for k in range(pieces)
    ]
    scratch = [
        VMEM((pieces, *tiles.shape[1:]), BF16),
        pltpu.SemaphoreType.DMA((pieces, tiles.shape[1] // UNROLL)),
        VMEM(ys.shape, BF16),
        pltpu.SemaphoreType.DMA((1,)),
        VMEM((pieces, blocks, rows, LANES), F32),
        pltpu.SemaphoreType.DMA((pieces,)),
    ]
    if added:
        scratch += [VMEM((pieces, blocks, rows, LANES), BF16), pltpu.SemaphoreType.DMA((pieces,))]
    parts = pl.pallas_call(
        functools.partial(backward_kernel, hops, added),
        out_shape=outs, in_specs=specs, out_specs=[spec(ANY)] * pieces, scratch_shapes=scratch,
        compiler_params=params(), cost_estimate=cost(pieces, tiles), name="backward_tiles",
    )(*args)
    return [p.reshape(blocks, rows, LANES) for p in parts]


def dense_kernel(place, agg, received, norm, back, sent):
    peers, blocks, feat_local = agg.shape[0], agg.shape[1], agg.shape[2]
    hid_local = sent.shape[2]
    halves = hid_local // feat_local
    weight = jnp.concatenate(
        [
            jnp.concatenate([received[g, blocks, pl.ds(h * feat_local, feat_local), :] for h in range(halves)], axis=1)
            for g in range(peers)
        ],
        axis=0,
    )
    bias_rows = []
    for g in range(peers):
        parts = received[g, blocks + 1].astype(F32)
        bias_rows.append((parts[0:1] + parts[1:2] + parts[2:3])[:, :hid_local])
    bias = jnp.concatenate(bias_rows, axis=1)
    bias = jnp.transpose(jnp.broadcast_to(bias, (8, bias.shape[1])))[:, 0:1]
    grad = jnp.zeros((peers * feat_local + 8, weight.shape[1]), F32)
    for b in range(blocks):
        agg_b = jnp.concatenate([agg[g, b] for g in range(peers)], axis=0)
        cot_b = jnp.concatenate([received[g, b] for g in range(peers)], axis=0).astype(F32)
        pre = lax.dot_general(weight, agg_b, (((0,), (0,)), ((), ())), preferred_element_type=F32) + bias
        sig = 1.0 / (1.0 + jnp.exp(-pre))
        hid = (pre * sig).astype(BF16)
        grad_pre = (cot_b * sig * (1.0 + pre * (1.0 - sig))).astype(BF16)
        back_b = jnp.dot(weight, grad_pre, preferred_element_type=F32)
        back_b = (norm[pl.ds(place[0] * blocks + b, 1), :] * back_b).astype(BF16)
        left = jnp.concatenate([agg_b, jnp.ones((8, LANES), BF16)], axis=0)
        grad = grad + lax.dot_general(left, grad_pre, (((1,), (1,)), ((), ())), preferred_element_type=F32)
        for g in range(peers):
            sent[g, b] = hid[g * hid_local:(g + 1) * hid_local]
            back[g, b] = back_b[g * feat_local:(g + 1) * feat_local]
    for g in range(peers):
        for source, slot in ((grad[g * feat_local:(g + 1) * feat_local], blocks), (grad[peers * feat_local:], blocks + 2)):
            high = source.astype(BF16).astype(F32)
            for i, part in enumerate((high, source - high)):
                part = jnp.concatenate([part[:, h * LANES:(h + 1) * LANES] for h in range(halves)], axis=0)
                short = hid_local - part.shape[0]
                if slot == blocks + 2:
                    sent[g, slot, pl.ds(i * part.shape[0], part.shape[0]), :] = part.astype(BF16)
                else:
                    sent[g, slot + i] = part.astype(BF16)


def collect_kernel(received, hidden, grads):
    peers, per_peer = received.shape[0], received.shape[1] - 3
    for b in range(peers * per_peer):
        hidden[:, pl.ds(b * LANES, LANES)] = received[b // per_peer, b % per_peer]
    rows = received.shape[2]
    total = jnp.zeros((rows, LANES), F32)
    tail = jnp.zeros((rows, LANES), F32)
    for g in range(peers):
        total = total + (received[g, per_peer].astype(F32) + received[g, per_peer + 1].astype(F32))
        tail = tail + received[g, per_peer + 2].astype(F32)
    grads[0:rows] = total
    grads[rows:2 * rows] = tail


def finish_kernel(kept, norm, *refs):
    out = refs[-1]
    for b in range(kept.shape[0]):
        total = kept[b]
        for r in refs[:-1]:
            total = total + r[b].astype(F32)
        out[:, pl.ds(b * LANES, LANES)] = norm[pl.ds(b, 1), :] * total


def on_device(feats, tiles, dst_block, src_block, tile_counts, norm, weight, bias, cotangent):
    rows, feat_local = feats.shape
    tile = tiles.shape[-1]
    blocks = rows // tile
    hid_local = cotangent.shape[1]
    peers = lax.axis_size("feat")
    slabs = lax.axis_size("nodes")
    per_peer = blocks // peers
    slots = tiles.shape[2]
    own_tiles = tiles[0]
    norm_blocks = norm.reshape(blocks, tile)
    me = lax.axis_index("nodes").astype(jnp.int32)
    place = lax.axis_index("feat").astype(jnp.int32).reshape(1)
    meta = jnp.concatenate(
        [
            src_block[0] + 64 * dst_block[0],
            jnp.concatenate([tile_counts, tile_counts], axis=1),
            jnp.full((1, slots), me, jnp.int32),
        ],
        axis=0,
    )

    def move(value, dx, dy, dc):
        pairs = []
        for i in range(slabs):
            x, y, c = i // 8, (i // 2) % 4, i % 2
            pairs.append((i, ((x + dx) % 2) * 8 + ((y + dy) % 4) * 2 + (c + dc) % 2))
        return lax.ppermute(value, "nodes", pairs)

    scaled = pl.pallas_call(
        scale_kernel,
        out_shape=jax.ShapeDtypeStruct((blocks, feat_local, LANES), BF16),
        compiler_params=params(), name="scale",
    )(feats.T, norm_blocks)
    payload = pl.pallas_call(
        payload_kernel,
        out_shape=jax.ShapeDtypeStruct((peers, per_peer + 2, hid_local, LANES), BF16),
        compiler_params=params(), name="payload",
    )(cotangent.T, weight, bias.reshape(1, hid_local))
    hops = [(0, 0), (0, 1), (0, 3), (1, 0), (1, 1), (1, 3), (0, 2), (1, 2)]
    pieces = {hop: scaled if hop == (0, 0) else move(scaled, *hop, 0) for hop in hops}
    received = lax.all_to_all(payload, "feat", 0, 0)
    total = None
    groups = [hops[:1], hops[1:4], hops[4:6], hops[6:]]
    for g, group in enumerate(groups):
        xs, froms = [], []
        for dx, dy in group:
            for dc in (0, 1):
                xs.append(move(pieces[dx, dy], 0, 0, 1) if dc else pieces[dx, dy])
                froms.append(((-dx) % 2, (-dy) % 4, dc))
        total = forward_call(froms, xs, meta, own_tiles, total, norm_blocks if g == len(groups) - 1 else None, peers)
    agg = lax.all_to_all(total, "feat", 0, 0)
    back, sent = pl.pallas_call(
        dense_kernel,
        out_shape=(
            jax.ShapeDtypeStruct((peers, per_peer, feat_local, LANES), BF16),
            jax.ShapeDtypeStruct((peers, per_peer + 3, hid_local, LANES), BF16),
        ),
        in_specs=[spec(SMEM), spec(VMEM), spec(VMEM), spec(VMEM)],
        compiler_params=params(), name="dense",
    )(place, agg, received, norm_blocks)
    back = lax.all_to_all(back, "feat", 0, 0)
    collected = lax.all_to_all(sent, "feat", 0, 0)

    order = [(1, 2), (0, 2), (1, 1), (1, 3), (0, 1), (0, 3), (1, 0), (0, 0)]
    halves = [order[:4], order[4:]]
    swapped = []
    for half in halves:
        parts = backward_call([(dx, dy, 1) for dx, dy in half], back, meta, own_tiles, None, None)
        swapped.append([move(p, 0, 0, 1) for p in parts])
    arrived, kept = [], None
    for half, adds in zip(halves, swapped):
        stay = half.index((0, 0)) if (0, 0) in half else None
        parts = backward_call([(dx, dy, 0) for dx, dy in half], back, meta, own_tiles, adds, stay)
        for (dx, dy), p in zip(half, parts):
            if (dx, dy) == (0, 0):
                kept = p
            else:
                arrived.append(move(p, dx, dy, 0))

    hidden, summed = pl.pallas_call(
        collect_kernel,
        out_shape=(
            jax.ShapeDtypeStruct((hid_local, rows), BF16),
            jax.ShapeDtypeStruct((2 * hid_local, LANES), F32),
        ),
        compiler_params=params(), name="collect",
    )(collected)
    for i in range(4):
        pairs = []
        for n in range(slabs):
            x, y, c = n // 8, (n // 2) % 4, n % 2
            c, y, x = (c ^ 1, y, x) if i == 0 else (c, y ^ 1, x) if i == 1 else (c, 3 - y, x) if i == 2 else (c, y, x ^ 1)
            pairs.append((n, x * 8 + y * 2 + c))
        summed = summed + lax.ppermute(summed, "nodes", pairs)
    summed = summed * (rows * slabs) ** (-0.5)
    halves_of = hid_local // feat_local
    grad_weight = jnp.concatenate([summed[h * feat_local:(h + 1) * feat_local] for h in range(halves_of)], axis=1)
    low = hid_local + 8 * halves_of
    bias_row = jnp.concatenate([summed[hid_local + 8 * h] + summed[low + 8 * h] for h in range(halves_of)])
    grad_bias = lax.dynamic_slice(bias_row, (place[0] * hid_local,), (hid_local,))

    grad_feats = pl.pallas_call(
        finish_kernel,
        out_shape=jax.ShapeDtypeStruct((feat_local, rows), F32),
        compiler_params=params(), name="finish",
    )(kept, norm_blocks, *arrived).T
    return hidden.T, grad_weight, grad_bias, grad_feats


def solution(mesh):
    return jax.shard_map(
        on_device,
        mesh=mesh,
        in_specs=(
            P("nodes", "feat"),
            P("nodes", None, None, None, None),
            P("nodes", None, None),
            P("nodes", None, None),
            P("nodes", None),
            P("nodes"),
            P("feat", None),
            P("feat"),
            P("nodes", "feat"),
        ),
        out_specs=(P("nodes", "feat"), P("feat", None), P("feat"), P("nodes", "feat")),
        check_vma=False,
    )
```

time: 167 us -> 158 us (0.946); the launches traced: 165 us -> 158 us
  local copies, waits for them, and re-layouts: 9 us -> 26 us
  Pallas kernels: 47.7 us -> 36.9 us
  starting transfers between devices: 65.7 us -> 60.1 us
  waiting for transfers between devices: 26.7 us -> 21.6 us
  other arithmetic: 4.43 us -> 2.17 us
    unnamed x60 -> x20, local copies, waits for them, and re-layouts: 3.53 us -> 25.3 us
    pallas_call x9 -> x11, Pallas kernels: 41.5 us -> 33.3 us  [the longest x4 16.7 us: forward_call(): pl.pallas_call(functools.partial(forward_kernel, hops, first, last), out_...]
    all_to_all x3 -> x2, waiting for transfers between devices: 14.1 us -> 7.23 us  [the longest x1 7.23 us: on_device(): agg = lax.all_to_all(total, 'feat', 0, 0)]
    another operation x7 -> x0, other arithmetic: 4.38 us -> none  [the longest x3 1.84 us: on_device(): jnp.stack(ids).astype(jnp.int32)]
    ppermute x30, starting transfers between devices: 45.4 us -> 41.5 us  [move(): return lax.ppermute(value, 'nodes', pairs)]
    all_to_all x3 -> x2, starting transfers between devices: 13.1 us -> 9.5 us  [the longest x1 5.96 us: on_device(): agg = lax.all_to_all(total, 'feat', 0, 0)]
    slice x4 -> x1, local copies, waits for them, and re-layouts: 2.22 us -> 0.01 us  [on_device(): summed[h * feat_local:(h + 1) * feat_local]]
    ppermute x4, starting transfers between devices: 1.91 us -> 3.75 us  [on_device(): summed = summed + lax.ppermute(summed, 'nodes', pairs)]
  transfers between devices with their start and end apart: 38 -> 37, of which waited for: 7 -> 10; matrix products, arithmetic and copies ran while one was open for 4% -> 1% of each run, Pallas kernels for 24% -> 22%
where the time goes in v2:
time: 158 us
  starting transfers between devices  60.1 us (38%)
  Pallas kernels  36.9 us (23%)
  local copies, waits for them, and re-layouts  26 us (16%)
  waiting for transfers between devices  21.6 us (14%)
  blocking collectives  9.8 us (6%)
  other arithmetic  2.17 us (1%)
    ppermute x30, starting transfers between devices, move(): return lax.ppermute(value, 'nodes', pairs)  41.5 us
    unnamed x20, local copies, waits for them, and re-layouts  25.3 us
    pallas_call x4, Pallas kernels, forward_call(): pl.pallas_call(functools.partial(forward_kernel, hops, first, last), out_...  16.7 us
    pallas_call x4, Pallas kernels, backward_call(): pl.pallas_call(functools.partial(backward_kernel, hops, added), out_shape...  14.7 us
    ppermute x30, waiting for transfers between devices, move(): return lax.ppermute(value, 'nodes', pairs)  13.4 us
    all_to_all x1, blocking collectives, on_device(): back = lax.all_to_all(back, 'feat', 0, 0)  9.8 us
    all_to_all x1, waiting for transfers between devices, on_device(): agg = lax.all_to_all(total, 'feat', 0, 0)  7.23 us
    all_to_all x1, starting transfers between devices, on_device(): agg = lax.all_to_all(total, 'feat', 0, 0)  5.96 us
  transfers between devices with their start and end apart: 37, of which 10 were waited for; matrix products, arithmetic and copies ran while one was open for 1% of the time, Pallas kernels for 22%

profile of v2, /device:TPU:0, one launch (start us, length us, event | category | flops | bytes accessed | tf_op | source)
XLA Modules:
  0.0 157.5 jit_solution(3897369438854314843)
XLA Ops:
  2.5 3.2 %collective-permute-start.12 = (bf16[64,16,128]{2,1,0:T(8,128)(2,1)S(1)}, bf16[64,16,128]{2,1,0:T(8,128)(2,1)S(1)}, u32[]{:S(2)}, u32[]{:S(2)}) collective-permute-start(bf16[64,16,128]{2,1,0:T(8,128)(2,1)S(1)} %scale.1.refs_0_), channel_id=1, source_target_pairs={{0,64},{8,72},{16,80},{24,88},{32,96},{40,104},{48,112},{56,120},{... | collective-permute-start | bytes 786440 | tf_op jit(solution)/shard_map/ppermute | solution.py:345
  5.7 3.0 %collective-permute-start.10 = (bf16[64,16,128]{2,1,0:T(8,128)(2,1)S(1)}, bf16[64,16,128]{2,1,0:T(8,128)(2,1)S(1)}, u32[]{:S(2)}, u32[]{:S(2)}) collective-permute-start(bf16[64,16,128]{2,1,0:T(8,128)(2,1)S(1)} %scale.1.refs_0_), channel_id=1, source_target_pairs={{0,48},{8,56},{16,0},{24,8},{32,16},{40,24},{48,32},{56,40},{64,11... | collective-permute-start | bytes 786440 | tf_op jit(solution)/shard_map/ppermute | solution.py:345
  8.7 3.2 %collective-permute-start.6 = (bf16[64,16,128]{2,1,0:T(8,128)(2,1)S(1)}, bf16[64,16,128]{2,1,0:T(8,128)(2,1)S(1)}, u32[]{:S(2)}, u32[]{:S(2)}) collective-permute-start(bf16[64,16,128]{2,1,0:T(8,128)(2,1)S(1)} %scale.1.refs_0_), channel_id=1, source_target_pairs={{0,112},{8,120},{16,64},{24,72},{32,80},{40,88},{48,96},{56,104},{... | collective-permute-start | bytes 786440 | tf_op jit(solution)/shard_map/ppermute | solution.py:345
  11.9 1.3 collective-permute-start.4
  13.1 5.8 %collective-permute-start.2 = (bf16[64,16,128]{2,1,0:T(8,128)(2,1)S(1)}, bf16[64,16,128]{2,1,0:T(8,128)(2,1)S(1)}, u32[]{:S(2)}, u32[]{:S(2)}) collective-permute-start(bf16[64,16,128]{2,1,0:T(8,128)(2,1)S(1)} %scale.1.refs_0_), channel_id=1, source_target_pairs={{0,96},{8,104},{16,112},{24,120},{32,64},{40,72},{48,80},{56,88},{... | collective-permute-start | bytes 786440 | tf_op jit(solution)/shard_map/ppermute | solution.py:345
  19.1 3.7 %collective-permute-start = (bf16[64,16,128]{2,1,0:T(8,128)(2,1)S(1)}, bf16[64,16,128]{2,1,0:T(8,128)(2,1)S(1)}, u32[]{:S(2)}, u32[]{:S(2)}) collective-permute-start(bf16[64,16,128]{2,1,0:T(8,128)(2,1)S(1)} %scale.1.refs_0_), channel_id=1, source_target_pairs={{0,32},{8,40},{16,48},{24,56},{32,0},{40,8},{48,16},{56,24},{64,96... | collective-permute-start | bytes 786440 | tf_op jit(solution)/shard_map/ppermute | solution.py:345
  26.7 5.3 %all-to-all-start.1 = ((bf16[8,10,32,128]{3,2,1,0:T(8,128)(2,1)}), bf16[8,10,32,128]{3,2,1,0:T(8,128)(2,1)S(1)}, u32[]{:S(2)}, u32[]{:S(2)}) async-start(bf16[8,10,32,128]{3,2,1,0:T(8,128)(2,1)} %payload.1), calls=%async_computation.1 | async-start | bytes 1310720 | tf_op jit(solution)/shard_map/all_to_all | solution.py:359
  32.6 5.3 %collective-permute-done.refs_0_ = bf16[64,16,128]{2,1,0:T(8,128)(2,1)S(1)} collective-permute-done((bf16[64,16,128]{2,1,0:T(8,128)(2,1)S(1)}, bf16[64,16,128]{2,1,0:T(8,128)(2,1)S(1)}, u32[]{:S(2)}, u32[]{:S(2)}) %collective-permute-start) | collective-permute-done | bytes 262176 | tf_op jit(solution)/shard_map/ppermute | solution.py:345
  40.1 5.8 %copy-done = bf16[1,16,32,128,128]{4,3,2,1,0:T(8,128)(2,1)S(1)} copy-done((bf16[1,16,32,128,128]{4,3,2,1,0:T(8,128)(2,1)S(1)}, bf16[1,16,32,128,128]{4,3,2,1,0:T(8,128)(2,1)}, u32[]{:S(2)}) %copy-start) | copy-done | bytes 16777240
  45.9 1.9 %forward_tiles.4.refs_7_ = f32[64,16,128]{2,1,0:T(8,128)S(1)} custom-call(s32[18,32]{1,0:T(8,128)S(1)} %add_add_fusion.meta, bf16[64,16,128]{2,1,0:T(8,128)(2,1)S(1)} %scale.1.refs_0_, bf16[64,16,128]{2,1,0:T(8,128)(2,1)S(1)} %collective-permute-done.14.refs_1_, bf16[16,32,128,128]{3,2,1,0:T(8,128)(2,1)S(1)} %bitcast.30), custom_call_target="tpu_custom_call" | custom-call | flops 16777216 | bytes 2097152 | tf_op jit(solution)/shard_map/forward_tiles/pallas_call | solution.py:152
  47.8 3.9 %copy-done.1 = bf16[1,16,32,128,128]{4,3,2,1,0:T(8,128)(2,1)S(1)} copy-done((bf16[1,16,32,128,128]{4,3,2,1,0:T(8,128)(2,1)S(1)}, bf16[1,16,32,128,128]{4,3,2,1,0:T(8,128)(2,1)}, u32[]{:S(2)}) %copy-start.1) | copy-done | bytes 16777240
  51.7 6.3 %forward_tiles.5.refs_5_ = f32[64,16,128]{2,1,0:T(8,128)S(1)} custom-call(s32[18,32]{1,0:T(8,128)S(1)} %add_add_fusion.meta, bf16[64,16,128]{2,1,0:T(8,128)(2,1)S(1)} %collective-permute-done.8.refs_0_, bf16[64,16,128]{2,1,0:T(8,128)(2,1)} %collective-permute-done.9.refs_1_, bf16[64,16,128]{2,1,0:T(8,128)(2,1)S(1)} %collective-permute-done.10.refs_2_, ...), custom_call_target="tpu_custom_call" | custom-call | flops 50331648 | bytes 6291456 | tf_op jit(solution)/shard_map/forward_tiles/pallas_call | solution.py:152
  58.0 3.9 %forward_tiles.6.refs_5_ = f32[64,16,128]{2,1,0:T(8,128)S(1)} custom-call(s32[18,32]{1,0:T(8,128)S(1)} %add_add_fusion.meta, bf16[64,16,128]{2,1,0:T(8,128)(2,1)S(1)} %collective-permute-done.4.refs_0_, bf16[64,16,128]{2,1,0:T(8,128)(2,1)} %collective-permute-done.5.refs_1_, bf16[64,16,128]{2,1,0:T(8,128)(2,1)S(1)} %collective-permute-done.6.refs_2_, ...), custom_call_target="tpu_custom_call" | custom-call | flops 33554432 | bytes 4194304 | tf_op jit(solution)/shard_map/forward_tiles/pallas_call | solution.py:152
  62.0 4.6 %forward_tiles.7 = bf16[8,8,16,128]{3,2,1,0:T(8,128)(2,1)} custom-call(s32[18,32]{1,0:T(8,128)S(1)} %add_add_fusion.meta, bf16[64,16,128]{2,1,0:T(8,128)(2,1)S(1)} %collective-permute-done.refs_0_, bf16[64,16,128]{2,1,0:T(8,128)(2,1)} %collective-permute-done.1.refs_1_, bf16[64,16,128]{2,1,0:T(8,128)(2,1)S(1)} %collective-permute-done.2.refs_2_, ...), custom_call_target="tpu_custom_call" | custom-call | flops 33554432 | bytes 4194304 | tf_op jit(solution)/shard_map/forward_tiles/pallas_call | solution.py:152
  66.6 6.0 %all-to-all-start = ((bf16[8,8,16,128]{3,2,1,0:T(8,128)(2,1)}), bf16[8,8,16,128]{3,2,1,0:T(8,128)(2,1)S(1)}, u32[]{:S(2)}, u32[]{:S(2)}) async-start(bf16[8,8,16,128]{3,2,1,0:T(8,128)(2,1)} %forward_tiles.7), calls=%async_computation | async-start | bytes 524288 | tf_op jit(solution)/shard_map/all_to_all | solution.py:369
  72.6 7.2 %all-to-all-done.agg = bf16[8,8,16,128]{3,2,1,0:T(8,128)(2,1)S(1)} async-done(((bf16[8,8,16,128]{3,2,1,0:T(8,128)(2,1)}), bf16[8,8,16,128]{3,2,1,0:T(8,128)(2,1)S(1)}, u32[]{:S(2)}, u32[]{:S(2)}) %all-to-all-start) | async-done | bytes 262176 | tf_op jit(solution)/shard_map/all_to_all | solution.py:369
  79.8 2.5 %dense.1 = (bf16[8,8,16,128]{3,2,1,0:T(8,128)(2,1)S(1)}, bf16[8,11,32,128]{3,2,1,0:T(8,128)(2,1)}) custom-call(s32[1]{0:T(128)} %bitcast.place, bf16[8,8,16,128]{3,2,1,0:T(8,128)(2,1)S(1)} %all-to-all-done.agg, bf16[8,10,32,128]{3,2,1,0:T(8,128)(2,1)S(1)} %all-to-all-done.1.received, f32[64,128]{1,0:T(8,128)S(1)} %bitcast.40), custom_call_target="tpu_custom_call" | custom-call | tf_op jit(solution)/shard_map/dense/pallas_call | solution.py:370
  82.3 9.8 %all_to_all.20.refs_0_ = bf16[8,8,16,128]{3,2,1,0:T(8,128)(2,1)S(1)} all-to-all(bf16[8,8,16,128]{3,2,1,0:T(8,128)(2,1)S(1)} %get-tuple-element.27), channel_id=1, replica_groups=mesh['nodes'=16,'feat'=8] {'feat'}, dimensions={0} | all-to-all | bytes 524288 | tf_op jit(solution)/shard_map/all_to_all | solution.py:379
  92.1 3.5 %all-to-all-start.2 = ((bf16[8,11,32,128]{3,2,1,0:T(8,128)(2,1)}), bf16[8,11,32,128]{3,2,1,0:T(8,128)(2,1)S(1)}, u32[]{:S(2)}, u32[]{:S(2)}) async-start(bf16[8,11,32,128]{3,2,1,0:T(8,128)(2,1)} %get-tuple-element.24), calls=%async_computation.2 | async-start | bytes 1441792 | tf_op jit(solution)/shard_map/all_to_all | solution.py:380
  95.7 5.8 %copy-done.2 = bf16[1,16,32,128,128]{4,3,2,1,0:T(8,128)(2,1)S(1)} copy-done((bf16[1,16,32,128,128]{4,3,2,1,0:T(8,128)(2,1)S(1)}, bf16[1,16,32,128,128]{4,3,2,1,0:T(8,128)(2,1)}, u32[]{:S(2)}) %copy-start.2) | copy-done | bytes 16777240
  101.5 3.8 %backward_tiles.6 = (bf16[8,128,128]{2,1,0:T(8,128)(2,1)}, bf16[8,128,128]{2,1,0:T(8,128)(2,1)}, bf16[8,128,128]{2,1,0:T(8,128)(2,1)}, bf16[8,128,128]{2,1,0:T(8,128)(2,1)S(1)}) custom-call(s32[18,32]{1,0:T(8,128)S(1)} %add_add_fusion.meta, bf16[8,8,16,128]{3,2,1,0:T(8,128)(2,1)S(1)} %all_to_all.20.refs_0_, bf16[16,32,128,128]{3,2,1,0:T(8,128)(2,1)S(1)} %bitcast.34), custom_call_target="tpu_custom_call" | custom-call | flops 33554432 | bytes 4194304 | tf_op jit(solution)/shard_map/backward_tiles/pallas_call | solution.py:243
  106.4 4.1 %backward_tiles.4 = (bf16[8,128,128]{2,1,0:T(8,128)(2,1)S(1)}, bf16[8,128,128]{2,1,0:T(8,128)(2,1)}, bf16[8,128,128]{2,1,0:T(8,128)(2,1)S(1)}, bf16[8,128,128]{2,1,0:T(8,128)(2,1)S(1)}) custom-call(s32[18,32]{1,0:T(8,128)S(1)} %add_add_fusion.meta, bf16[8,8,16,128]{3,2,1,0:T(8,128)(2,1)S(1)} %all_to_all.20.refs_0_, bf16[16,32,128,128]{3,2,1,0:T(8,128)(2,1)S(1)} %bitcast.35), custom_call_target="tpu_custom_call" | custom-call | flops 33554432 | bytes 4194304 | tf_op jit(solution)/shard_map/backward_tiles/pallas_call | solution.py:243
  113.9 5.8 %copy-done.3 = bf16[1,16,32,128,128]{4,3,2,1,0:T(8,128)(2,1)S(1)} copy-done((bf16[1,16,32,128,128]{4,3,2,1,0:T(8,128)(2,1)S(1)}, bf16[1,16,32,128,128]{4,3,2,1,0:T(8,128)(2,1)}, u32[]{:S(2)}) %copy-start.3) | copy-done | bytes 16777240
  119.7 3.6 %backward_tiles.7 = (bf16[8,128,128]{2,1,0:T(8,128)(2,1)S(1)}, bf16[8,128,128]{2,1,0:T(8,128)(2,1)S(1)}, bf16[8,128,128]{2,1,0:T(8,128)(2,1)S(1)}, bf16[8,128,128]{2,1,0:T(8,128)(2,1)S(1)}) custom-call(s32[18,32]{1,0:T(8,128)S(1)} %add_add_fusion.meta, bf16[8,8,16,128]{3,2,1,0:T(8,128)(2,1)S(1)} %all_to_all.20.refs_0_, ...), custom_call_target="tpu_custom_call" | custom-call | flops 33554432 | bytes 4194304 | tf_op jit(solution)/shard_map/backward_tiles/pallas_call | solution.py:243
  123.4 4.6 %collective-permute-start.27 = (bf16[64,16,128]{2,1,0:T(8,128)(2,1)S(1)}, bf16[64,16,128]{2,1,0:T(8,128)(2,1)S(1)}, u32[]{:S(2)}, u32[]{:S(2)}) collective-permute-start(bf16[64,16,128]{2,1,0:T(8,128)(2,1)S(1)} %bitcast.50), channel_id=1, source_target_pairs={{0,96},{8,104},{16,112},{24,120},{32,64},{40,72},{48,80},{56,88},{... | collective-permute-start | bytes 786440 | tf_op jit(solution)/shard_map/ppermute | solution.py:345
  128.0 3.2 %collective-permute-start.17 = (f32[64,128]{1,0:T(8,128)S(1)}, f32[64,128]{1,0:T(8,128)S(1)}, u32[]{:S(2)}, u32[]{:S(2)}) collective-permute-start(f32[64,128]{1,0:T(8,128)S(1)} %add.36), channel_id=1, source_target_pairs={{0,48},{8,56},{16,32},{24,40},{32,16},{40,24},{48,0},{56,8},{64,11... | collective-permute-start | bytes 98312 | tf_op jit(solution)/shard_map/ppermute | solution.py:412
  131.2 5.6 %collective-permute-start.30 = (bf16[64,16,128]{2,1,0:T(8,128)(2,1)S(1)}, bf16[64,16,128]{2,1,0:T(8,128)(2,1)S(1)}, u32[]{:S(2)}, u32[]{:S(2)}) collective-permute-start(bf16[64,16,128]{2,1,0:T(8,128)(2,1)S(1)} %bitcast.45), channel_id=1, source_target_pairs={{0,112},{8,120},{16,64},{24,72},{32,80},{40,88},{48,96},{56,104},{... | collective-permute-start | bytes 786440 | tf_op jit(solution)/shard_map/ppermute | solution.py:345
  136.8 3.2 %backward_tiles.5 = (bf16[8,128,128]{2,1,0:T(8,128)(2,1)}, bf16[8,128,128]{2,1,0:T(8,128)(2,1)S(1)}, bf16[8,128,128]{2,1,0:T(8,128)(2,1)S(1)}, f32[64,16,128]{2,1,0:T(8,128)S(1)}) custom-call(s32[18,32]{1,0:T(8,128)S(1)} %add_add_fusion.meta, bf16[8,8,16,128]{3,2,1,0:T(8,128)(2,1)S(1)} %all_to_all.20.refs_0_, bf16[16,32,128,128]{3,2,1,0:T(8,128)(2,1)S(1)} %bitcast.37, ...), custom_call_target="tpu_custom_call" | custom-call | flops 33554432 | bytes 4194304 | tf_op jit(solution)/shard_map/backward_tiles/pallas_call | solution.py:243
  140.0 2.4 %collective-permute-start.31 = (bf16[64,16,128]{2,1,0:T(8,128)(2,1)}, bf16[64,16,128]{2,1,0:T(8,128)(2,1)S(1)}, u32[]{:S(2)}, u32[]{:S(2)}) collective-permute-start(bf16[64,16,128]{2,1,0:T(8,128)(2,1)} %bitcast.22), channel_id=1, source_target_pairs={{0,16},{8,24},{16,32},{24,40},{32,48},{40,56},{48,0},{56,8},{64,80... | collective-permute-start | bytes 786440 | tf_op jit(solution)/shard_map/ppermute | solution.py:345
  142.4 3.4 %collective-permute-done.28.refs_1_ = bf16[64,16,128]{2,1,0:T(8,128)(2,1)S(1)} collective-permute-done((bf16[64,16,128]{2,1,0:T(8,128)(2,1)S(1)}, bf16[64,16,128]{2,1,0:T(8,128)(2,1)S(1)}, u32[]{:S(2)}, u32[]{:S(2)}) %collective-permute-start.28) | collective-permute-done | bytes 262176 | tf_op jit(solution)/shard_map/ppermute | solution.py:345
  145.7 5.0 %collective-permute-start.33 = (bf16[64,16,128]{2,1,0:T(8,128)(2,1)S(1)}, bf16[64,16,128]{2,1,0:T(8,128)(2,1)S(1)}, u32[]{:S(2)}, u32[]{:S(2)}) collective-permute-start(bf16[64,16,128]{2,1,0:T(8,128)(2,1)S(1)} %bitcast.53), channel_id=1, source_target_pairs={{0,64},{8,72},{16,80},{24,88},{32,96},{40,104},{48,112},{56,120},{... | collective-permute-start | bytes 786440 | tf_op jit(solution)/shard_map/ppermute | solution.py:345
  151.3 2.7 %collective-permute-done.32.refs_5_ = bf16[64,16,128]{2,1,0:T(8,128)(2,1)S(1)} collective-permute-done((bf16[64,16,128]{2,1,0:T(8,128)(2,1)S(1)}, bf16[64,16,128]{2,1,0:T(8,128)(2,1)S(1)}, u32[]{:S(2)}, u32[]{:S(2)}) %collective-permute-start.32) | collective-permute-done | bytes 262176 | tf_op jit(solution)/shard_map/ppermute | solution.py:345
  (88 shorter events, 17.3 us)
Async XLA Ops:
  2.4 9.5 %collective-permute-start.14 = (bf16[64,16,128]{2,1,0:T(8,128)(2,1)S(1)}, bf16[64,16,128]{2,1,0:T(8,128)(2,1)S(1)}, u32[]{:S(2)}, u32[]{:S(2)}) collective-permute-start(bf16[64,16,128]{2,1,0:T(8,128)(2,1)S(1)} %scale.1.refs_0_), channel_id=1, source_target_pairs={{0,8},{8,0},{16,24},{24,16},{32,40},{40,32},{48,56},{56,48},{64,72... | collective-permute-start | bytes 786440 | tf_op jit(solution)/shard_map/ppermute | solution.py:345
  2.5 10.6 %collective-permute-start.12 = (bf16[64,16,128]{2,1,0:T(8,128)(2,1)S(1)}, bf16[64,16,128]{2,1,0:T(8,128)(2,1)S(1)}, u32[]{:S(2)}, u32[]{:S(2)}) collective-permute-start(bf16[64,16,128]{2,1,0:T(8,128)(2,1)S(1)} %scale.1.refs_0_), channel_id=1, source_target_pairs={{0,64},{8,72},{16,80},{24,88},{32,96},{40,104},{48,112},{56,120},{... | collective-permute-start | bytes 786440 | tf_op jit(solution)/shard_map/ppermute | solution.py:345
  5.7 13.4 %collective-permute-start.10 = (bf16[64,16,128]{2,1,0:T(8,128)(2,1)S(1)}, bf16[64,16,128]{2,1,0:T(8,128)(2,1)S(1)}, u32[]{:S(2)}, u32[]{:S(2)}) collective-permute-start(bf16[64,16,128]{2,1,0:T(8,128)(2,1)S(1)} %scale.1.refs_0_), channel_id=1, source_target_pairs={{0,48},{8,56},{16,0},{24,8},{32,16},{40,24},{48,32},{56,40},{64,11... | collective-permute-start | bytes 786440 | tf_op jit(solution)/shard_map/ppermute | solution.py:345
  8.7 14.2 %collective-permute-start.8 = (bf16[64,16,128]{2,1,0:T(8,128)(2,1)S(1)}, bf16[64,16,128]{2,1,0:T(8,128)(2,1)S(1)}, u32[]{:S(2)}, u32[]{:S(2)}) collective-permute-start(bf16[64,16,128]{2,1,0:T(8,128)(2,1)S(1)} %scale.1.refs_0_), channel_id=1, source_target_pairs={{0,16},{8,24},{16,32},{24,40},{32,48},{40,56},{48,0},{56,8},{64,80... | collective-permute-start | bytes 786440 | tf_op jit(solution)/shard_map/ppermute | solution.py:345
  8.7 14.2 %collective-permute-start.6 = (bf16[64,16,128]{2,1,0:T(8,128)(2,1)S(1)}, bf16[64,16,128]{2,1,0:T(8,128)(2,1)S(1)}, u32[]{:S(2)}, u32[]{:S(2)}) collective-permute-start(bf16[64,16,128]{2,1,0:T(8,128)(2,1)S(1)} %scale.1.refs_0_), channel_id=1, source_target_pairs={{0,112},{8,120},{16,64},{24,72},{32,80},{40,88},{48,96},{56,104},{... | collective-permute-start | bytes 786440 | tf_op jit(solution)/shard_map/ppermute | solution.py:345
  11.9 20.2 %collective-permute-start.4 = (bf16[64,16,128]{2,1,0:T(8,128)(2,1)S(1)}, bf16[64,16,128]{2,1,0:T(8,128)(2,1)S(1)}, u32[]{:S(2)}, u32[]{:S(2)}) collective-permute-start(bf16[64,16,128]{2,1,0:T(8,128)(2,1)S(1)} %scale.1.refs_0_), channel_id=1, source_target_pairs={{0,80},{8,88},{16,96},{24,104},{32,112},{40,120},{48,64},{56,72},{... | collective-permute-start | bytes 786440 | tf_op jit(solution)/shard_map/ppermute | solution.py:345
  13.1 19.3 %collective-permute-start.2 = (bf16[64,16,128]{2,1,0:T(8,128)(2,1)S(1)}, bf16[64,16,128]{2,1,0:T(8,128)(2,1)S(1)}, u32[]{:S(2)}, u32[]{:S(2)}) collective-permute-start(bf16[64,16,128]{2,1,0:T(8,128)(2,1)S(1)} %scale.1.refs_0_), channel_id=1, source_target_pairs={{0,96},{8,104},{16,112},{24,120},{32,64},{40,72},{48,80},{56,88},{... | collective-permute-start | bytes 786440 | tf_op jit(solution)/shard_map/ppermute | solution.py:345
  19.1 18.8 %collective-permute-start = (bf16[64,16,128]{2,1,0:T(8,128)(2,1)S(1)}, bf16[64,16,128]{2,1,0:T(8,128)(2,1)S(1)}, u32[]{:S(2)}, u32[]{:S(2)}) collective-permute-start(bf16[64,16,128]{2,1,0:T(8,128)(2,1)S(1)} %scale.1.refs_0_), channel_id=1, source_target_pairs={{0,32},{8,40},{16,48},{24,56},{32,0},{40,8},{48,16},{56,24},{64,96... | collective-permute-start | bytes 786440 | tf_op jit(solution)/shard_map/ppermute | solution.py:345
  22.8 15.1 %collective-permute-start.13 = (bf16[64,16,128]{2,1,0:T(8,128)(2,1)S(1)}, bf16[64,16,128]{2,1,0:T(8,128)(2,1)S(1)}, u32[]{:S(2)}, u32[]{:S(2)}) collective-permute-start(bf16[64,16,128]{2,1,0:T(8,128)(2,1)S(1)} %collective-permute-done.12.refs_4_), channel_id=1, source_target_pairs={{0,8},{8,0},{16,24},{24,16},{32,40},{40,32},{48,56},{56,48},{64,72... | collective-permute-start | bytes 786440 | tf_op jit(solution)/shard_map/ppermute | solution.py:345
  22.9 15.6 %collective-permute-start.11 = (bf16[64,16,128]{2,1,0:T(8,128)(2,1)S(1)}, bf16[64,16,128]{2,1,0:T(8,128)(2,1)}, u32[]{:S(2)}, u32[]{:S(2)}) collective-permute-start(bf16[64,16,128]{2,1,0:T(8,128)(2,1)S(1)} %collective-permute-done.10.refs_2_), channel_id=1, source_target_pairs={{0,8},{8,0},{16,24},{24,16},{32,40},{40,32},{48,56},{56,48},{64,72... | collective-permute-start | bytes 786440 | tf_op jit(solution)/shard_map/ppermute | solution.py:345
  26.7 39.9 %all-to-all-start.1 = ((bf16[8,10,32,128]{3,2,1,0:T(8,128)(2,1)}), bf16[8,10,32,128]{3,2,1,0:T(8,128)(2,1)S(1)}, u32[]{:S(2)}, u32[]{:S(2)}) async-start(bf16[8,10,32,128]{3,2,1,0:T(8,128)(2,1)} %payload.1), calls=%async_computation.1 | async-start | bytes 1310720 | tf_op jit(solution)/shard_map/all_to_all | solution.py:359
  32.0 15.8 %collective-permute-start.9 = (bf16[64,16,128]{2,1,0:T(8,128)(2,1)S(1)}, bf16[64,16,128]{2,1,0:T(8,128)(2,1)}, u32[]{:S(2)}, u32[]{:S(2)}) collective-permute-start(bf16[64,16,128]{2,1,0:T(8,128)(2,1)S(1)} %collective-permute-done.8.refs_0_), channel_id=1, source_target_pairs={{0,8},{8,0},{16,24},{24,16},{32,40},{40,32},{48,56},{56,48},{64,72... | collective-permute-start | bytes 786440 | tf_op jit(solution)/shard_map/ppermute | solution.py:345
  32.4 25.6 %collective-permute-start.7 = (bf16[64,16,128]{2,1,0:T(8,128)(2,1)S(1)}, bf16[64,16,128]{2,1,0:T(8,128)(2,1)}, u32[]{:S(2)}, u32[]{:S(2)}) collective-permute-start(bf16[64,16,128]{2,1,0:T(8,128)(2,1)S(1)} %collective-permute-done.6.refs_2_), channel_id=1, source_target_pairs={{0,8},{8,0},{16,24},{24,16},{32,40},{40,32},{48,56},{56,48},{64,72... | collective-permute-start | bytes 786440 | tf_op jit(solution)/shard_map/ppermute | solution.py:345
  37.9 20.1 %collective-permute-start.5 = (bf16[64,16,128]{2,1,0:T(8,128)(2,1)S(1)}, bf16[64,16,128]{2,1,0:T(8,128)(2,1)}, u32[]{:S(2)}, u32[]{:S(2)}) collective-permute-start(bf16[64,16,128]{2,1,0:T(8,128)(2,1)S(1)} %collective-permute-done.4.refs_0_), channel_id=1, source_target_pairs={{0,8},{8,0},{16,24},{24,16},{32,40},{40,32},{48,56},{56,48},{64,72... | collective-permute-start | bytes 786440 | tf_op jit(solution)/shard_map/ppermute | solution.py:345
  38.0 24.0 %collective-permute-start.3 = (bf16[64,16,128]{2,1,0:T(8,128)(2,1)S(1)}, bf16[64,16,128]{2,1,0:T(8,128)(2,1)}, u32[]{:S(2)}, u32[]{:S(2)}) collective-permute-start(bf16[64,16,128]{2,1,0:T(8,128)(2,1)S(1)} %collective-permute-done.2.refs_2_), channel_id=1, source_target_pairs={{0,8},{8,0},{16,24},{24,16},{32,40},{40,32},{48,56},{56,48},{64,72... | collective-permute-start | bytes 786440 | tf_op jit(solution)/shard_map/ppermute | solution.py:345
  38.5 23.5 %collective-permute-start.1 = (bf16[64,16,128]{2,1,0:T(8,128)(2,1)S(1)}, bf16[64,16,128]{2,1,0:T(8,128)(2,1)}, u32[]{:S(2)}, u32[]{:S(2)}) collective-permute-start(bf16[64,16,128]{2,1,0:T(8,128)(2,1)S(1)} %collective-permute-done.refs_0_), channel_id=1, source_target_pairs={{0,8},{8,0},{16,24},{24,16},{32,40},{40,32},{48,56},{56,48},{64,72... | collective-permute-start | bytes 786440 | tf_op jit(solution)/shard_map/ppermute | solution.py:345
  66.6 13.2 %all-to-all-start = ((bf16[8,8,16,128]{3,2,1,0:T(8,128)(2,1)}), bf16[8,8,16,128]{3,2,1,0:T(8,128)(2,1)S(1)}, u32[]{:S(2)}, u32[]{:S(2)}) async-start(bf16[8,8,16,128]{3,2,1,0:T(8,128)(2,1)} %forward_tiles.7), calls=%async_computation | async-start | bytes 524288 | tf_op jit(solution)/shard_map/all_to_all | solution.py:369
  92.1 18.5 %all-to-all-start.2 = ((bf16[8,11,32,128]{3,2,1,0:T(8,128)(2,1)}), bf16[8,11,32,128]{3,2,1,0:T(8,128)(2,1)S(1)}, u32[]{:S(2)}, u32[]{:S(2)}) async-start(bf16[8,11,32,128]{3,2,1,0:T(8,128)(2,1)} %get-tuple-element.24), calls=%async_computation.2 | async-start | bytes 1441792 | tf_op jit(solution)/shard_map/all_to_all | solution.py:380
  105.4 7.8 %collective-permute-start.23 = (bf16[64,16,128]{2,1,0:T(8,128)(2,1)}, bf16[64,16,128]{2,1,0:T(8,128)(2,1)S(1)}, u32[]{:S(2)}, u32[]{:S(2)}) collective-permute-start(bf16[64,16,128]{2,1,0:T(8,128)(2,1)} %bitcast.14), channel_id=1, source_target_pairs={{0,8},{8,0},{16,24},{24,16},{32,40},{40,32},{48,56},{56,48},{64,72... | collective-permute-start | bytes 786440 | tf_op jit(solution)/shard_map/ppermute | solution.py:345
  110.5 12.8 %collective-permute-start.20 = (bf16[64,16,128]{2,1,0:T(8,128)(2,1)}, bf16[64,16,128]{2,1,0:T(8,128)(2,1)S(1)}, u32[]{:S(2)}, u32[]{:S(2)}) collective-permute-start(bf16[64,16,128]{2,1,0:T(8,128)(2,1)} %bitcast.11), channel_id=1, source_target_pairs={{0,8},{8,0},{16,24},{24,16},{32,40},{40,32},{48,56},{56,48},{64,72... | collective-permute-start | bytes 786440 | tf_op jit(solution)/shard_map/ppermute | solution.py:345
  112.8 15.2 %collective-permute-start.19 = (bf16[64,16,128]{2,1,0:T(8,128)(2,1)S(1)}, bf16[64,16,128]{2,1,0:T(8,128)(2,1)S(1)}, u32[]{:S(2)}, u32[]{:S(2)}) collective-permute-start(bf16[64,16,128]{2,1,0:T(8,128)(2,1)S(1)} %bitcast.48), channel_id=1, source_target_pairs={{0,8},{8,0},{16,24},{24,16},{32,40},{40,32},{48,56},{56,48},{64,72... | collective-permute-start | bytes 786440 | tf_op jit(solution)/shard_map/ppermute | solution.py:345
  113.2 10.2 %collective-permute-start.16 = (f32[64,128]{1,0:T(8,128)S(1)}, f32[64,128]{1,0:T(8,128)S(1)}, u32[]{:S(2)}, u32[]{:S(2)}) collective-permute-start(f32[64,128]{1,0:T(8,128)S(1)} %add.35), channel_id=1, source_target_pairs={{0,16},{8,24},{16,0},{24,8},{32,48},{40,56},{48,32},{56,40},{64,80... | collective-permute-start | bytes 98312 | tf_op jit(solution)/shard_map/ppermute | solution.py:412
  113.3 17.9 %collective-permute-start.21 = (bf16[64,16,128]{2,1,0:T(8,128)(2,1)S(1)}, bf16[64,16,128]{2,1,0:T(8,128)(2,1)S(1)}, u32[]{:S(2)}, u32[]{:S(2)}) collective-permute-start(bf16[64,16,128]{2,1,0:T(8,128)(2,1)S(1)} %bitcast.47), channel_id=1, source_target_pairs={{0,8},{8,0},{16,24},{24,16},{32,40},{40,32},{48,56},{56,48},{64,72... | collective-permute-start | bytes 786440 | tf_op jit(solution)/shard_map/ppermute | solution.py:345
  113.6 17.6 %collective-permute-start.22 = (bf16[64,16,128]{2,1,0:T(8,128)(2,1)S(1)}, bf16[64,16,128]{2,1,0:T(8,128)(2,1)S(1)}, u32[]{:S(2)}, u32[]{:S(2)}) collective-permute-start(bf16[64,16,128]{2,1,0:T(8,128)(2,1)S(1)} %bitcast.46), channel_id=1, source_target_pairs={{0,8},{8,0},{16,24},{24,16},{32,40},{40,32},{48,56},{56,48},{64,72... | collective-permute-start | bytes 786440 | tf_op jit(solution)/shard_map/ppermute | solution.py:345
  123.3 22.4 %collective-permute-start.28 = (bf16[64,16,128]{2,1,0:T(8,128)(2,1)S(1)}, bf16[64,16,128]{2,1,0:T(8,128)(2,1)S(1)}, u32[]{:S(2)}, u32[]{:S(2)}) collective-permute-start(bf16[64,16,128]{2,1,0:T(8,128)(2,1)S(1)} %bitcast.52), channel_id=1, source_target_pairs={{0,32},{8,40},{16,48},{24,56},{32,0},{40,8},{48,16},{56,24},{64,96... | collective-permute-start | bytes 786440 | tf_op jit(solution)/shard_map/ppermute | solution.py:345
  123.4 22.3 %collective-permute-start.27 = (bf16[64,16,128]{2,1,0:T(8,128)(2,1)S(1)}, bf16[64,16,128]{2,1,0:T(8,128)(2,1)S(1)}, u32[]{:S(2)}, u32[]{:S(2)}) collective-permute-start(bf16[64,16,128]{2,1,0:T(8,128)(2,1)S(1)} %bitcast.50), channel_id=1, source_target_pairs={{0,96},{8,104},{16,112},{24,120},{32,64},{40,72},{48,80},{56,88},{... | collective-permute-start | bytes 786440 | tf_op jit(solution)/shard_map/ppermute | solution.py:345
  128.0 12.0 %collective-permute-start.17 = (f32[64,128]{1,0:T(8,128)S(1)}, f32[64,128]{1,0:T(8,128)S(1)}, u32[]{:S(2)}, u32[]{:S(2)}) collective-permute-start(f32[64,128]{1,0:T(8,128)S(1)} %add.36), channel_id=1, source_target_pairs={{0,48},{8,56},{16,32},{24,40},{32,16},{40,24},{48,0},{56,8},{64,11... | collective-permute-start | bytes 98312 | tf_op jit(solution)/shard_map/ppermute | solution.py:412
  131.2 19.6 %collective-permute-start.29 = (bf16[64,16,128]{2,1,0:T(8,128)(2,1)S(1)}, bf16[64,16,128]{2,1,0:T(8,128)(2,1)S(1)}, u32[]{:S(2)}, u32[]{:S(2)}) collective-permute-start(bf16[64,16,128]{2,1,0:T(8,128)(2,1)S(1)} %bitcast.49), channel_id=1, source_target_pairs={{0,80},{8,88},{16,96},{24,104},{32,112},{40,120},{48,64},{56,72},{... | collective-permute-start | bytes 786440 | tf_op jit(solution)/shard_map/ppermute | solution.py:345
  131.2 19.7 %collective-permute-start.30 = (bf16[64,16,128]{2,1,0:T(8,128)(2,1)S(1)}, bf16[64,16,128]{2,1,0:T(8,128)(2,1)S(1)}, u32[]{:S(2)}, u32[]{:S(2)}) collective-permute-start(bf16[64,16,128]{2,1,0:T(8,128)(2,1)S(1)} %bitcast.45), channel_id=1, source_target_pairs={{0,112},{8,120},{16,64},{24,72},{32,80},{40,88},{48,96},{56,104},{... | collective-permute-start | bytes 786440 | tf_op jit(solution)/shard_map/ppermute | solution.py:345
  140.0 11.3 %collective-permute-start.31 = (bf16[64,16,128]{2,1,0:T(8,128)(2,1)}, bf16[64,16,128]{2,1,0:T(8,128)(2,1)S(1)}, u32[]{:S(2)}, u32[]{:S(2)}) collective-permute-start(bf16[64,16,128]{2,1,0:T(8,128)(2,1)} %bitcast.22), channel_id=1, source_target_pairs={{0,16},{8,24},{16,32},{24,40},{32,48},{40,56},{48,0},{56,8},{64,80... | collective-permute-start | bytes 786440 | tf_op jit(solution)/shard_map/ppermute | solution.py:345
  145.7 8.3 %collective-permute-start.32 = (bf16[64,16,128]{2,1,0:T(8,128)(2,1)S(1)}, bf16[64,16,128]{2,1,0:T(8,128)(2,1)S(1)}, u32[]{:S(2)}, u32[]{:S(2)}) collective-permute-start(bf16[64,16,128]{2,1,0:T(8,128)(2,1)S(1)} %bitcast.54), channel_id=1, source_target_pairs={{0,48},{8,56},{16,0},{24,8},{32,16},{40,24},{48,32},{56,40},{64,11... | collective-permute-start | bytes 786440 | tf_op jit(solution)/shard_map/ppermute | solution.py:345
  145.7 9.4 %collective-permute-start.33 = (bf16[64,16,128]{2,1,0:T(8,128)(2,1)S(1)}, bf16[64,16,128]{2,1,0:T(8,128)(2,1)S(1)}, u32[]{:S(2)}, u32[]{:S(2)}) collective-permute-start(bf16[64,16,128]{2,1,0:T(8,128)(2,1)S(1)} %bitcast.53), channel_id=1, source_target_pairs={{0,64},{8,72},{16,80},{24,88},{32,96},{40,104},{48,112},{56,120},{... | collective-permute-start | bytes 786440 | tf_op jit(solution)/shard_map/ppermute | solution.py:345
  (15 other events, 69.3 us)

commit v3 on v2

--- a/solution.py
+++ b/solution.py
@@ -18,11 +18,11 @@
     return pl.BlockSpec(memory_space=space)
 
 
-ANY, VMEM, SMEM = pl.ANY, pltpu.VMEM, pltpu.SMEM
-
-
-def params():
-    return pltpu.CompilerParams(vmem_limit_bytes=16 << 20)
+ANY, VMEM, SMEM, HBM = pl.ANY, pltpu.VMEM, pltpu.SMEM, pltpu.HBM
+
+
+def params(megabytes=16):
+    return pltpu.CompilerParams(vmem_limit_bytes=megabytes << 20)
 
 
 def scale_kernel(feats, norm, scaled):
@@ -49,6 +49,10 @@
         payload[g, per_peer + 1] = packed
 
 
+def after(value, *held):
+    return lax.optimization_barrier((value, *held))[0] if held else value
+
+
 def slab_id(meta, hop):
     me = meta[META_ME, 0]
     dx, dy, dc = hop
@@ -73,12 +77,17 @@
             tiles.at[slab, pl.ds(first, UNROLL)], buffer.at[k, pl.ds(first, UNROLL)], sems.at[k, chunk]
         ).wait()
         products, targets = [], []
-        for j in range(UNROLL):
+        for j in range(0, UNROLL, 2):
             c = first + j
-            entry = meta[slab, c]
-            r = lax.dot_general(source_of(entry), buffer[k, c], (dims, ((), ())), preferred_element_type=F32)
-            products.append(jnp.where(c < count, r, 0.0))
-            targets.append(target_of(entry))
+            pair = [meta[slab, c], meta[slab, c + 1]]
+            left = jnp.concatenate([source_of(e) for e in pair], axis=0)
+            right = jnp.concatenate([buffer[k, c], buffer[k, c + 1]], axis=0 if dims[1] == (1,) else 1)
+            r = lax.dot_general(left, right, (dims, ((), ())), preferred_element_type=F32)
+            rows = r.shape[0] // 2
+            for i in range(2):
+                part = r[i * rows:(i + 1) * rows, i * LANES:(i + 1) * LANES]
+                products.append(jnp.where(c + i < count, part, 0.0))
+                targets.append(target_of(pair[i]))
         for t, r in zip(targets, products):
             accumulator[t] = accumulator[t] + r
         return carry
@@ -94,10 +103,11 @@
     )
 
 
-def forward_kernel(hops, first, last, meta, *refs):
+def forward_kernel(hops, where, first, last, meta, *refs):
     refs = list(refs)
     pieces = len(hops)
-    xs = [refs.pop(0) for _ in range(pieces)]
+    arrays = [refs.pop(0) for _ in range(1 + max(a for a, _ in where))]
+    xs = [arrays[a] if i is None else arrays[a].at[i] for a, i in where]
     tiles = refs.pop(0)
     start = None if first else refs.pop(0)
     norm = refs.pop(0) if last else None
@@ -134,12 +144,19 @@
         save.wait()
 
 
-def forward_call(hops, xs, meta, tiles, start, norm, peers):
-    pieces = len(xs)
+def forward_call(entries, meta, tiles, start, norm, peers):
+    pieces = len(entries)
     first, last = start is None, norm is not None
-    shape = xs[0].shape
-    args = [meta, *xs, tiles]
-    specs = [spec(SMEM)] + [spec(ANY)] * (pieces + 1)
+    arrays, where = [], []
+    for array, index, _ in entries:
+        at = [i for i, other in enumerate(arrays) if other is array]
+        if not at:
+            arrays.append(array)
+        where.append((at[0] if at else len(arrays) - 1, index))
+    hops = [hop for _, _, hop in entries]
+    shape = arrays[0].shape if entries[0][1] is None else arrays[0].shape[1:]
+    args = [meta, *arrays, tiles]
+    specs = [spec(SMEM)] + [spec(ANY)] * len(arrays) + [spec(HBM)]
     if not first:
         args.append(start)
         specs.append(spec(ANY))
@@ -150,7 +167,7 @@
     else:
         out = jax.ShapeDtypeStruct(shape, F32)
     return pl.pallas_call(
-        functools.partial(forward_kernel, hops, first, last),
+        functools.partial(forward_kernel, hops, where, first, last),
         out_shape=out, in_specs=specs, out_specs=spec(VMEM) if last else spec(ANY),
         scratch_shapes=[
             VMEM((pieces, *tiles.shape[1:]), BF16),
@@ -159,17 +176,21 @@
             pltpu.SemaphoreType.DMA((pieces + 2,)),
             VMEM(shape, F32),
         ],
-        compiler_params=params(), cost_estimate=cost(pieces, tiles), name="forward_tiles",
+        compiler_params=params(48), cost_estimate=cost(pieces, tiles), name="forward_tiles",
     )(*args)
 
 
-def backward_kernel(hops, added, meta, *refs):
+def backward_kernel(hops, mode, meta, *refs):
     refs = list(refs)
     pieces = len(hops)
+    added = mode != "swap"
     ys = refs.pop(0)
     tiles = refs.pop(0)
-    adds = [refs.pop(0) for _ in range(pieces)] if added else None
-    outs = [refs.pop(0) for _ in range(pieces)]
+    adds = refs.pop(0) if added else None
+    extra = refs.pop(0) if mode == "send" else None
+    outs = [refs.pop(0) for _ in range(1 if mode == "swap" else pieces)]
+    if mode == "swap":
+        outs = [outs[0].at[k] for k in range(pieces)]
     buffer, sems, y_buffer, y_sem, acc, save_sems = refs[:6]
     if added:
         add_buffer, add_sems = refs[6:]
@@ -180,18 +201,22 @@
         slab = slab_id(meta, hops[k])
         start_tiles(k, slab, meta[META_COUNTS, slab], tiles, buffer, sems)
         if added:
-            seed = pltpu.make_async_copy(adds[k], add_buffer.at[k], add_sems.at[k])
+            seed = pltpu.make_async_copy(adds.at[k], add_buffer.at[k], add_sems.at[k])
             seed.start()
             seeds.append(seed)
-    per_peer = ys.shape[1]
-    blocks = acc.shape[1]
+    blocks, rows = acc.shape[1], acc.shape[2]
+    per_peer = blocks // ys.shape[0]
+    per_tile = LANES // rows
     saves = []
     for k in range(pieces):
         slab = slab_id(meta, hops[k])
         if added:
             seeds[k].wait()
         for b in range(blocks):
-            acc[k, b] = add_buffer[k, b].astype(F32) if added else jnp.zeros(acc.shape[2:], F32)
+            if added:
+                acc[k, b] = add_buffer[k, b // per_tile, pl.ds((b % per_tile) * rows, rows), :].astype(F32)
+            else:
+                acc[k, b] = jnp.zeros(acc.shape[2:], F32)
         if k == 0:
             load.wait()
 
@@ -206,11 +231,11 @@
         if outs[k].dtype == F32:
             save = pltpu.make_async_copy(acc.at[k], outs[k], save_sems.at[k])
         else:
-            held = buffer.at[k, pl.ds(0, acc.shape[1] * acc.shape[2] // LANES)]
-            rows = acc.shape[2]
-            per_tile = LANES // rows
+            held = buffer.at[k, pl.ds(0, outs[k].shape[0])]
             for b in range(blocks):
                 held[b // per_tile, pl.ds((b % per_tile) * rows, rows), :] = acc[k, b].astype(BF16)
+            if extra is not None:
+                split(extra[...], held.at[blocks // per_tile])
             save = pltpu.make_async_copy(held, outs[k], save_sems.at[k])
         save.start()
         saves.append(save)
@@ -218,18 +243,34 @@
         save.wait()
 
 
-def backward_call(hops, ys, meta, tiles, adds, kept):
+def split(value, tile):
+    high = value.astype(BF16)
+    tile[0:value.shape[0], :] = high
+    tile[value.shape[0]:2 * value.shape[0], :] = (value - high.astype(F32)).astype(BF16)
+
+
+def joined(tile):
+    half = tile.shape[0] // 2
+    return tile[0:half, :].astype(F32) + tile[half:2 * half, :].astype(F32)
+
+
+def backward_call(hops, mode, ys, blocks, meta, tiles, adds=None, extra=None):
     pieces = len(hops)
     rows = ys.shape[2]
-    blocks = ys.shape[0] * ys.shape[1]
-    added = adds is not None
-    args = [meta, ys, tiles] + (list(adds) if added else [])
-    specs = [spec(SMEM), spec(ANY), spec(ANY)] + [spec(ANY)] * (pieces if added else 0)
     packed = (blocks * rows // LANES, LANES, LANES)
-    outs = [
-        jax.ShapeDtypeStruct((blocks, rows, LANES), F32) if k == kept else jax.ShapeDtypeStruct(packed, BF16)
-        for k in range(pieces)
-    ]
+    more = (packed[0] + 1, LANES, LANES)
+    args, specs = [meta, ys, tiles], [spec(SMEM), spec(ANY), spec(HBM)]
+    if mode != "swap":
+        args.append(adds)
+        specs.append(spec(ANY))
+    if mode == "swap":
+        outs = jax.ShapeDtypeStruct((pieces, *packed), BF16)
+    elif mode == "send":
+        args.append(extra)
+        specs.append(spec(VMEM))
+        outs = [jax.ShapeDtypeStruct(more, BF16)] * pieces
+    else:
+        outs = [jax.ShapeDtypeStruct((blocks, rows, LANES), F32)] + [jax.ShapeDtypeStruct(packed, BF16)] * (pieces - 1)
     scratch = [
         VMEM((pieces, *tiles.shape[1:]), BF16),
         pltpu.SemaphoreType.DMA((pieces, tiles.shape[1] // UNROLL)),
@@ -238,14 +279,14 @@
         VMEM((pieces, blocks, rows, LANES), F32),
         pltpu.SemaphoreType.DMA((pieces,)),
     ]
-    if added:
-        scratch += [VMEM((pieces, blocks, rows, LANES), BF16), pltpu.SemaphoreType.DMA((pieces,))]
-    parts = pl.pallas_call(
-        functools.partial(backward_kernel, hops, added),
-        out_shape=outs, in_specs=specs, out_specs=[spec(ANY)] * pieces, scratch_shapes=scratch,
-        compiler_params=params(), cost_estimate=cost(pieces, tiles), name="backward_tiles",
+    if mode != "swap":
+        scratch += [VMEM((pieces, *packed), BF16), pltpu.SemaphoreType.DMA((pieces,))]
+    return pl.pallas_call(
+        functools.partial(backward_kernel, hops, mode),
+        out_shape=outs, in_specs=specs,
+        out_specs=spec(ANY) if mode == "swap" else [spec(ANY)] * pieces, scratch_shapes=scratch,
+        compiler_params=params(48), cost_estimate=cost(pieces, tiles), name="backward_tiles",
     )(*args)
-    return [p.reshape(blocks, rows, LANES) for p in parts]
 
 
 def dense_kernel(place, agg, received, norm, back, sent):
@@ -281,38 +322,68 @@
             sent[g, b] = hid[g * hid_local:(g + 1) * hid_local]
             back[g, b] = back_b[g * feat_local:(g + 1) * feat_local]
     for g in range(peers):
-        for source, slot in ((grad[g * feat_local:(g + 1) * feat_local], blocks), (grad[peers * feat_local:], blocks + 2)):
+        for source, slot in ((grad[g * feat_local:(g + 1) * feat_local], blocks), (grad[peers * feat_local:], blocks + 4)):
             high = source.astype(BF16).astype(F32)
             for i, part in enumerate((high, source - high)):
                 part = jnp.concatenate([part[:, h * LANES:(h + 1) * LANES] for h in range(halves)], axis=0)
-                short = hid_local - part.shape[0]
-                if slot == blocks + 2:
-                    sent[g, slot, pl.ds(i * part.shape[0], part.shape[0]), :] = part.astype(BF16)
+                part = part.astype(BF16)
+                if slot == blocks + 4:
+                    back[g, slot + i] = part
                 else:
-                    sent[g, slot + i] = part.astype(BF16)
-
-
-def collect_kernel(received, hidden, grads):
-    peers, per_peer = received.shape[0], received.shape[1] - 3
+                    for h in range(halves):
+                        back[g, slot + i * halves + h] = part[h * feat_local:(h + 1) * feat_local]
+
+
+def collect_kernel(received, hidden):
+    peers, per_peer = received.shape[0], received.shape[1]
     for b in range(peers * per_peer):
         hidden[:, pl.ds(b * LANES, LANES)] = received[b // per_peer, b % per_peer]
-    rows = received.shape[2]
-    total = jnp.zeros((rows, LANES), F32)
-    tail = jnp.zeros((rows, LANES), F32)
-    for g in range(peers):
-        total = total + (received[g, per_peer].astype(F32) + received[g, per_peer + 1].astype(F32))
-        tail = tail + received[g, per_peer + 2].astype(F32)
-    grads[0:rows] = total
-    grads[rows:2 * rows] = tail
-
-
-def finish_kernel(kept, norm, *refs):
-    out = refs[-1]
+
+
+def weight_sums_kernel(back, sums):
+    rows = back.shape[2]
+    first = back.shape[1] - 6
+    for i in range(2):
+        total = jnp.zeros((rows, LANES), F32)
+        for g in range(back.shape[0]):
+            total = total + (back[g, first + i].astype(F32) + back[g, first + 2 + i].astype(F32))
+        sums[i * rows:(i + 1) * rows] = total
+        tail = jnp.zeros((rows, LANES), F32)
+        for g in range(back.shape[0]):
+            tail = tail + back[g, first + 4 + i].astype(F32)
+        sums[(2 + i) * rows:(3 + i) * rows] = tail
+
+
+def cross_kernel(own, down, up, far, out):
+    last = out.shape[0] - 1
+    for t in range(last):
+        total = (own[t].astype(F32) + far[t].astype(F32)) + (down[t].astype(F32) + up[t].astype(F32))
+        out[t] = total.astype(BF16)
+    split((joined(own.at[last]) + joined(far.at[last])) + (joined(down.at[last]) + joined(up.at[last])), out.at[last])
+
+
+def finish_with_scale(scale, place, kept, norm, down, up, far, sent, came, out, grad_weight, grad_bias):
+    rows = kept.shape[1]
+    per_tile = LANES // rows
     for b in range(kept.shape[0]):
         total = kept[b]
-        for r in refs[:-1]:
-            total = total + r[b].astype(F32)
+        for r in (down, up, far, came):
+            total = total + r[b // per_tile, pl.ds((b % per_tile) * rows, rows), :].astype(F32)
         out[:, pl.ds(b * LANES, LANES)] = norm[pl.ds(b, 1), :] * total
+    last = sent.shape[0] - 1
+    sums = (joined(sent.at[last]) + joined(came.at[last])) * scale
+    hid_local = grad_bias.shape[1]
+    halves = grad_weight.shape[1] // LANES
+    for h in range(halves):
+        grad_weight[:, h * LANES:(h + 1) * LANES] = sums[h * rows:(h + 1) * rows]
+    low = 2 * rows + 8 * halves
+    bias = jnp.zeros((1, hid_local), F32)
+    for h in range(halves):
+        row = sums[2 * rows + 8 * h:2 * rows + 8 * h + 1] + sums[low + 8 * h:low + 8 * h + 1]
+        for i in range(LANES // hid_local):
+            here = place[0] == h * (LANES // hid_local) + i
+            bias = jnp.where(here, row[:, i * hid_local:(i + 1) * hid_local], bias)
+    grad_bias[...] = bias
 
 
 def on_device(feats, tiles, dst_block, src_block, tile_counts, norm, weight, bias, cotangent):
@@ -354,75 +425,76 @@
         out_shape=jax.ShapeDtypeStruct((peers, per_peer + 2, hid_local, LANES), BF16),
         compiler_params=params(), name="payload",
     )(cotangent.T, weight, bias.reshape(1, hid_local))
-    hops = [(0, 0), (0, 1), (0, 3), (1, 0), (1, 1), (1, 3), (0, 2), (1, 2)]
-    pieces = {hop: scaled if hop == (0, 0) else move(scaled, *hop, 0) for hop in hops}
+    across = move(scaled, 1, 0, 0)
+    down, up = move(scaled, 0, 1, 0), move(scaled, 0, 3, 0)
+    entries = [(scaled, None, (0, 0, 0)), (move(scaled, 0, 0, 1), None, (0, 0, 1))]
+    across, down, up = lax.optimization_barrier((across, down, up))
+    down_across, up_across = move(across, 0, 1, 0), move(across, 0, 3, 0)
     received = lax.all_to_all(payload, "feat", 0, 0)
-    total = None
-    groups = [hops[:1], hops[1:4], hops[4:6], hops[6:]]
-    for g, group in enumerate(groups):
-        xs, froms = [], []
-        for dx, dy in group:
-            for dc in (0, 1):
-                xs.append(move(pieces[dx, dy], 0, 0, 1) if dc else pieces[dx, dy])
-                froms.append(((-dx) % 2, (-dy) % 4, dc))
-        total = forward_call(froms, xs, meta, own_tiles, total, norm_blocks if g == len(groups) - 1 else None, peers)
+    far, far_across, received = lax.optimization_barrier((scaled, across, received))
+    far, far_across = move(far, 0, 2, 0), move(far_across, 0, 2, 0)
+
+    def group(values, hops):
+        moved = move(jnp.stack(values), 0, 0, 1)
+        near = [(v, None, (*hop, 0)) for v, hop in zip(values, hops)]
+        return near, [(moved, i, (*hop, 1)) for i, hop in enumerate(hops)]
+
+    near, other = group([across, down, up], [(1, 0), (0, 3), (0, 1)])
+    total = forward_call(entries + near + other, meta, own_tiles, None, None, peers)
+    *values, total = lax.optimization_barrier((down_across, up_across, far, far_across, total))
+    near, other = group(values, [(1, 3), (1, 1), (0, 2), (1, 2)])
+    total = forward_call(near, meta, own_tiles, total, None, peers)
+    total = forward_call(other, meta, own_tiles, total, norm_blocks, peers)
     agg = lax.all_to_all(total, "feat", 0, 0)
     back, sent = pl.pallas_call(
         dense_kernel,
         out_shape=(
-            jax.ShapeDtypeStruct((peers, per_peer, feat_local, LANES), BF16),
-            jax.ShapeDtypeStruct((peers, per_peer + 3, hid_local, LANES), BF16),
+            jax.ShapeDtypeStruct((peers, per_peer + 6, feat_local, LANES), BF16),
+            jax.ShapeDtypeStruct((peers, per_peer, hid_local, LANES), BF16),
         ),
         in_specs=[spec(SMEM), spec(VMEM), spec(VMEM), spec(VMEM)],
         compiler_params=params(), name="dense",
     )(place, agg, received, norm_blocks)
     back = lax.all_to_all(back, "feat", 0, 0)
-    collected = lax.all_to_all(sent, "feat", 0, 0)
-
-    order = [(1, 2), (0, 2), (1, 1), (1, 3), (0, 1), (0, 3), (1, 0), (0, 0)]
-    halves = [order[:4], order[4:]]
-    swapped = []
-    for half in halves:
-        parts = backward_call([(dx, dy, 1) for dx, dy in half], back, meta, own_tiles, None, None)
-        swapped.append([move(p, 0, 0, 1) for p in parts])
-    arrived, kept = [], None
-    for half, adds in zip(halves, swapped):
-        stay = half.index((0, 0)) if (0, 0) in half else None
-        parts = backward_call([(dx, dy, 0) for dx, dy in half], back, meta, own_tiles, adds, stay)
-        for (dx, dy), p in zip(half, parts):
-            if (dx, dy) == (0, 0):
-                kept = p
-            else:
-                arrived.append(move(p, dx, dy, 0))
-
-    hidden, summed = pl.pallas_call(
+
+    summed = pl.pallas_call(
+        weight_sums_kernel,
+        out_shape=jax.ShapeDtypeStruct((4 * feat_local, LANES), F32),
+        compiler_params=params(), name="weight_sums",
+    )(back)
+    ways = [(0, 0), (0, 1), (0, 3), (0, 2)]
+    over = [(1, dy) for _, dy in ways]
+    mine = backward_call([(*hop, 1) for hop in over], "swap", back, blocks, meta, own_tiles)
+    mine_too = backward_call([(*hop, 1) for hop in ways], "swap", after(back, mine), blocks, meta, own_tiles)
+    swapped, mine_too, theirs = lax.optimization_barrier((move(mine, 0, 0, 1), mine_too, move(summed, 0, 0, 1)))
+    sums = backward_call([(*hop, 0) for hop in over], "send", back, blocks, meta, own_tiles, swapped, summed + theirs)
+    crossing = [move(p, *hop, 0) for p, hop in zip(sums[1:], ways[1:])]
+    swapped = after(move(mine_too, 0, 0, 1), sums[1])
+    parts = backward_call([(*hop, 0) for hop in ways], "keep", back, blocks, meta, own_tiles, swapped)
+    arrived = [move(p, *hop, 0) for p, hop in zip(parts[1:], ways[1:])]
+    *crossing, _ = lax.optimization_barrier((*crossing, parts[1]))
+    crossed = pl.pallas_call(
+        cross_kernel,
+        out_shape=jax.ShapeDtypeStruct(sums[0].shape, BF16),
+        compiler_params=params(), name="cross",
+    )(sums[0], *crossing)
+    hidden = pl.pallas_call(
         collect_kernel,
+        out_shape=jax.ShapeDtypeStruct((hid_local, rows), BF16),
+        compiler_params=params(), name="collect",
+    )(lax.all_to_all(after(sent, parts[1]), "feat", 0, 0))
+    came = move(crossed, 1, 0, 0)
+    grad_feats, grad_weight, grad_bias = pl.pallas_call(
+        functools.partial(finish_with_scale, float((rows * slabs) ** -0.5)),
         out_shape=(
-            jax.ShapeDtypeStruct((hid_local, rows), BF16),
-            jax.ShapeDtypeStruct((2 * hid_local, LANES), F32),
+            jax.ShapeDtypeStruct((feat_local, rows), F32),
+            jax.ShapeDtypeStruct(weight.shape, F32),
+            jax.ShapeDtypeStruct((1, hid_local), F32),
         ),
-        compiler_params=params(), name="collect",
-    )(collected)
-    for i in range(4):
-        pairs = []
-        for n in range(slabs):
-            x, y, c = n // 8, (n // 2) % 4, n % 2
-            c, y, x = (c ^ 1, y, x) if i == 0 else (c, y ^ 1, x) if i == 1 else (c, 3 - y, x) if i == 2 else (c, y, x ^ 1)
-            pairs.append((n, x * 8 + y * 2 + c))
-        summed = summed + lax.ppermute(summed, "nodes", pairs)
-    summed = summed * (rows * slabs) ** (-0.5)
-    halves_of = hid_local // feat_local
-    grad_weight = jnp.concatenate([summed[h * feat_local:(h + 1) * feat_local] for h in range(halves_of)], axis=1)
-    low = hid_local + 8 * halves_of
-    bias_row = jnp.concatenate([summed[hid_local + 8 * h] + summed[low + 8 * h] for h in range(halves_of)])
-    grad_bias = lax.dynamic_slice(bias_row, (place[0] * hid_local,), (hid_local,))
-
-    grad_feats = pl.pallas_call(
-        finish_kernel,
-        out_shape=jax.ShapeDtypeStruct((feat_local, rows), F32),
+        in_specs=[spec(SMEM)] + [spec(VMEM)] * 7,
         compiler_params=params(), name="finish",
-    )(kept, norm_blocks, *arrived).T
-    return hidden.T, grad_weight, grad_bias, grad_feats
+    )(place, parts[0], norm_blocks, *arrived, crossed, came)
+    return hidden.T, grad_weight, grad_bias.reshape(hid_local), grad_feats.T
 
 
 def solution(mesh):

time: 158 us -> 129 us (0.82)
  starting transfers between devices: 60.1 us -> 36.2 us
  local copies, waits for them, and re-layouts: 26 us -> 7.31 us
  Pallas kernels: 36.9 us -> 43.3 us
  waiting for transfers between devices: 21.6 us -> 26.6 us
    unnamed x20 -> x24, local copies, waits for them, and re-layouts: 25.3 us -> 7.24 us
    ppermute x30 -> x20, starting transfers between devices: 41.5 us -> 23.9 us  [move(): return lax.ppermute(value, 'nodes', pairs)]
    pallas_call x10 -> x11, Pallas kernels: 33.4 us -> 40 us  [the longest x4 19.8 us: backward_call(): pl.pallas_call(functools.partial(backward_kernel, hops, mode), out_shape=...]
    all_to_all x1, waiting for transfers between devices: 0.01 us -> 5.37 us  [on_device(): received = lax.all_to_all(payload, 'feat', 0, 0)]
    ppermute x4 -> x0, starting transfers between devices: 3.75 us -> none  [on_device(): summed = summed + lax.ppermute(summed, 'nodes', pairs)]
    all_to_all x1, starting transfers between devices: 5.96 us -> 3.42 us  [on_device(): agg = lax.all_to_all(total, 'feat', 0, 0)]
    ppermute x30 -> x20, waiting for transfers between devices: 13.4 us -> 14.1 us  [move(): return lax.ppermute(value, 'nodes', pairs)]
  transfers between devices with their start and end apart: 37 -> 23, of which waited for: 10 -> 6; matrix products, arithmetic and copies ran while one was open for 1% -> 2% of each run, Pallas kernels for 22% -> 24%
where the time goes in v3:
time: 129 us; the launch traced here: 128 us
  Pallas kernels  43.3 us (34%)
  starting transfers between devices  36.2 us (28%)
  waiting for transfers between devices  26.6 us (21%)
  blocking collectives  10.9 us (8%)
  local copies, waits for them, and re-layouts  7.31 us (6%)
  other arithmetic  3.24 us (3%)
    ppermute x20, starting transfers between devices, move(): return lax.ppermute(value, 'nodes', pairs)  23.9 us
    pallas_call x4, Pallas kernels, backward_call(): pl.pallas_call(functools.partial(backward_kernel, hops, mode), out_shape=...  19.8 us
    pallas_call x3, Pallas kernels, forward_call(): pl.pallas_call(functools.partial(forward_kernel, hops, where, first, last...  17.7 us
    ppermute x20, waiting for transfers between devices, move(): return lax.ppermute(value, 'nodes', pairs)  14.1 us
    all_to_all x1, blocking collectives, on_device(): back = lax.all_to_all(back, 'feat', 0, 0)  10.9 us
    unnamed x24, local copies, waits for them, and re-layouts  7.24 us
    all_to_all x1, waiting for transfers between devices, on_device(): agg = lax.all_to_all(total, 'feat', 0, 0)  7.16 us
    all_to_all x1, waiting for transfers between devices, on_device(): received = lax.all_to_all(payload, 'feat', 0, 0)  5.37 us
  transfers between devices with their start and end apart: 23, of which 6 were waited for; matrix products, arithmetic and copies ran while one was open for 2% of the time, Pallas kernels for 24%

profile of v3, /device:TPU:0, one launch (start us, length us, event | category | flops | bytes accessed | tf_op | source)
XLA Modules:
  0.0 128.3 jit_solution(11920864056972984477)
XLA Ops:
  2.4 3.2 %collective-permute-start = (bf16[64,16,128]{2,1,0:T(8,128)(2,1)S(1)}, bf16[64,16,128]{2,1,0:T(8,128)(2,1)S(1)}, u32[]{:S(2)}, u32[]{:S(2)}) collective-permute-start(bf16[64,16,128]{2,1,0:T(8,128)(2,1)S(1)} %scale.1.refs_0_), channel_id=1, source_target_pairs={{0,64},{8,72},{16,80},{24,88},{32,96},{40,104},{48,112},{56,120},{... | collective-permute-start | bytes 786440 | tf_op jit(solution)/shard_map/ppermute | solution.py:416
  5.6 1.6 %collective-permute-start.1 = (bf16[64,16,128]{2,1,0:T(8,128)(2,1)S(1)}, bf16[64,16,128]{2,1,0:T(8,128)(2,1)S(1)}, u32[]{:S(2)}, u32[]{:S(2)}) collective-permute-start(bf16[64,16,128]{2,1,0:T(8,128)(2,1)S(1)} %scale.1.refs_0_), channel_id=1, source_target_pairs={{0,16},{8,24},{16,32},{24,40},{32,48},{40,56},{48,0},{56,8},{64,80... | collective-permute-start | bytes 786440 | tf_op jit(solution)/shard_map/ppermute | solution.py:416
  7.2 1.7 %collective-permute-start.2 = (bf16[64,16,128]{2,1,0:T(8,128)(2,1)S(1)}, bf16[64,16,128]{2,1,0:T(8,128)(2,1)S(1)}, u32[]{:S(2)}, u32[]{:S(2)}) collective-permute-start(bf16[64,16,128]{2,1,0:T(8,128)(2,1)S(1)} %scale.1.refs_0_), channel_id=1, source_target_pairs={{0,48},{8,56},{16,0},{24,8},{32,16},{40,24},{48,32},{56,40},{64,11... | collective-permute-start | bytes 786440 | tf_op jit(solution)/shard_map/ppermute | solution.py:416
  8.8 1.0 copy-done.3
  12.2 5.3 %all-to-all-start = ((bf16[8,10,32,128]{3,2,1,0:T(8,128)(2,1)}), bf16[8,10,32,128]{3,2,1,0:T(8,128)(2,1)S(1)}, u32[]{:S(2)}, u32[]{:S(2)}) async-start(bf16[8,10,32,128]{3,2,1,0:T(8,128)(2,1)} %payload.1), calls=%async_computation | async-start | bytes 1310720 | tf_op jit(solution)/shard_map/all_to_all | solution.py:433
  17.5 1.0 pad_maximum_fusion.1
  19.4 2.9 %collective-permute-start.4 = (bf16[64,16,128]{2,1,0:T(8,128)(2,1)S(1)}, bf16[64,16,128]{2,1,0:T(8,128)(2,1)S(1)}, u32[]{:S(2)}, u32[]{:S(2)}) collective-permute-start(bf16[64,16,128]{2,1,0:T(8,128)(2,1)S(1)} %collective-permute-done.refs_2_), channel_id=1, source_target_pairs={{0,48},{8,56},{16,0},{24,8},{32,16},{40,24},{48,32},{56,40},{64,11... | collective-permute-start | bytes 786440 | tf_op jit(solution)/shard_map/ppermute | solution.py:416
  22.3 5.4 %all-to-all-done.received = bf16[8,10,32,128]{3,2,1,0:T(8,128)(2,1)S(1)} async-done(((bf16[8,10,32,128]{3,2,1,0:T(8,128)(2,1)}), bf16[8,10,32,128]{3,2,1,0:T(8,128)(2,1)S(1)}, u32[]{:S(2)}, u32[]{:S(2)}) %all-to-all-start) | async-done | bytes 655392 | tf_op jit(solution)/shard_map/all_to_all | solution.py:433
  27.6 1.9 %collective-permute-start.5 = (bf16[64,16,128]{2,1,0:T(8,128)(2,1)S(1)}, bf16[64,16,128]{2,1,0:T(8,128)(2,1)S(1)}, u32[]{:S(2)}, u32[]{:S(2)}) collective-permute-start(bf16[64,16,128]{2,1,0:T(8,128)(2,1)S(1)} %scale.1.refs_0_), channel_id=1, source_target_pairs={{0,32},{8,40},{16,48},{24,56},{32,0},{40,8},{48,16},{56,24},{64,96... | collective-permute-start | bytes 786440 | tf_op jit(solution)/shard_map/ppermute | solution.py:416
  30.3 1.6 %collective-permute-start.6 = (bf16[64,16,128]{2,1,0:T(8,128)(2,1)S(1)}, bf16[64,16,128]{2,1,0:T(8,128)(2,1)S(1)}, u32[]{:S(2)}, u32[]{:S(2)}) collective-permute-start(bf16[64,16,128]{2,1,0:T(8,128)(2,1)S(1)} %collective-permute-done.refs_2_), channel_id=1, source_target_pairs={{0,32},{8,40},{16,48},{24,56},{32,0},{40,8},{48,16},{56,24},{64,96... | collective-permute-start | bytes 786440 | tf_op jit(solution)/shard_map/ppermute | solution.py:416
  31.9 1.3 %add_bitcast_fusion = s32[16,32]{1,0:T(8,128)} fusion(s32[1,16,32]{2,1,0:T(8,128)} %param.12, s32[1,16,32]{2,1,0:T(8,128)} %param.11), kind=kLoop, calls=%fused_computation.3 | loop fusion | flops 1024 | bytes 6144 | tf_op jit(solution)/shard_map/add | solution.py:404
  35.0 8.0 %forward_tiles.3.refs_5_ = f32[64,16,128]{2,1,0:T(8,128)S(1)} custom-call(s32[18,32]{1,0:T(8,128)S(1)} %add_add_fusion.meta, bf16[64,16,128]{2,1,0:T(8,128)(2,1)S(1)} %scale.1.refs_0_, bf16[64,16,128]{2,1,0:T(8,128)(2,1)S(1)} %copy-done.5, bf16[64,16,128]{2,1,0:T(8,128)(2,1)S(1)} %collective-permute-done.refs_2_, ...), custom_call_target="tpu_custom_call" | custom-call | flops 67108864 | bytes 8388608 | tf_op jit(solution)/shard_map/forward_tiles/pallas_call | solution.py:169
  43.3 4.9 %forward_tiles.4.refs_2_ = f32[64,16,128]{2,1,0:T(8,128)S(1)} custom-call(s32[18,32]{1,0:T(8,128)S(1)} %add_add_fusion.meta, bf16[64,16,128]{2,1,0:T(8,128)(2,1)S(1)} %collective-permute-done.3.refs_0_, bf16[64,16,128]{2,1,0:T(8,128)(2,1)S(1)} %collective-permute-done.4.refs_1_, bf16[64,16,128]{2,1,0:T(8,128)(2,1)S(1)} %collective-permute-done.5.refs_2_, ...), custom_call_target="tpu_custom_call" | custom-call | flops 33554432 | bytes 4194304 | tf_op jit(solution)/shard_map/forward_tiles/pallas_call | solution.py:169
  48.3 4.8 %forward_tiles.5 = bf16[8,8,16,128]{3,2,1,0:T(8,128)(2,1)} custom-call(s32[18,32]{1,0:T(8,128)S(1)} %add_add_fusion.meta, bf16[4,64,16,128]{3,2,1,0:T(8,128)(2,1)S(1)} %collective-permute-done.9.refs_0_, bf16[16,32,128,128]{3,2,1,0:T(8,128)(2,1)} %bitcast.35, f32[64,16,128]{2,1,0:T(8,128)S(1)} %forward_tiles.4.refs_2_, f32[64,128]{1,0:T(8,128)S(1)} %bitcast.27), custom_call_target="tpu_custom_call" | custom-call | flops 33554432 | bytes 4194304 | tf_op jit(solution)/shard_map/forward_tiles/pallas_call | solution.py:169
  53.1 3.4 %all-to-all-start.1 = ((bf16[8,8,16,128]{3,2,1,0:T(8,128)(2,1)}), bf16[8,8,16,128]{3,2,1,0:T(8,128)(2,1)S(1)}, u32[]{:S(2)}, u32[]{:S(2)}) async-start(bf16[8,8,16,128]{3,2,1,0:T(8,128)(2,1)} %forward_tiles.5), calls=%async_computation.1 | async-start | bytes 524288 | tf_op jit(solution)/shard_map/all_to_all | solution.py:448
  56.5 7.2 %all-to-all-done.1.agg = bf16[8,8,16,128]{3,2,1,0:T(8,128)(2,1)S(1)} async-done(((bf16[8,8,16,128]{3,2,1,0:T(8,128)(2,1)}), bf16[8,8,16,128]{3,2,1,0:T(8,128)(2,1)S(1)}, u32[]{:S(2)}, u32[]{:S(2)}) %all-to-all-start.1) | async-done | bytes 262176 | tf_op jit(solution)/shard_map/all_to_all | solution.py:448
  63.7 2.2 %dense.1 = (bf16[8,14,16,128]{3,2,1,0:T(8,128)(2,1)S(1)}, bf16[8,8,32,128]{3,2,1,0:T(8,128)(2,1)}) custom-call(s32[1]{0:T(128)} %bitcast.place, bf16[8,8,16,128]{3,2,1,0:T(8,128)(2,1)S(1)} %all-to-all-done.1.agg, bf16[8,10,32,128]{3,2,1,0:T(8,128)(2,1)S(1)} %all-to-all-done.received, f32[64,128]{1,0:T(8,128)S(1)} %bitcast.28), custom_call_target="tpu_custom_call" | custom-call | tf_op jit(solution)/shard_map/dense/pallas_call | solution.py:449
  65.9 10.9 %all_to_all.20.refs_0_.back = bf16[8,14,16,128]{3,2,1,0:T(8,128)(2,1)S(1)} all-to-all(bf16[8,14,16,128]{3,2,1,0:T(8,128)(2,1)S(1)} %get-tuple-element.49), channel_id=1, replica_groups=mesh['nodes'=16,'feat'=8] {'feat'}, dimensions={0} | all-to-all | bytes 917504 | tf_op jit(solution)/shard_map/all_to_all | solution.py:458
  76.8 4.3 %backward_tiles.4 = bf16[4,8,128,128]{3,2,1,0:T(8,128)(2,1)S(1)} custom-call(s32[18,32]{1,0:T(8,128)S(1)} %add_add_fusion.meta, bf16[8,14,16,128]{3,2,1,0:T(8,128)(2,1)S(1)} %all_to_all.20.refs_0_.back, bf16[16,32,128,128]{3,2,1,0:T(8,128)(2,1)} %bitcast.36), custom_call_target="tpu_custom_call" | custom-call | flops 33554432 | bytes 4194304 | tf_op jit(solution)/shard_map/backward_tiles/pallas_call | solution.py:284
  81.8 4.9 %backward_tiles.5 = bf16[4,8,128,128]{3,2,1,0:T(8,128)(2,1)S(1)} custom-call(s32[18,32]{1,0:T(8,128)S(1)} %add_add_fusion.meta, bf16[8,14,16,128]{3,2,1,0:T(8,128)(2,1)S(1)} %all_to_all.20.refs_0_.back, bf16[16,32,128,128]{3,2,1,0:T(8,128)(2,1)} %bitcast.37), custom_call_target="tpu_custom_call" | custom-call | flops 33554432 | bytes 4194304 | tf_op jit(solution)/shard_map/backward_tiles/pallas_call | solution.py:284
  86.8 5.3 %backward_tiles.6 = (bf16[9,128,128]{2,1,0:T(8,128)(2,1)S(1)}, bf16[9,128,128]{2,1,0:T(8,128)(2,1)S(1)}, bf16[9,128,128]{2,1,0:T(8,128)(2,1)S(1)}, bf16[9,128,128]{2,1,0:T(8,128)(2,1)S(1)}) custom-call(s32[18,32]{1,0:T(8,128)S(1)} %add_add_fusion.meta, bf16[8,14,16,128]{3,2,1,0:T(8,128)(2,1)S(1)} %all_to_all.20.refs_0_.back, ...), custom_call_target="tpu_custom_call" | custom-call | flops 33554432 | bytes 4194304 | tf_op jit(solution)/shard_map/backward_tiles/pallas_call | solution.py:284
  92.4 3.2 %collective-permute-start.17 = (bf16[9,128,128]{2,1,0:T(8,128)(2,1)S(1)}, bf16[9,128,128]{2,1,0:T(8,128)(2,1)S(1)}, u32[]{:S(2)}, u32[]{:S(2)}) collective-permute-start(bf16[9,128,128]{2,1,0:T(8,128)(2,1)S(1)} %get-tuple-element.62), channel_id=1, source_target_pairs={{0,48},{8,56},{16,0},{24,8},{32,16},{40,24},{48,32},{56,40},{64,11... | collective-permute-start | bytes 884744 | tf_op jit(solution)/shard_map/ppermute | solution.py:416
  95.7 5.3 %backward_tiles.7 = (f32[64,16,128]{2,1,0:T(8,128)S(1)}, bf16[8,128,128]{2,1,0:T(8,128)(2,1)S(1)}, bf16[8,128,128]{2,1,0:T(8,128)(2,1)S(1)}, bf16[8,128,128]{2,1,0:T(8,128)(2,1)S(1)}) custom-call(s32[18,32]{1,0:T(8,128)S(1)} %add_add_fusion.meta, bf16[8,14,16,128]{3,2,1,0:T(8,128)(2,1)S(1)} %all_to_all.20.refs_0_.back, bf16[16,32,128,128]{3,2,1,0:T(8,128)(2,1)} %bitcast.39, ...), custom_call_target="tpu_custom_call" | custom-call | flops 33554432 | bytes 4194304 | tf_op jit(solution)/shard_map/backward_tiles/pallas_call | solution.py:284
  102.5 3.5 %all-to-all-start.3 = ((bf16[8,8,32,128]{3,2,1,0:T(8,128)(2,1)}), bf16[8,8,32,128]{3,2,1,0:T(8,128)(2,1)S(1)}, u32[]{:S(2)}, u32[]{:S(2)}) async-start(bf16[8,8,32,128]{3,2,1,0:T(8,128)(2,1)} %get-tuple-element.57), calls=%async_computation.3 | async-start | bytes 1048576 | tf_op jit(solution)/shard_map/all_to_all | solution.py:485
  106.0 2.5 %collective-permute-done.16.down = bf16[9,128,128]{2,1,0:T(8,128)(2,1)S(1)} collective-permute-done((bf16[9,128,128]{2,1,0:T(8,128)(2,1)S(1)}, bf16[9,128,128]{2,1,0:T(8,128)(2,1)S(1)}, u32[]{:S(2)}, u32[]{:S(2)}) %collective-permute-start.16) | collective-permute-done | bytes 294944 | tf_op jit(solution)/shard_map/ppermute | solution.py:416
  108.6 1.5 %collective-permute-start.19 = (bf16[9,128,128]{2,1,0:T(8,128)(2,1)S(1)}, bf16[9,128,128]{2,1,0:T(8,128)(2,1)S(1)}, u32[]{:S(2)}, u32[]{:S(2)}) collective-permute-start(bf16[9,128,128]{2,1,0:T(8,128)(2,1)S(1)} %cross.1.sent), channel_id=1, source_target_pairs={{0,64},{8,72},{16,80},{24,88},{32,96},{40,104},{48,112},{56,120},{... | collective-permute-start | bytes 884744 | tf_op jit(solution)/shard_map/ppermute | solution.py:416
  110.9 2.4 %collective-permute-start.14 = (bf16[8,128,128]{2,1,0:T(8,128)(2,1)}, bf16[8,128,128]{2,1,0:T(8,128)(2,1)S(1)}, u32[]{:S(2)}, u32[]{:S(2)}) collective-permute-start(bf16[8,128,128]{2,1,0:T(8,128)(2,1)} %copy-done.10), channel_id=1, source_target_pairs={{0,48},{8,56},{16,0},{24,8},{32,16},{40,24},{48,32},{56,40},{64,11... | collective-permute-start | bytes 786440 | tf_op jit(solution)/shard_map/ppermute | solution.py:416
  113.3 1.2 collective-permute-start.15
  114.5 5.4 %collective-permute-done.13.down = bf16[8,128,128]{2,1,0:T(8,128)(2,1)S(1)} collective-permute-done((bf16[8,128,128]{2,1,0:T(8,128)(2,1)}, bf16[8,128,128]{2,1,0:T(8,128)(2,1)S(1)}, u32[]{:S(2)}, u32[]{:S(2)}) %collective-permute-start.13) | collective-permute-done | bytes 262176 | tf_op jit(solution)/shard_map/ppermute | solution.py:416
  119.9 4.5 %collective-permute-done.14.up = bf16[8,128,128]{2,1,0:T(8,128)(2,1)S(1)} collective-permute-done((bf16[8,128,128]{2,1,0:T(8,128)(2,1)}, bf16[8,128,128]{2,1,0:T(8,128)(2,1)S(1)}, u32[]{:S(2)}, u32[]{:S(2)}) %collective-permute-start.14) | collective-permute-done | bytes 262176 | tf_op jit(solution)/shard_map/ppermute | solution.py:416
  124.4 1.6 %collective-permute-done.15.far = bf16[8,128,128]{2,1,0:T(8,128)(2,1)S(1)} collective-permute-done((bf16[8,128,128]{2,1,0:T(8,128)(2,1)}, bf16[8,128,128]{2,1,0:T(8,128)(2,1)S(1)}, u32[]{:S(2)}, u32[]{:S(2)}) %collective-permute-start.15) | collective-permute-done | bytes 262176 | tf_op jit(solution)/shard_map/ppermute | solution.py:416
  126.0 1.4 %finish.1 = (f32[16,8192]{1,0:T(8,128)}, f32[16,256]{1,0:T(8,128)}, f32[1,32]{1,0:T(1,128)}) custom-call(s32[1]{0:T(128)} %bitcast.place, f32[64,16,128]{2,1,0:T(8,128)S(1)} %get-tuple-element.58.kept, f32[64,128]{1,0:T(8,128)S(1)} %bitcast.29, bf16[8,128,128]{2,1,0:T(8,128)(2,1)S(1)} %collective-permute-done.13.down, ...), custom_call_target="tpu_custom_call" | custom-call | tf_op jit(solution)/shard_map/finish/pallas_call | solution.py:487
  (59 shorter events, 12.2 us)
Async XLA Ops:
  0.6 0.8 copy-start
  1.4 0.9 copy-start.6
  2.4 15.1 %collective-permute-start = (bf16[64,16,128]{2,1,0:T(8,128)(2,1)S(1)}, bf16[64,16,128]{2,1,0:T(8,128)(2,1)S(1)}, u32[]{:S(2)}, u32[]{:S(2)}) collective-permute-start(bf16[64,16,128]{2,1,0:T(8,128)(2,1)S(1)} %scale.1.refs_0_), channel_id=1, source_target_pairs={{0,64},{8,72},{16,80},{24,88},{32,96},{40,104},{48,112},{56,120},{... | collective-permute-start | bytes 786440 | tf_op jit(solution)/shard_map/ppermute | solution.py:416
  5.6 11.9 %collective-permute-start.1 = (bf16[64,16,128]{2,1,0:T(8,128)(2,1)S(1)}, bf16[64,16,128]{2,1,0:T(8,128)(2,1)S(1)}, u32[]{:S(2)}, u32[]{:S(2)}) collective-permute-start(bf16[64,16,128]{2,1,0:T(8,128)(2,1)S(1)} %scale.1.refs_0_), channel_id=1, source_target_pairs={{0,16},{8,24},{16,32},{24,40},{32,48},{40,56},{48,0},{56,8},{64,80... | collective-permute-start | bytes 786440 | tf_op jit(solution)/shard_map/ppermute | solution.py:416
  7.2 10.4 %collective-permute-start.2 = (bf16[64,16,128]{2,1,0:T(8,128)(2,1)S(1)}, bf16[64,16,128]{2,1,0:T(8,128)(2,1)S(1)}, u32[]{:S(2)}, u32[]{:S(2)}) collective-permute-start(bf16[64,16,128]{2,1,0:T(8,128)(2,1)S(1)} %scale.1.refs_0_), channel_id=1, source_target_pairs={{0,48},{8,56},{16,0},{24,8},{32,16},{40,24},{48,32},{56,40},{64,11... | collective-permute-start | bytes 786440 | tf_op jit(solution)/shard_map/ppermute | solution.py:416
  8.8 1.0 copy-start.3
  12.2 15.5 %all-to-all-start = ((bf16[8,10,32,128]{3,2,1,0:T(8,128)(2,1)}), bf16[8,10,32,128]{3,2,1,0:T(8,128)(2,1)S(1)}, u32[]{:S(2)}, u32[]{:S(2)}) async-start(bf16[8,10,32,128]{3,2,1,0:T(8,128)(2,1)} %payload.1), calls=%async_computation | async-start | bytes 1310720 | tf_op jit(solution)/shard_map/all_to_all | solution.py:433
  18.5 15.6 %collective-permute-start.8 = (bf16[3,64,16,128]{3,2,1,0:T(8,128)(2,1)}, bf16[3,64,16,128]{3,2,1,0:T(8,128)(2,1)S(1)}, u32[]{:S(2)}, u32[]{:S(2)}) collective-permute-start(bf16[3,64,16,128]{3,2,1,0:T(8,128)(2,1)} %pad_maximum_fusion.1), channel_id=1, source_target_pairs={{0,8},{8,0},{16,24},{24,16},{32,40},{40,32},{48,56},{56,48},{64,72... | collective-permute-start | bytes 2359304 | tf_op jit(solution)/shard_map/ppermute | solution.py:416
  18.5 11.0 %collective-permute-start.7 = (bf16[64,16,128]{2,1,0:T(8,128)(2,1)S(1)}, bf16[64,16,128]{2,1,0:T(8,128)(2,1)S(1)}, u32[]{:S(2)}, u32[]{:S(2)}) collective-permute-start(bf16[64,16,128]{2,1,0:T(8,128)(2,1)S(1)} %scale.1.refs_0_), channel_id=1, source_target_pairs={{0,8},{8,0},{16,24},{24,16},{32,40},{40,32},{48,56},{56,48},{64,72... | collective-permute-start | bytes 786440 | tf_op jit(solution)/shard_map/ppermute | solution.py:416
  19.0 24.0 %collective-permute-start.3 = (bf16[64,16,128]{2,1,0:T(8,128)(2,1)S(1)}, bf16[64,16,128]{2,1,0:T(8,128)(2,1)S(1)}, u32[]{:S(2)}, u32[]{:S(2)}) collective-permute-start(bf16[64,16,128]{2,1,0:T(8,128)(2,1)S(1)} %collective-permute-done.refs_2_), channel_id=1, source_target_pairs={{0,16},{8,24},{16,32},{24,40},{32,48},{40,56},{48,0},{56,8},{64,80... | collective-permute-start | bytes 786440 | tf_op jit(solution)/shard_map/ppermute | solution.py:416
  19.4 23.7 %collective-permute-start.4 = (bf16[64,16,128]{2,1,0:T(8,128)(2,1)S(1)}, bf16[64,16,128]{2,1,0:T(8,128)(2,1)S(1)}, u32[]{:S(2)}, u32[]{:S(2)}) collective-permute-start(bf16[64,16,128]{2,1,0:T(8,128)(2,1)S(1)} %collective-permute-done.refs_2_), channel_id=1, source_target_pairs={{0,48},{8,56},{16,0},{24,8},{32,16},{40,24},{48,32},{56,40},{64,11... | collective-permute-start | bytes 786440 | tf_op jit(solution)/shard_map/ppermute | solution.py:416
  27.6 15.4 %collective-permute-start.5 = (bf16[64,16,128]{2,1,0:T(8,128)(2,1)S(1)}, bf16[64,16,128]{2,1,0:T(8,128)(2,1)S(1)}, u32[]{:S(2)}, u32[]{:S(2)}) collective-permute-start(bf16[64,16,128]{2,1,0:T(8,128)(2,1)S(1)} %scale.1.refs_0_), channel_id=1, source_target_pairs={{0,32},{8,40},{16,48},{24,56},{32,0},{40,8},{48,16},{56,24},{64,96... | collective-permute-start | bytes 786440 | tf_op jit(solution)/shard_map/ppermute | solution.py:416
  29.6 0.7 copy-start.4
  30.3 12.8 %collective-permute-start.6 = (bf16[64,16,128]{2,1,0:T(8,128)(2,1)S(1)}, bf16[64,16,128]{2,1,0:T(8,128)(2,1)S(1)}, u32[]{:S(2)}, u32[]{:S(2)}) collective-permute-start(bf16[64,16,128]{2,1,0:T(8,128)(2,1)S(1)} %collective-permute-done.refs_2_), channel_id=1, source_target_pairs={{0,32},{8,40},{16,48},{24,56},{32,0},{40,8},{48,16},{56,24},{64,96... | collective-permute-start | bytes 786440 | tf_op jit(solution)/shard_map/ppermute | solution.py:416
  34.1 1.0 copy-start.5
  35.0 13.2 %copy-start.1 = (f32[8192]{0:T(1024)S(1)}, f32[8192]{0:T(1024)}, u32[]{:S(2)}) copy-start(f32[8192]{0:T(1024)} %param.14) | copy-start | bytes 98308
  43.2 20.5 %copy-start.2 = (f32[8192]{0:T(1024)S(1)}, f32[8192]{0:T(1024)}, u32[]{:S(2)}) copy-start(f32[8192]{0:T(1024)} %param.14) | copy-start | bytes 98308
  43.2 5.0 %collective-permute-start.9 = (bf16[4,64,16,128]{3,2,1,0:T(8,128)(2,1)S(1)}, bf16[4,64,16,128]{3,2,1,0:T(8,128)(2,1)S(1)}, u32[]{:S(2)}, u32[]{:S(2)}) collective-permute-start(bf16[4,64,16,128]{3,2,1,0:T(8,128)(2,1)S(1)} %pad_maximum_fusion), channel_id=1, source_target_pairs={{0,8},{8,0},{16,24},{24,16},{32,40},{40,32},{48,56},{56,48},{64,72... | collective-permute-start | bytes 3145736 | tf_op jit(solution)/shard_map/ppermute | solution.py:416
  53.1 10.6 %all-to-all-start.1 = ((bf16[8,8,16,128]{3,2,1,0:T(8,128)(2,1)}), bf16[8,8,16,128]{3,2,1,0:T(8,128)(2,1)S(1)}, u32[]{:S(2)}, u32[]{:S(2)}) async-start(bf16[8,8,16,128]{3,2,1,0:T(8,128)(2,1)} %forward_tiles.5), calls=%async_computation.1 | async-start | bytes 524288 | tf_op jit(solution)/shard_map/all_to_all | solution.py:448
  81.1 5.6 %collective-permute-start.10 = (bf16[4,8,128,128]{3,2,1,0:T(8,128)(2,1)S(1)}, bf16[4,8,128,128]{3,2,1,0:T(8,128)(2,1)S(1)}, u32[]{:S(2)}, u32[]{:S(2)}) collective-permute-start(bf16[4,8,128,128]{3,2,1,0:T(8,128)(2,1)S(1)} %backward_tiles.4), channel_id=1, source_target_pairs={{0,8},{8,0},{16,24},{24,16},{32,40},{40,32},{48,56},{56,48},{64,72... | collective-permute-start | bytes 3145736 | tf_op jit(solution)/shard_map/ppermute | solution.py:416
  81.3 5.4 %collective-permute-start.11 = (f32[64,128]{1,0:T(8,128)S(1)}, f32[64,128]{1,0:T(8,128)S(1)}, u32[]{:S(2)}, u32[]{:S(2)}) collective-permute-start(f32[64,128]{1,0:T(8,128)S(1)} %weight_sums.1), channel_id=1, source_target_pairs={{0,8},{8,0},{16,24},{24,16},{32,40},{40,32},{48,56},{56,48},{64,72... | collective-permute-start | bytes 98312 | tf_op jit(solution)/shard_map/ppermute | solution.py:416
  86.7 8.9 %collective-permute-start.12 = (bf16[4,8,128,128]{3,2,1,0:T(8,128)(2,1)S(1)}, bf16[4,8,128,128]{3,2,1,0:T(8,128)(2,1)S(1)}, u32[]{:S(2)}, u32[]{:S(2)}) collective-permute-start(bf16[4,8,128,128]{3,2,1,0:T(8,128)(2,1)S(1)} %backward_tiles.5), channel_id=1, source_target_pairs={{0,8},{8,0},{16,24},{24,16},{32,40},{40,32},{48,56},{56,48},{64,72... | collective-permute-start | bytes 3145736 | tf_op jit(solution)/shard_map/ppermute | solution.py:416
  92.2 16.2 %collective-permute-start.16 = (bf16[9,128,128]{2,1,0:T(8,128)(2,1)S(1)}, bf16[9,128,128]{2,1,0:T(8,128)(2,1)S(1)}, u32[]{:S(2)}, u32[]{:S(2)}) collective-permute-start(bf16[9,128,128]{2,1,0:T(8,128)(2,1)S(1)} %get-tuple-element.54), channel_id=1, source_target_pairs={{0,16},{8,24},{16,32},{24,40},{32,48},{40,56},{48,0},{56,8},{64,80... | collective-permute-start | bytes 884744 | tf_op jit(solution)/shard_map/ppermute | solution.py:416
  92.4 16.0 %collective-permute-start.17 = (bf16[9,128,128]{2,1,0:T(8,128)(2,1)S(1)}, bf16[9,128,128]{2,1,0:T(8,128)(2,1)S(1)}, u32[]{:S(2)}, u32[]{:S(2)}) collective-permute-start(bf16[9,128,128]{2,1,0:T(8,128)(2,1)S(1)} %get-tuple-element.62), channel_id=1, source_target_pairs={{0,48},{8,56},{16,0},{24,8},{32,16},{40,24},{48,32},{56,40},{64,11... | collective-permute-start | bytes 884744 | tf_op jit(solution)/shard_map/ppermute | solution.py:416
  95.7 12.8 %collective-permute-start.18 = (bf16[9,128,128]{2,1,0:T(8,128)(2,1)S(1)}, bf16[9,128,128]{2,1,0:T(8,128)(2,1)S(1)}, u32[]{:S(2)}, u32[]{:S(2)}) collective-permute-start(bf16[9,128,128]{2,1,0:T(8,128)(2,1)S(1)} %get-tuple-element.63), channel_id=1, source_target_pairs={{0,32},{8,40},{16,48},{24,56},{32,0},{40,8},{48,16},{56,24},{64,96... | collective-permute-start | bytes 884744 | tf_op jit(solution)/shard_map/ppermute | solution.py:416
  101.0 0.7 copy-start.9
  101.7 0.8 copy-start.11
  102.5 25.0 %all-to-all-start.3 = ((bf16[8,8,32,128]{3,2,1,0:T(8,128)(2,1)}), bf16[8,8,32,128]{3,2,1,0:T(8,128)(2,1)S(1)}, u32[]{:S(2)}, u32[]{:S(2)}) async-start(bf16[8,8,32,128]{3,2,1,0:T(8,128)(2,1)} %get-tuple-element.57), calls=%async_computation.3 | async-start | bytes 1048576 | tf_op jit(solution)/shard_map/all_to_all | solution.py:485
  108.6 17.4 %collective-permute-start.19 = (bf16[9,128,128]{2,1,0:T(8,128)(2,1)S(1)}, bf16[9,128,128]{2,1,0:T(8,128)(2,1)S(1)}, u32[]{:S(2)}, u32[]{:S(2)}) collective-permute-start(bf16[9,128,128]{2,1,0:T(8,128)(2,1)S(1)} %cross.1.sent), channel_id=1, source_target_pairs={{0,64},{8,72},{16,80},{24,88},{32,96},{40,104},{48,112},{56,120},{... | collective-permute-start | bytes 884744 | tf_op jit(solution)/shard_map/ppermute | solution.py:416
  110.1 9.9 %collective-permute-start.13 = (bf16[8,128,128]{2,1,0:T(8,128)(2,1)}, bf16[8,128,128]{2,1,0:T(8,128)(2,1)S(1)}, u32[]{:S(2)}, u32[]{:S(2)}) collective-permute-start(bf16[8,128,128]{2,1,0:T(8,128)(2,1)} %copy-done.11), channel_id=1, source_target_pairs={{0,16},{8,24},{16,32},{24,40},{32,48},{40,56},{48,0},{56,8},{64,80... | collective-permute-start | bytes 786440 | tf_op jit(solution)/shard_map/ppermute | solution.py:416
  110.9 13.5 %collective-permute-start.14 = (bf16[8,128,128]{2,1,0:T(8,128)(2,1)}, bf16[8,128,128]{2,1,0:T(8,128)(2,1)S(1)}, u32[]{:S(2)}, u32[]{:S(2)}) collective-permute-start(bf16[8,128,128]{2,1,0:T(8,128)(2,1)} %copy-done.10), channel_id=1, source_target_pairs={{0,48},{8,56},{16,0},{24,8},{32,16},{40,24},{48,32},{56,40},{64,11... | collective-permute-start | bytes 786440 | tf_op jit(solution)/shard_map/ppermute | solution.py:416
  113.3 12.7 %collective-permute-start.15 = (bf16[8,128,128]{2,1,0:T(8,128)(2,1)}, bf16[8,128,128]{2,1,0:T(8,128)(2,1)S(1)}, u32[]{:S(2)}, u32[]{:S(2)}) collective-permute-start(bf16[8,128,128]{2,1,0:T(8,128)(2,1)} %copy-done.9), channel_id=1, source_target_pairs={{0,32},{8,40},{16,48},{24,56},{32,0},{40,8},{48,16},{56,24},{64,96... | collective-permute-start | bytes 786440 | tf_op jit(solution)/shard_map/ppermute | solution.py:416
  (3 other events, 2.0 us)

commit v4 on v3

--- a/solution.py
+++ b/solution.py
@@ -8,7 +8,7 @@
 from jax.sharding import PartitionSpec as P
 
 LANES = 128
-UNROLL = 8
+UNROLL, LOAD = 16, 8
 BF16 = jnp.bfloat16
 F32 = jnp.float32
 META_COUNTS, META_ME = 16, 17
@@ -60,22 +60,24 @@
 
 
 def start_tiles(k, slab, count, tiles, buffer, sems):
-    for chunk in range(tiles.shape[1] // UNROLL):
-        @pl.when(chunk * UNROLL < count)
+    for chunk in range(tiles.shape[1] // LOAD):
+        @pl.when(chunk * LOAD < count)
         def _():
-            pltpu.make_async_copy(
-                tiles.at[slab, pl.ds(chunk * UNROLL, UNROLL)],
-                buffer.at[k, pl.ds(chunk * UNROLL, UNROLL)],
-                sems.at[k, chunk],
-            ).start()
+            load_tiles(k, slab, chunk, tiles, buffer, sems).start()
+
+
+def load_tiles(k, slab, chunk, tiles, buffer, sems):
+    these = pl.ds(chunk * LOAD, LOAD)
+    return pltpu.make_async_copy(tiles.at[slab, these], buffer.at[k, these], sems.at[k, chunk])
 
 
 def over_tiles(k, slab, count, meta, tiles, buffer, sems, source_of, target_of, dims, accumulator):
     def step(chunk, carry):
         first = chunk * UNROLL
-        pltpu.make_async_copy(
-            tiles.at[slab, pl.ds(first, UNROLL)], buffer.at[k, pl.ds(first, UNROLL)], sems.at[k, chunk]
-        ).wait()
+        for part in range(UNROLL // LOAD):
+            @pl.when(first + part * LOAD < count)
+            def _():
+                load_tiles(k, slab, chunk * (UNROLL // LOAD) + part, tiles, buffer, sems).wait()
         products, targets = [], []
         for j in range(0, UNROLL, 2):
             c = first + j
@@ -171,7 +173,7 @@
         out_shape=out, in_specs=specs, out_specs=spec(VMEM) if last else spec(ANY),
         scratch_shapes=[
             VMEM((pieces, *tiles.shape[1:]), BF16),
-            pltpu.SemaphoreType.DMA((pieces, tiles.shape[1] // UNROLL)),
+            pltpu.SemaphoreType.DMA((pieces, tiles.shape[1] // LOAD)),
             VMEM((pieces, *shape), BF16),
             pltpu.SemaphoreType.DMA((pieces + 2,)),
             VMEM(shape, F32),
@@ -273,7 +275,7 @@
         outs = [jax.ShapeDtypeStruct((blocks, rows, LANES), F32)] + [jax.ShapeDtypeStruct(packed, BF16)] * (pieces - 1)
     scratch = [
         VMEM((pieces, *tiles.shape[1:]), BF16),
-        pltpu.SemaphoreType.DMA((pieces, tiles.shape[1] // UNROLL)),
+        pltpu.SemaphoreType.DMA((pieces, tiles.shape[1] // LOAD)),
         VMEM(ys.shape, BF16),
         pltpu.SemaphoreType.DMA((1,)),
         VMEM((pieces, blocks, rows, LANES), F32),
@@ -418,12 +420,12 @@
     scaled = pl.pallas_call(
         scale_kernel,
         out_shape=jax.ShapeDtypeStruct((blocks, feat_local, LANES), BF16),
-        compiler_params=params(), name="scale",
+        compiler_params=params(56), name="scale",
     )(feats.T, norm_blocks)
     payload = pl.pallas_call(
         payload_kernel,
         out_shape=jax.ShapeDtypeStruct((peers, per_peer + 2, hid_local, LANES), BF16),
-        compiler_params=params(), name="payload",
+        compiler_params=params(56), name="payload",
     )(cotangent.T, weight, bias.reshape(1, hid_local))
     across = move(scaled, 1, 0, 0)
     down, up = move(scaled, 0, 1, 0), move(scaled, 0, 3, 0)
@@ -493,7 +495,7 @@
         ),
         in_specs=[spec(SMEM)] + [spec(VMEM)] * 7,
         compiler_params=params(), name="finish",
-    )(place, parts[0], norm_blocks, *arrived, crossed, came)
+    )(after(place, hidden), parts[0], norm_blocks, *arrived, crossed, came)
     return hidden.T, grad_weight, grad_bias.reshape(hid_local), grad_feats.T
 
 

time: 129 us -> 125 us (0.969)
  Pallas kernels: 43.3 us -> 38.3 us
  local copies, waits for them, and re-layouts: 7.31 us -> 3.37 us
  starting transfers between devices: 36.2 us -> 39.4 us
  waiting for transfers between devices: 26.6 us -> 28 us
    pallas_call x3, Pallas kernels: 17.7 us -> 13.5 us  [forward_call(): pl.pallas_call(functools.partial(forward_kernel, hops, where, first, last...]
    unnamed x24 -> x12, local copies, waits for them, and re-layouts: 7.24 us -> 3.29 us
    pallas_call x4, Pallas kernels: 19.8 us -> 16.3 us  [backward_call(): pl.pallas_call(functools.partial(backward_kernel, hops, mode), out_shape=...]
    ppermute x20, starting transfers between devices: 23.9 us -> 25.7 us  [move(): return lax.ppermute(value, 'nodes', pairs)]
    pallas_call x1, Pallas kernels: 0.05 us -> 1.7 us  [on_device(): pl.pallas_call(scale_kernel, out_shape=jax.ShapeDtypeStruct((blocks, feat...]
    all_to_all x1, starting transfers between devices: 3.42 us -> 4.88 us  [on_device(): agg = lax.all_to_all(total, 'feat', 0, 0)]
  transfers between devices with their start and end apart: 23 -> 23, of which waited for: 6 -> 4; matrix products, arithmetic and copies ran while one was open for 2% -> 2% of each run, Pallas kernels for 24% -> 20%
where the time goes in v4:
time: 125 us; the launch traced here: 124 us
  starting transfers between devices  39.4 us (32%)
  Pallas kernels  38.3 us (31%)
  waiting for transfers between devices  28 us (22%)
  blocking collectives  11.9 us (10%)
  local copies, waits for them, and re-layouts  3.37 us (3%)
  other arithmetic  2.64 us (2%)
    ppermute x20, starting transfers between devices, move(): return lax.ppermute(value, 'nodes', pairs)  25.7 us
    pallas_call x4, Pallas kernels, backward_call(): pl.pallas_call(functools.partial(backward_kernel, hops, mode), out_shape=...  16.3 us
    ppermute x20, waiting for transfers between devices, move(): return lax.ppermute(value, 'nodes', pairs)  15 us
    pallas_call x3, Pallas kernels, forward_call(): pl.pallas_call(functools.partial(forward_kernel, hops, where, first, last...  13.5 us
    all_to_all x1, blocking collectives, on_device(): back = lax.all_to_all(back, 'feat', 0, 0)  11.9 us
    all_to_all x1, waiting for transfers between devices, on_device(): agg = lax.all_to_all(total, 'feat', 0, 0)  7.59 us
    all_to_all x1, waiting for transfers between devices, on_device(): received = lax.all_to_all(payload, 'feat', 0, 0)  5.37 us
    all_to_all x1, starting transfers between devices, on_device(): received = lax.all_to_all(payload, 'feat', 0, 0)  5.34 us
  transfers between devices with their start and end apart: 23, of which 4 were waited for; matrix products, arithmetic and copies ran while one was open for 2% of the time, Pallas kernels for 20%

profile of v4, /device:TPU:0, one launch (start us, length us, event | category | flops | bytes accessed | tf_op | source)
XLA Modules:
  0.0 124.5 jit_solution(14574784488232524668)
XLA Ops:
  0.6 1.7 %scale.1.refs_0_ = bf16[64,16,128]{2,1,0:T(8,128)(2,1)} custom-call(bf16[16,8192]{1,0:T(8,128)(2,1)} %bitcast.39, f32[64,128]{1,0:T(8,128)} %bitcast.26), custom_call_target="tpu_custom_call" | custom-call | tf_op jit(solution)/shard_map/scale/pallas_call | solution.py:420
  2.3 3.1 %collective-permute-start = (bf16[64,16,128]{2,1,0:T(8,128)(2,1)}, bf16[64,16,128]{2,1,0:T(8,128)(2,1)S(1)}, u32[]{:S(2)}, u32[]{:S(2)}) collective-permute-start(bf16[64,16,128]{2,1,0:T(8,128)(2,1)} %scale.1.refs_0_), channel_id=1, source_target_pairs={{0,64},{8,72},{16,80},{24,88},{32,96},{40,104},{48,112},{56,120},{... | collective-permute-start | bytes 786440 | tf_op jit(solution)/shard_map/ppermute | solution.py:418
  5.4 1.6 %collective-permute-start.1 = (bf16[64,16,128]{2,1,0:T(8,128)(2,1)}, bf16[64,16,128]{2,1,0:T(8,128)(2,1)S(1)}, u32[]{:S(2)}, u32[]{:S(2)}) collective-permute-start(bf16[64,16,128]{2,1,0:T(8,128)(2,1)} %scale.1.refs_0_), channel_id=1, source_target_pairs={{0,16},{8,24},{16,32},{24,40},{32,48},{40,56},{48,0},{56,8},{64,80... | collective-permute-start | bytes 786440 | tf_op jit(solution)/shard_map/ppermute | solution.py:418
  7.0 1.7 %collective-permute-start.2 = (bf16[64,16,128]{2,1,0:T(8,128)(2,1)}, bf16[64,16,128]{2,1,0:T(8,128)(2,1)S(1)}, u32[]{:S(2)}, u32[]{:S(2)}) collective-permute-start(bf16[64,16,128]{2,1,0:T(8,128)(2,1)} %scale.1.refs_0_), channel_id=1, source_target_pairs={{0,48},{8,56},{16,0},{24,8},{32,16},{40,24},{48,32},{56,40},{64,11... | collective-permute-start | bytes 786440 | tf_op jit(solution)/shard_map/ppermute | solution.py:418
  8.7 2.0 %payload.1 = bf16[8,10,32,128]{3,2,1,0:T(8,128)(2,1)} custom-call(bf16[32,8192]{1,0:T(8,128)(2,1)} %bitcast.37, bf16[16,256]{1,0:T(8,128)(2,1)} %weight.1, f32[1,32]{1,0:T(1,128)} %bitcast.40), custom_call_target="tpu_custom_call" | custom-call | tf_op jit(solution)/shard_map/payload/pallas_call | solution.py:425
  10.7 5.3 %all-to-all-start = ((bf16[8,10,32,128]{3,2,1,0:T(8,128)(2,1)}), bf16[8,10,32,128]{3,2,1,0:T(8,128)(2,1)S(1)}, u32[]{:S(2)}, u32[]{:S(2)}) async-start(bf16[8,10,32,128]{3,2,1,0:T(8,128)(2,1)} %payload.1), calls=%async_computation | async-start | bytes 1310720 | tf_op jit(solution)/shard_map/all_to_all | solution.py:435
  16.1 1.0 pad_maximum_fusion.1
  17.9 2.9 %collective-permute-start.4 = (bf16[64,16,128]{2,1,0:T(8,128)(2,1)S(1)}, bf16[64,16,128]{2,1,0:T(8,128)(2,1)S(1)}, u32[]{:S(2)}, u32[]{:S(2)}) collective-permute-start(bf16[64,16,128]{2,1,0:T(8,128)(2,1)S(1)} %collective-permute-done.refs_2_), channel_id=1, source_target_pairs={{0,48},{8,56},{16,0},{24,8},{32,16},{40,24},{48,32},{56,40},{64,11... | collective-permute-start | bytes 786440 | tf_op jit(solution)/shard_map/ppermute | solution.py:418
  20.8 5.4 %all-to-all-done.received = bf16[8,10,32,128]{3,2,1,0:T(8,128)(2,1)S(1)} async-done(((bf16[8,10,32,128]{3,2,1,0:T(8,128)(2,1)}), bf16[8,10,32,128]{3,2,1,0:T(8,128)(2,1)S(1)}, u32[]{:S(2)}, u32[]{:S(2)}) %all-to-all-start) | async-done | bytes 655392 | tf_op jit(solution)/shard_map/all_to_all | solution.py:435
  26.2 1.9 %collective-permute-start.5 = (bf16[64,16,128]{2,1,0:T(8,128)(2,1)}, bf16[64,16,128]{2,1,0:T(8,128)(2,1)S(1)}, u32[]{:S(2)}, u32[]{:S(2)}) collective-permute-start(bf16[64,16,128]{2,1,0:T(8,128)(2,1)} %scale.1.refs_0_), channel_id=1, source_target_pairs={{0,32},{8,40},{16,48},{24,56},{32,0},{40,8},{48,16},{56,24},{64,96... | collective-permute-start | bytes 786440 | tf_op jit(solution)/shard_map/ppermute | solution.py:418
  28.8 1.6 %collective-permute-start.6 = (bf16[64,16,128]{2,1,0:T(8,128)(2,1)S(1)}, bf16[64,16,128]{2,1,0:T(8,128)(2,1)S(1)}, u32[]{:S(2)}, u32[]{:S(2)}) collective-permute-start(bf16[64,16,128]{2,1,0:T(8,128)(2,1)S(1)} %collective-permute-done.refs_2_), channel_id=1, source_target_pairs={{0,32},{8,40},{16,48},{24,56},{32,0},{40,8},{48,16},{56,24},{64,96... | collective-permute-start | bytes 786440 | tf_op jit(solution)/shard_map/ppermute | solution.py:418
  32.0 0.9 copy-done
  33.0 0.9 copy-done.3
  33.9 5.8 %forward_tiles.3.refs_5_ = f32[64,16,128]{2,1,0:T(8,128)S(1)} custom-call(s32[18,32]{1,0:T(8,128)S(1)} %add_add_fusion.meta, bf16[64,16,128]{2,1,0:T(8,128)(2,1)S(1)} %copy-done, bf16[64,16,128]{2,1,0:T(8,128)(2,1)S(1)} %copy-done.3, bf16[64,16,128]{2,1,0:T(8,128)(2,1)S(1)} %collective-permute-done.refs_2_, ...), custom_call_target="tpu_custom_call" | custom-call | flops 67108864 | bytes 8388608 | tf_op jit(solution)/shard_map/forward_tiles/pallas_call | solution.py:171
  40.0 3.2 %forward_tiles.4.refs_2_ = f32[64,16,128]{2,1,0:T(8,128)S(1)} custom-call(s32[18,32]{1,0:T(8,128)S(1)} %add_add_fusion.meta, bf16[64,16,128]{2,1,0:T(8,128)(2,1)S(1)} %collective-permute-done.3.refs_0_, bf16[64,16,128]{2,1,0:T(8,128)(2,1)S(1)} %collective-permute-done.4.refs_1_, bf16[64,16,128]{2,1,0:T(8,128)(2,1)S(1)} %collective-permute-done.5.refs_2_, ...), custom_call_target="tpu_custom_call" | custom-call | flops 33554432 | bytes 4194304 | tf_op jit(solution)/shard_map/forward_tiles/pallas_call | solution.py:171
  43.2 4.6 %forward_tiles.5 = bf16[8,8,16,128]{3,2,1,0:T(8,128)(2,1)} custom-call(s32[18,32]{1,0:T(8,128)S(1)} %add_add_fusion.meta, bf16[4,64,16,128]{3,2,1,0:T(8,128)(2,1)S(1)} %collective-permute-done.9.refs_0_, bf16[16,32,128,128]{3,2,1,0:T(8,128)(2,1)} %bitcast.32, f32[64,16,128]{2,1,0:T(8,128)S(1)} %forward_tiles.4.refs_2_, f32[64,128]{1,0:T(8,128)S(1)} %bitcast.27), custom_call_target="tpu_custom_call" | custom-call | flops 33554432 | bytes 4194304 | tf_op jit(solution)/shard_map/forward_tiles/pallas_call | solution.py:171
  47.8 4.9 %all-to-all-start.1 = ((bf16[8,8,16,128]{3,2,1,0:T(8,128)(2,1)}), bf16[8,8,16,128]{3,2,1,0:T(8,128)(2,1)S(1)}, u32[]{:S(2)}, u32[]{:S(2)}) async-start(bf16[8,8,16,128]{3,2,1,0:T(8,128)(2,1)} %forward_tiles.5), calls=%async_computation.1 | async-start | bytes 524288 | tf_op jit(solution)/shard_map/all_to_all | solution.py:450
  52.7 7.6 %all-to-all-done.1.agg = bf16[8,8,16,128]{3,2,1,0:T(8,128)(2,1)S(1)} async-done(((bf16[8,8,16,128]{3,2,1,0:T(8,128)(2,1)}), bf16[8,8,16,128]{3,2,1,0:T(8,128)(2,1)S(1)}, u32[]{:S(2)}, u32[]{:S(2)}) %all-to-all-start.1) | async-done | bytes 262176 | tf_op jit(solution)/shard_map/all_to_all | solution.py:450
  60.3 2.2 %dense.1 = (bf16[8,14,16,128]{3,2,1,0:T(8,128)(2,1)S(1)}, bf16[8,8,32,128]{3,2,1,0:T(8,128)(2,1)}) custom-call(s32[1]{0:T(128)} %bitcast.place, bf16[8,8,16,128]{3,2,1,0:T(8,128)(2,1)S(1)} %all-to-all-done.1.agg, bf16[8,10,32,128]{3,2,1,0:T(8,128)(2,1)S(1)} %all-to-all-done.received, f32[64,128]{1,0:T(8,128)S(1)} %bitcast.28), custom_call_target="tpu_custom_call" | custom-call | tf_op jit(solution)/shard_map/dense/pallas_call | solution.py:451
  62.5 11.9 %all_to_all.20.refs_0_.back = bf16[8,14,16,128]{3,2,1,0:T(8,128)(2,1)S(1)} all-to-all(bf16[8,14,16,128]{3,2,1,0:T(8,128)(2,1)S(1)} %get-tuple-element.50), channel_id=1, replica_groups=mesh['nodes'=16,'feat'=8] {'feat'}, dimensions={0} | all-to-all | bytes 917504 | tf_op jit(solution)/shard_map/all_to_all | solution.py:460
  74.4 4.0 %backward_tiles.4 = bf16[4,8,128,128]{3,2,1,0:T(8,128)(2,1)S(1)} custom-call(s32[18,32]{1,0:T(8,128)S(1)} %add_add_fusion.meta, bf16[8,14,16,128]{3,2,1,0:T(8,128)(2,1)S(1)} %all_to_all.20.refs_0_.back, bf16[16,32,128,128]{3,2,1,0:T(8,128)(2,1)} %bitcast.33), custom_call_target="tpu_custom_call" | custom-call | flops 33554432 | bytes 4194304 | tf_op jit(solution)/shard_map/backward_tiles/pallas_call | solution.py:286
  79.2 4.0 %backward_tiles.5 = bf16[4,8,128,128]{3,2,1,0:T(8,128)(2,1)S(1)} custom-call(s32[18,32]{1,0:T(8,128)S(1)} %add_add_fusion.meta, bf16[8,14,16,128]{3,2,1,0:T(8,128)(2,1)S(1)} %all_to_all.20.refs_0_.back, bf16[16,32,128,128]{3,2,1,0:T(8,128)(2,1)} %bitcast.34), custom_call_target="tpu_custom_call" | custom-call | flops 33554432 | bytes 4194304 | tf_op jit(solution)/shard_map/backward_tiles/pallas_call | solution.py:286
  83.3 4.1 %backward_tiles.6 = (bf16[9,128,128]{2,1,0:T(8,128)(2,1)S(1)}, bf16[9,128,128]{2,1,0:T(8,128)(2,1)}, bf16[9,128,128]{2,1,0:T(8,128)(2,1)S(1)}, bf16[9,128,128]{2,1,0:T(8,128)(2,1)S(1)}) custom-call(s32[18,32]{1,0:T(8,128)S(1)} %add_add_fusion.meta, bf16[8,14,16,128]{3,2,1,0:T(8,128)(2,1)S(1)} %all_to_all.20.refs_0_.back, ...), custom_call_target="tpu_custom_call" | custom-call | flops 33554432 | bytes 4194304 | tf_op jit(solution)/shard_map/backward_tiles/pallas_call | solution.py:286
  87.4 2.7 %collective-permute-start.16 = (bf16[9,128,128]{2,1,0:T(8,128)(2,1)}, bf16[9,128,128]{2,1,0:T(8,128)(2,1)S(1)}, u32[]{:S(2)}, u32[]{:S(2)}) collective-permute-start(bf16[9,128,128]{2,1,0:T(8,128)(2,1)} %get-tuple-element.55), channel_id=1, source_target_pairs={{0,16},{8,24},{16,32},{24,40},{32,48},{40,56},{48,0},{56,8},{64,80... | collective-permute-start | bytes 884744 | tf_op jit(solution)/shard_map/ppermute | solution.py:418
  90.7 1.6 %collective-permute-start.18 = (bf16[9,128,128]{2,1,0:T(8,128)(2,1)S(1)}, bf16[9,128,128]{2,1,0:T(8,128)(2,1)S(1)}, u32[]{:S(2)}, u32[]{:S(2)}) collective-permute-start(bf16[9,128,128]{2,1,0:T(8,128)(2,1)S(1)} %get-tuple-element.65), channel_id=1, source_target_pairs={{0,32},{8,40},{16,48},{24,56},{32,0},{40,8},{48,16},{56,24},{64,96... | collective-permute-start | bytes 884744 | tf_op jit(solution)/shard_map/ppermute | solution.py:418
  92.3 4.2 %backward_tiles.7 = (f32[64,16,128]{2,1,0:T(8,128)S(1)}, bf16[8,128,128]{2,1,0:T(8,128)(2,1)S(1)}, bf16[8,128,128]{2,1,0:T(8,128)(2,1)S(1)}, bf16[8,128,128]{2,1,0:T(8,128)(2,1)S(1)}) custom-call(s32[18,32]{1,0:T(8,128)S(1)} %add_add_fusion.meta, bf16[8,14,16,128]{3,2,1,0:T(8,128)(2,1)S(1)} %all_to_all.20.refs_0_.back, bf16[16,32,128,128]{3,2,1,0:T(8,128)(2,1)} %bitcast.36, ...), custom_call_target="tpu_custom_call" | custom-call | flops 33554432 | bytes 4194304 | tf_op jit(solution)/shard_map/backward_tiles/pallas_call | solution.py:286
  97.1 3.5 %all-to-all-start.3 = ((bf16[8,8,32,128]{3,2,1,0:T(8,128)(2,1)}), bf16[8,8,32,128]{3,2,1,0:T(8,128)(2,1)S(1)}, u32[]{:S(2)}, u32[]{:S(2)}) async-start(bf16[8,8,32,128]{3,2,1,0:T(8,128)(2,1)} %get-tuple-element.58), calls=%async_computation.3 | async-start | bytes 1048576 | tf_op jit(solution)/shard_map/all_to_all | solution.py:487
  100.7 4.4 %collective-permute-done.18.far = bf16[9,128,128]{2,1,0:T(8,128)(2,1)S(1)} collective-permute-done((bf16[9,128,128]{2,1,0:T(8,128)(2,1)S(1)}, bf16[9,128,128]{2,1,0:T(8,128)(2,1)S(1)}, u32[]{:S(2)}, u32[]{:S(2)}) %collective-permute-start.18) | collective-permute-done | bytes 294944 | tf_op jit(solution)/shard_map/ppermute | solution.py:418
  105.3 3.1 %collective-permute-start.19 = (bf16[9,128,128]{2,1,0:T(8,128)(2,1)S(1)}, bf16[9,128,128]{2,1,0:T(8,128)(2,1)S(1)}, u32[]{:S(2)}, u32[]{:S(2)}) collective-permute-start(bf16[9,128,128]{2,1,0:T(8,128)(2,1)S(1)} %cross.1.sent), channel_id=1, source_target_pairs={{0,64},{8,72},{16,80},{24,88},{32,96},{40,104},{48,112},{56,120},{... | collective-permute-start | bytes 884744 | tf_op jit(solution)/shard_map/ppermute | solution.py:418
  109.3 2.3 %collective-permute-start.14 = (bf16[8,128,128]{2,1,0:T(8,128)(2,1)S(1)}, bf16[8,128,128]{2,1,0:T(8,128)(2,1)S(1)}, u32[]{:S(2)}, u32[]{:S(2)}) collective-permute-start(bf16[8,128,128]{2,1,0:T(8,128)(2,1)S(1)} %get-tuple-element.61), channel_id=1, source_target_pairs={{0,48},{8,56},{16,0},{24,8},{32,16},{40,24},{48,32},{56,40},{64,11... | collective-permute-start | bytes 786440 | tf_op jit(solution)/shard_map/ppermute | solution.py:418
  112.5 10.6 %collective-permute-done.13.down = bf16[8,128,128]{2,1,0:T(8,128)(2,1)S(1)} collective-permute-done((bf16[8,128,128]{2,1,0:T(8,128)(2,1)}, bf16[8,128,128]{2,1,0:T(8,128)(2,1)S(1)}, u32[]{:S(2)}, u32[]{:S(2)}) %collective-permute-start.13) | collective-permute-done | bytes 262176 | tf_op jit(solution)/shard_map/ppermute | solution.py:418
  123.0 1.4 %finish.1 = (f32[16,8192]{1,0:T(8,128)}, f32[16,256]{1,0:T(8,128)}, f32[1,32]{1,0:T(1,128)}) custom-call(s32[1]{0:T(128)} %bitcast.place, f32[64,16,128]{2,1,0:T(8,128)S(1)} %get-tuple-element.60.kept, f32[64,128]{1,0:T(8,128)S(1)} %bitcast.29, bf16[8,128,128]{2,1,0:T(8,128)(2,1)S(1)} %collective-permute-done.13.down, ...), custom_call_target="tpu_custom_call" | custom-call | tf_op jit(solution)/shard_map/finish/pallas_call | solution.py:489
  (47 shorter events, 7.5 us)
Async XLA Ops:
  2.3 13.7 %collective-permute-start = (bf16[64,16,128]{2,1,0:T(8,128)(2,1)}, bf16[64,16,128]{2,1,0:T(8,128)(2,1)S(1)}, u32[]{:S(2)}, u32[]{:S(2)}) collective-permute-start(bf16[64,16,128]{2,1,0:T(8,128)(2,1)} %scale.1.refs_0_), channel_id=1, source_target_pairs={{0,64},{8,72},{16,80},{24,88},{32,96},{40,104},{48,112},{56,120},{... | collective-permute-start | bytes 786440 | tf_op jit(solution)/shard_map/ppermute | solution.py:418
  5.4 10.6 %collective-permute-start.1 = (bf16[64,16,128]{2,1,0:T(8,128)(2,1)}, bf16[64,16,128]{2,1,0:T(8,128)(2,1)S(1)}, u32[]{:S(2)}, u32[]{:S(2)}) collective-permute-start(bf16[64,16,128]{2,1,0:T(8,128)(2,1)} %scale.1.refs_0_), channel_id=1, source_target_pairs={{0,16},{8,24},{16,32},{24,40},{32,48},{40,56},{48,0},{56,8},{64,80... | collective-permute-start | bytes 786440 | tf_op jit(solution)/shard_map/ppermute | solution.py:418
  7.0 9.1 %collective-permute-start.2 = (bf16[64,16,128]{2,1,0:T(8,128)(2,1)}, bf16[64,16,128]{2,1,0:T(8,128)(2,1)S(1)}, u32[]{:S(2)}, u32[]{:S(2)}) collective-permute-start(bf16[64,16,128]{2,1,0:T(8,128)(2,1)} %scale.1.refs_0_), channel_id=1, source_target_pairs={{0,48},{8,56},{16,0},{24,8},{32,16},{40,24},{48,32},{56,40},{64,11... | collective-permute-start | bytes 786440 | tf_op jit(solution)/shard_map/ppermute | solution.py:418
  10.7 15.5 %all-to-all-start = ((bf16[8,10,32,128]{3,2,1,0:T(8,128)(2,1)}), bf16[8,10,32,128]{3,2,1,0:T(8,128)(2,1)S(1)}, u32[]{:S(2)}, u32[]{:S(2)}) async-start(bf16[8,10,32,128]{3,2,1,0:T(8,128)(2,1)} %payload.1), calls=%async_computation | async-start | bytes 1310720 | tf_op jit(solution)/shard_map/all_to_all | solution.py:435
  17.1 15.0 %collective-permute-start.8 = (bf16[3,64,16,128]{3,2,1,0:T(8,128)(2,1)}, bf16[3,64,16,128]{3,2,1,0:T(8,128)(2,1)S(1)}, u32[]{:S(2)}, u32[]{:S(2)}) collective-permute-start(bf16[3,64,16,128]{3,2,1,0:T(8,128)(2,1)} %pad_maximum_fusion.1), channel_id=1, source_target_pairs={{0,8},{8,0},{16,24},{24,16},{32,40},{40,32},{48,56},{56,48},{64,72... | collective-permute-start | bytes 2359304 | tf_op jit(solution)/shard_map/ppermute | solution.py:418
  17.1 11.0 %collective-permute-start.7 = (bf16[64,16,128]{2,1,0:T(8,128)(2,1)}, bf16[64,16,128]{2,1,0:T(8,128)(2,1)S(1)}, u32[]{:S(2)}, u32[]{:S(2)}) collective-permute-start(bf16[64,16,128]{2,1,0:T(8,128)(2,1)} %scale.1.refs_0_), channel_id=1, source_target_pairs={{0,8},{8,0},{16,24},{24,16},{32,40},{40,32},{48,56},{56,48},{64,72... | collective-permute-start | bytes 786440 | tf_op jit(solution)/shard_map/ppermute | solution.py:418
  17.6 22.2 %collective-permute-start.3 = (bf16[64,16,128]{2,1,0:T(8,128)(2,1)S(1)}, bf16[64,16,128]{2,1,0:T(8,128)(2,1)S(1)}, u32[]{:S(2)}, u32[]{:S(2)}) collective-permute-start(bf16[64,16,128]{2,1,0:T(8,128)(2,1)S(1)} %collective-permute-done.refs_2_), channel_id=1, source_target_pairs={{0,16},{8,24},{16,32},{24,40},{32,48},{40,56},{48,0},{56,8},{64,80... | collective-permute-start | bytes 786440 | tf_op jit(solution)/shard_map/ppermute | solution.py:418
  17.9 21.8 %collective-permute-start.4 = (bf16[64,16,128]{2,1,0:T(8,128)(2,1)S(1)}, bf16[64,16,128]{2,1,0:T(8,128)(2,1)S(1)}, u32[]{:S(2)}, u32[]{:S(2)}) collective-permute-start(bf16[64,16,128]{2,1,0:T(8,128)(2,1)S(1)} %collective-permute-done.refs_2_), channel_id=1, source_target_pairs={{0,48},{8,56},{16,0},{24,8},{32,16},{40,24},{48,32},{56,40},{64,11... | collective-permute-start | bytes 786440 | tf_op jit(solution)/shard_map/ppermute | solution.py:418
  26.2 13.6 %collective-permute-start.5 = (bf16[64,16,128]{2,1,0:T(8,128)(2,1)}, bf16[64,16,128]{2,1,0:T(8,128)(2,1)S(1)}, u32[]{:S(2)}, u32[]{:S(2)}) collective-permute-start(bf16[64,16,128]{2,1,0:T(8,128)(2,1)} %scale.1.refs_0_), channel_id=1, source_target_pairs={{0,32},{8,40},{16,48},{24,56},{32,0},{40,8},{48,16},{56,24},{64,96... | collective-permute-start | bytes 786440 | tf_op jit(solution)/shard_map/ppermute | solution.py:418
  28.1 0.7 copy-start.2
  28.8 11.0 %collective-permute-start.6 = (bf16[64,16,128]{2,1,0:T(8,128)(2,1)S(1)}, bf16[64,16,128]{2,1,0:T(8,128)(2,1)S(1)}, u32[]{:S(2)}, u32[]{:S(2)}) collective-permute-start(bf16[64,16,128]{2,1,0:T(8,128)(2,1)S(1)} %collective-permute-done.refs_2_), channel_id=1, source_target_pairs={{0,32},{8,40},{16,48},{24,56},{32,0},{40,8},{48,16},{56,24},{64,96... | collective-permute-start | bytes 786440 | tf_op jit(solution)/shard_map/ppermute | solution.py:418
  32.0 1.0 copy-start
  33.0 0.9 copy-start.3
  33.9 9.3 %copy-start.1 = (f32[8192]{0:T(1024)S(1)}, f32[8192]{0:T(1024)}, u32[]{:S(2)}) copy-start(f32[8192]{0:T(1024)} %param.14) | copy-start | bytes 98308
  39.9 3.3 %collective-permute-start.9 = (bf16[4,64,16,128]{3,2,1,0:T(8,128)(2,1)S(1)}, bf16[4,64,16,128]{3,2,1,0:T(8,128)(2,1)S(1)}, u32[]{:S(2)}, u32[]{:S(2)}) collective-permute-start(bf16[4,64,16,128]{3,2,1,0:T(8,128)(2,1)S(1)} %pad_maximum_fusion), channel_id=1, source_target_pairs={{0,8},{8,0},{16,24},{24,16},{32,40},{40,32},{48,56},{56,48},{64,72... | collective-permute-start | bytes 3145736 | tf_op jit(solution)/shard_map/ppermute | solution.py:418
  47.8 12.5 %all-to-all-start.1 = ((bf16[8,8,16,128]{3,2,1,0:T(8,128)(2,1)}), bf16[8,8,16,128]{3,2,1,0:T(8,128)(2,1)S(1)}, u32[]{:S(2)}, u32[]{:S(2)}) async-start(bf16[8,8,16,128]{3,2,1,0:T(8,128)(2,1)} %forward_tiles.5), calls=%async_computation.1 | async-start | bytes 524288 | tf_op jit(solution)/shard_map/all_to_all | solution.py:450
  78.4 4.7 %collective-permute-start.10 = (bf16[4,8,128,128]{3,2,1,0:T(8,128)(2,1)S(1)}, bf16[4,8,128,128]{3,2,1,0:T(8,128)(2,1)S(1)}, u32[]{:S(2)}, u32[]{:S(2)}) collective-permute-start(bf16[4,8,128,128]{3,2,1,0:T(8,128)(2,1)S(1)} %backward_tiles.4), channel_id=1, source_target_pairs={{0,8},{8,0},{16,24},{24,16},{32,40},{40,32},{48,56},{56,48},{64,72... | collective-permute-start | bytes 3145736 | tf_op jit(solution)/shard_map/ppermute | solution.py:418
  78.6 4.6 %collective-permute-start.11 = (f32[64,128]{1,0:T(8,128)S(1)}, f32[64,128]{1,0:T(8,128)S(1)}, u32[]{:S(2)}, u32[]{:S(2)}) collective-permute-start(f32[64,128]{1,0:T(8,128)S(1)} %weight_sums.1), channel_id=1, source_target_pairs={{0,8},{8,0},{16,24},{24,16},{32,40},{40,32},{48,56},{56,48},{64,72... | collective-permute-start | bytes 98312 | tf_op jit(solution)/shard_map/ppermute | solution.py:418
  83.2 9.1 %collective-permute-start.12 = (bf16[4,8,128,128]{3,2,1,0:T(8,128)(2,1)S(1)}, bf16[4,8,128,128]{3,2,1,0:T(8,128)(2,1)S(1)}, u32[]{:S(2)}, u32[]{:S(2)}) collective-permute-start(bf16[4,8,128,128]{3,2,1,0:T(8,128)(2,1)S(1)} %backward_tiles.5), channel_id=1, source_target_pairs={{0,8},{8,0},{16,24},{24,16},{32,40},{40,32},{48,56},{56,48},{64,72... | collective-permute-start | bytes 3145736 | tf_op jit(solution)/shard_map/ppermute | solution.py:418
  87.4 13.3 %collective-permute-start.16 = (bf16[9,128,128]{2,1,0:T(8,128)(2,1)}, bf16[9,128,128]{2,1,0:T(8,128)(2,1)S(1)}, u32[]{:S(2)}, u32[]{:S(2)}) collective-permute-start(bf16[9,128,128]{2,1,0:T(8,128)(2,1)} %get-tuple-element.55), channel_id=1, source_target_pairs={{0,16},{8,24},{16,32},{24,40},{32,48},{40,56},{48,0},{56,8},{64,80... | collective-permute-start | bytes 884744 | tf_op jit(solution)/shard_map/ppermute | solution.py:418
  90.1 10.5 %collective-permute-start.17 = (bf16[9,128,128]{2,1,0:T(8,128)(2,1)S(1)}, bf16[9,128,128]{2,1,0:T(8,128)(2,1)S(1)}, u32[]{:S(2)}, u32[]{:S(2)}) collective-permute-start(bf16[9,128,128]{2,1,0:T(8,128)(2,1)S(1)} %get-tuple-element.64), channel_id=1, source_target_pairs={{0,48},{8,56},{16,0},{24,8},{32,16},{40,24},{48,32},{56,40},{64,11... | collective-permute-start | bytes 884744 | tf_op jit(solution)/shard_map/ppermute | solution.py:418
  90.7 14.4 %collective-permute-start.18 = (bf16[9,128,128]{2,1,0:T(8,128)(2,1)S(1)}, bf16[9,128,128]{2,1,0:T(8,128)(2,1)S(1)}, u32[]{:S(2)}, u32[]{:S(2)}) collective-permute-start(bf16[9,128,128]{2,1,0:T(8,128)(2,1)S(1)} %get-tuple-element.65), channel_id=1, source_target_pairs={{0,32},{8,40},{16,48},{24,56},{32,0},{40,8},{48,16},{56,24},{64,96... | collective-permute-start | bytes 884744 | tf_op jit(solution)/shard_map/ppermute | solution.py:418
  96.4 0.7 copy-start.5
  97.1 8.1 %copy-start.4 = (bf16[8,128,128]{2,1,0:T(8,128)(2,1)}, bf16[8,128,128]{2,1,0:T(8,128)(2,1)S(1)}, u32[]{:S(2)}) copy-start(bf16[8,128,128]{2,1,0:T(8,128)(2,1)S(1)} %get-tuple-element.62) | copy-start | bytes 786436
  97.1 14.5 %all-to-all-start.3 = ((bf16[8,8,32,128]{3,2,1,0:T(8,128)(2,1)}), bf16[8,8,32,128]{3,2,1,0:T(8,128)(2,1)S(1)}, u32[]{:S(2)}, u32[]{:S(2)}) async-start(bf16[8,8,32,128]{3,2,1,0:T(8,128)(2,1)} %get-tuple-element.58), calls=%async_computation.3 | async-start | bytes 1048576 | tf_op jit(solution)/shard_map/all_to_all | solution.py:487
  105.3 17.8 %collective-permute-start.19 = (bf16[9,128,128]{2,1,0:T(8,128)(2,1)S(1)}, bf16[9,128,128]{2,1,0:T(8,128)(2,1)S(1)}, u32[]{:S(2)}, u32[]{:S(2)}) collective-permute-start(bf16[9,128,128]{2,1,0:T(8,128)(2,1)S(1)} %cross.1.sent), channel_id=1, source_target_pairs={{0,64},{8,72},{16,80},{24,88},{32,96},{40,104},{48,112},{56,120},{... | collective-permute-start | bytes 884744 | tf_op jit(solution)/shard_map/ppermute | solution.py:418
  108.4 14.7 %collective-permute-start.13 = (bf16[8,128,128]{2,1,0:T(8,128)(2,1)}, bf16[8,128,128]{2,1,0:T(8,128)(2,1)S(1)}, u32[]{:S(2)}, u32[]{:S(2)}) collective-permute-start(bf16[8,128,128]{2,1,0:T(8,128)(2,1)} %copy-done.5), channel_id=1, source_target_pairs={{0,16},{8,24},{16,32},{24,40},{32,48},{40,56},{48,0},{56,8},{64,80... | collective-permute-start | bytes 786440 | tf_op jit(solution)/shard_map/ppermute | solution.py:418
  109.3 13.8 %collective-permute-start.14 = (bf16[8,128,128]{2,1,0:T(8,128)(2,1)S(1)}, bf16[8,128,128]{2,1,0:T(8,128)(2,1)S(1)}, u32[]{:S(2)}, u32[]{:S(2)}) collective-permute-start(bf16[8,128,128]{2,1,0:T(8,128)(2,1)S(1)} %get-tuple-element.61), channel_id=1, source_target_pairs={{0,48},{8,56},{16,0},{24,8},{32,16},{40,24},{48,32},{56,40},{64,11... | collective-permute-start | bytes 786440 | tf_op jit(solution)/shard_map/ppermute | solution.py:418
  111.6 11.4 %collective-permute-start.15 = (bf16[8,128,128]{2,1,0:T(8,128)(2,1)}, bf16[8,128,128]{2,1,0:T(8,128)(2,1)S(1)}, u32[]{:S(2)}, u32[]{:S(2)}) collective-permute-start(bf16[8,128,128]{2,1,0:T(8,128)(2,1)} %copy-done.4), channel_id=1, source_target_pairs={{0,32},{8,40},{16,48},{24,56},{32,0},{40,8},{48,16},{56,24},{64,96... | collective-permute-start | bytes 786440 | tf_op jit(solution)/shard_map/ppermute | solution.py:418

commit v5 on v4

--- a/solution.py
+++ b/solution.py
@@ -8,7 +8,7 @@
 from jax.sharding import PartitionSpec as P
 
 LANES = 128
-UNROLL, LOAD = 16, 8
+UNROLL, LOAD = 16, 16
 BF16 = jnp.bfloat16
 F32 = jnp.float32
 META_COUNTS, META_ME = 16, 17
@@ -474,7 +474,7 @@
     swapped = after(move(mine_too, 0, 0, 1), sums[1])
     parts = backward_call([(*hop, 0) for hop in ways], "keep", back, blocks, meta, own_tiles, swapped)
     arrived = [move(p, *hop, 0) for p, hop in zip(parts[1:], ways[1:])]
-    *crossing, _ = lax.optimization_barrier((*crossing, parts[1]))
+    *crossing, arrived[2] = lax.optimization_barrier((*crossing, arrived[2]))
     crossed = pl.pallas_call(
         cross_kernel,
         out_shape=jax.ShapeDtypeStruct(sums[0].shape, BF16),

time: 125 us -> 126 us (level)
  starting transfers between devices: 39.4 us -> 41.3 us
  waiting for transfers between devices: 28 us -> 26.5 us
    ppermute x20, starting transfers between devices: 25.7 us -> 27.4 us  [move(): return lax.ppermute(value, 'nodes', pairs)]
    ppermute x20, waiting for transfers between devices: 15 us -> 13.5 us  [move(): return lax.ppermute(value, 'nodes', pairs)]
    unnamed x12 -> x10, local copies, waits for them, and re-layouts: 3.29 us -> 3.3 us
  transfers between devices with their start and end apart: 23 -> 23, of which waited for: 4 -> 5; matrix products, arithmetic and copies ran while one was open for 2% -> 2% of each run, Pallas kernels for 20% -> 20%
where the time goes in v5:
time: 126 us
  starting transfers between devices  41.3 us (33%)
  Pallas kernels  39.2 us (31%)
  waiting for transfers between devices  26.5 us (21%)
  blocking collectives  11.9 us (9%)
  local copies, waits for them, and re-layouts  3.37 us (3%)
  other arithmetic  2.65 us (2%)
    ppermute x20, starting transfers between devices, move(): return lax.ppermute(value, 'nodes', pairs)  27.4 us
    pallas_call x4, Pallas kernels, backward_call(): pl.pallas_call(functools.partial(backward_kernel, hops, mode), out_shape=...  17 us
    pallas_call x3, Pallas kernels, forward_call(): pl.pallas_call(functools.partial(forward_kernel, hops, where, first, last...  13.6 us
    ppermute x20, waiting for transfers between devices, move(): return lax.ppermute(value, 'nodes', pairs)  13.5 us
    all_to_all x1, blocking collectives, on_device(): back = lax.all_to_all(back, 'feat', 0, 0)  11.9 us
    all_to_all x1, waiting for transfers between devices, on_device(): agg = lax.all_to_all(total, 'feat', 0, 0)  7.59 us
    all_to_all x1, waiting for transfers between devices, on_device(): received = lax.all_to_all(payload, 'feat', 0, 0)  5.35 us
    all_to_all x1, starting transfers between devices, on_device(): received = lax.all_to_all(payload, 'feat', 0, 0)  5.34 us
  transfers between devices with their start and end apart: 23, of which 5 were waited for; matrix products, arithmetic and copies ran while one was open for 2% of the time, Pallas kernels for 20%

profile of v5, /device:TPU:0, one launch (start us, length us, event | category | flops | bytes accessed | tf_op | source)
XLA Modules:
  0.0 125.7 jit_solution(10769866945389496987)
XLA Ops:
  0.6 1.7 %scale.1.refs_0_ = bf16[64,16,128]{2,1,0:T(8,128)(2,1)} custom-call(bf16[16,8192]{1,0:T(8,128)(2,1)} %bitcast.39, f32[64,128]{1,0:T(8,128)} %bitcast.26), custom_call_target="tpu_custom_call" | custom-call | tf_op jit(solution)/shard_map/scale/pallas_call | solution.py:420
  2.3 3.1 %collective-permute-start = (bf16[64,16,128]{2,1,0:T(8,128)(2,1)}, bf16[64,16,128]{2,1,0:T(8,128)(2,1)S(1)}, u32[]{:S(2)}, u32[]{:S(2)}) collective-permute-start(bf16[64,16,128]{2,1,0:T(8,128)(2,1)} %scale.1.refs_0_), channel_id=1, source_target_pairs={{0,64},{8,72},{16,80},{24,88},{32,96},{40,104},{48,112},{56,120},{... | collective-permute-start | bytes 786440 | tf_op jit(solution)/shard_map/ppermute | solution.py:418
  5.4 1.6 %collective-permute-start.1 = (bf16[64,16,128]{2,1,0:T(8,128)(2,1)}, bf16[64,16,128]{2,1,0:T(8,128)(2,1)S(1)}, u32[]{:S(2)}, u32[]{:S(2)}) collective-permute-start(bf16[64,16,128]{2,1,0:T(8,128)(2,1)} %scale.1.refs_0_), channel_id=1, source_target_pairs={{0,16},{8,24},{16,32},{24,40},{32,48},{40,56},{48,0},{56,8},{64,80... | collective-permute-start | bytes 786440 | tf_op jit(solution)/shard_map/ppermute | solution.py:418
  7.0 1.7 %collective-permute-start.2 = (bf16[64,16,128]{2,1,0:T(8,128)(2,1)}, bf16[64,16,128]{2,1,0:T(8,128)(2,1)S(1)}, u32[]{:S(2)}, u32[]{:S(2)}) collective-permute-start(bf16[64,16,128]{2,1,0:T(8,128)(2,1)} %scale.1.refs_0_), channel_id=1, source_target_pairs={{0,48},{8,56},{16,0},{24,8},{32,16},{40,24},{48,32},{56,40},{64,11... | collective-permute-start | bytes 786440 | tf_op jit(solution)/shard_map/ppermute | solution.py:418
  8.7 2.1 %payload.1 = bf16[8,10,32,128]{3,2,1,0:T(8,128)(2,1)} custom-call(bf16[32,8192]{1,0:T(8,128)(2,1)} %bitcast.37, bf16[16,256]{1,0:T(8,128)(2,1)} %weight.1, f32[1,32]{1,0:T(1,128)} %bitcast.40), custom_call_target="tpu_custom_call" | custom-call | tf_op jit(solution)/shard_map/payload/pallas_call | solution.py:425
  10.7 5.3 %all-to-all-start = ((bf16[8,10,32,128]{3,2,1,0:T(8,128)(2,1)}), bf16[8,10,32,128]{3,2,1,0:T(8,128)(2,1)S(1)}, u32[]{:S(2)}, u32[]{:S(2)}) async-start(bf16[8,10,32,128]{3,2,1,0:T(8,128)(2,1)} %payload.1), calls=%async_computation | async-start | bytes 1310720 | tf_op jit(solution)/shard_map/all_to_all | solution.py:435
  16.1 1.0 pad_maximum_fusion.1
  18.0 2.9 %collective-permute-start.4 = (bf16[64,16,128]{2,1,0:T(8,128)(2,1)S(1)}, bf16[64,16,128]{2,1,0:T(8,128)(2,1)S(1)}, u32[]{:S(2)}, u32[]{:S(2)}) collective-permute-start(bf16[64,16,128]{2,1,0:T(8,128)(2,1)S(1)} %collective-permute-done.refs_2_), channel_id=1, source_target_pairs={{0,48},{8,56},{16,0},{24,8},{32,16},{40,24},{48,32},{56,40},{64,11... | collective-permute-start | bytes 786440 | tf_op jit(solution)/shard_map/ppermute | solution.py:418
  20.8 5.4 %all-to-all-done.received = bf16[8,10,32,128]{3,2,1,0:T(8,128)(2,1)S(1)} async-done(((bf16[8,10,32,128]{3,2,1,0:T(8,128)(2,1)}), bf16[8,10,32,128]{3,2,1,0:T(8,128)(2,1)S(1)}, u32[]{:S(2)}, u32[]{:S(2)}) %all-to-all-start) | async-done | bytes 655392 | tf_op jit(solution)/shard_map/all_to_all | solution.py:435
  26.2 1.9 %collective-permute-start.5 = (bf16[64,16,128]{2,1,0:T(8,128)(2,1)}, bf16[64,16,128]{2,1,0:T(8,128)(2,1)S(1)}, u32[]{:S(2)}, u32[]{:S(2)}) collective-permute-start(bf16[64,16,128]{2,1,0:T(8,128)(2,1)} %scale.1.refs_0_), channel_id=1, source_target_pairs={{0,32},{8,40},{16,48},{24,56},{32,0},{40,8},{48,16},{56,24},{64,96... | collective-permute-start | bytes 786440 | tf_op jit(solution)/shard_map/ppermute | solution.py:418
  28.8 1.6 %collective-permute-start.6 = (bf16[64,16,128]{2,1,0:T(8,128)(2,1)S(1)}, bf16[64,16,128]{2,1,0:T(8,128)(2,1)S(1)}, u32[]{:S(2)}, u32[]{:S(2)}) collective-permute-start(bf16[64,16,128]{2,1,0:T(8,128)(2,1)S(1)} %collective-permute-done.refs_2_), channel_id=1, source_target_pairs={{0,32},{8,40},{16,48},{24,56},{32,0},{40,8},{48,16},{56,24},{64,96... | collective-permute-start | bytes 786440 | tf_op jit(solution)/shard_map/ppermute | solution.py:418
  33.9 5.7 %forward_tiles.3.refs_5_ = f32[64,16,128]{2,1,0:T(8,128)S(1)} custom-call(s32[18,32]{1,0:T(8,128)S(1)} %add_add_fusion.meta, bf16[64,16,128]{2,1,0:T(8,128)(2,1)S(1)} %copy-done, bf16[64,16,128]{2,1,0:T(8,128)(2,1)S(1)} %copy-done.3, bf16[64,16,128]{2,1,0:T(8,128)(2,1)S(1)} %collective-permute-done.refs_2_, ...), custom_call_target="tpu_custom_call" | custom-call | flops 67108864 | bytes 8388608 | tf_op jit(solution)/shard_map/forward_tiles/pallas_call | solution.py:171
  39.9 3.5 %forward_tiles.4.refs_2_ = f32[64,16,128]{2,1,0:T(8,128)S(1)} custom-call(s32[18,32]{1,0:T(8,128)S(1)} %add_add_fusion.meta, bf16[64,16,128]{2,1,0:T(8,128)(2,1)S(1)} %collective-permute-done.3.refs_0_, bf16[64,16,128]{2,1,0:T(8,128)(2,1)S(1)} %collective-permute-done.4.refs_1_, bf16[64,16,128]{2,1,0:T(8,128)(2,1)S(1)} %collective-permute-done.5.refs_2_, ...), custom_call_target="tpu_custom_call" | custom-call | flops 33554432 | bytes 4194304 | tf_op jit(solution)/shard_map/forward_tiles/pallas_call | solution.py:171
  43.4 4.5 %forward_tiles.5 = bf16[8,8,16,128]{3,2,1,0:T(8,128)(2,1)} custom-call(s32[18,32]{1,0:T(8,128)S(1)} %add_add_fusion.meta, bf16[4,64,16,128]{3,2,1,0:T(8,128)(2,1)S(1)} %collective-permute-done.9.refs_0_, bf16[16,32,128,128]{3,2,1,0:T(8,128)(2,1)} %bitcast.32, f32[64,16,128]{2,1,0:T(8,128)S(1)} %forward_tiles.4.refs_2_, f32[64,128]{1,0:T(8,128)S(1)} %bitcast.27), custom_call_target="tpu_custom_call" | custom-call | flops 33554432 | bytes 4194304 | tf_op jit(solution)/shard_map/forward_tiles/pallas_call | solution.py:171
  47.9 5.0 %all-to-all-start.1 = ((bf16[8,8,16,128]{3,2,1,0:T(8,128)(2,1)}), bf16[8,8,16,128]{3,2,1,0:T(8,128)(2,1)S(1)}, u32[]{:S(2)}, u32[]{:S(2)}) async-start(bf16[8,8,16,128]{3,2,1,0:T(8,128)(2,1)} %forward_tiles.5), calls=%async_computation.1 | async-start | bytes 524288 | tf_op jit(solution)/shard_map/all_to_all | solution.py:450
  52.9 7.6 %all-to-all-done.1.agg = bf16[8,8,16,128]{3,2,1,0:T(8,128)(2,1)S(1)} async-done(((bf16[8,8,16,128]{3,2,1,0:T(8,128)(2,1)}), bf16[8,8,16,128]{3,2,1,0:T(8,128)(2,1)S(1)}, u32[]{:S(2)}, u32[]{:S(2)}) %all-to-all-start.1) | async-done | bytes 262176 | tf_op jit(solution)/shard_map/all_to_all | solution.py:450
  60.5 2.3 %dense.1 = (bf16[8,14,16,128]{3,2,1,0:T(8,128)(2,1)S(1)}, bf16[8,8,32,128]{3,2,1,0:T(8,128)(2,1)}) custom-call(s32[1]{0:T(128)} %bitcast.place, bf16[8,8,16,128]{3,2,1,0:T(8,128)(2,1)S(1)} %all-to-all-done.1.agg, bf16[8,10,32,128]{3,2,1,0:T(8,128)(2,1)S(1)} %all-to-all-done.received, f32[64,128]{1,0:T(8,128)S(1)} %bitcast.28), custom_call_target="tpu_custom_call" | custom-call | tf_op jit(solution)/shard_map/dense/pallas_call | solution.py:451
  62.8 11.9 %all_to_all.20.refs_0_.back = bf16[8,14,16,128]{3,2,1,0:T(8,128)(2,1)S(1)} all-to-all(bf16[8,14,16,128]{3,2,1,0:T(8,128)(2,1)S(1)} %get-tuple-element.51), channel_id=1, replica_groups=mesh['nodes'=16,'feat'=8] {'feat'}, dimensions={0} | all-to-all | bytes 917504 | tf_op jit(solution)/shard_map/all_to_all | solution.py:460
  74.7 4.3 %backward_tiles.4 = bf16[4,8,128,128]{3,2,1,0:T(8,128)(2,1)S(1)} custom-call(s32[18,32]{1,0:T(8,128)S(1)} %add_add_fusion.meta, bf16[8,14,16,128]{3,2,1,0:T(8,128)(2,1)S(1)} %all_to_all.20.refs_0_.back, bf16[16,32,128,128]{3,2,1,0:T(8,128)(2,1)} %bitcast.33), custom_call_target="tpu_custom_call" | custom-call | flops 33554432 | bytes 4194304 | tf_op jit(solution)/shard_map/backward_tiles/pallas_call | solution.py:286
  79.7 4.0 %backward_tiles.5 = bf16[4,8,128,128]{3,2,1,0:T(8,128)(2,1)S(1)} custom-call(s32[18,32]{1,0:T(8,128)S(1)} %add_add_fusion.meta, bf16[8,14,16,128]{3,2,1,0:T(8,128)(2,1)S(1)} %all_to_all.20.refs_0_.back, bf16[16,32,128,128]{3,2,1,0:T(8,128)(2,1)} %bitcast.34), custom_call_target="tpu_custom_call" | custom-call | flops 33554432 | bytes 4194304 | tf_op jit(solution)/shard_map/backward_tiles/pallas_call | solution.py:286
  84.3 4.0 %backward_tiles.6 = (bf16[9,128,128]{2,1,0:T(8,128)(2,1)S(1)}, bf16[9,128,128]{2,1,0:T(8,128)(2,1)}, bf16[9,128,128]{2,1,0:T(8,128)(2,1)S(1)}, bf16[9,128,128]{2,1,0:T(8,128)(2,1)S(1)}) custom-call(s32[18,32]{1,0:T(8,128)S(1)} %add_add_fusion.meta, bf16[8,14,16,128]{3,2,1,0:T(8,128)(2,1)S(1)} %all_to_all.20.refs_0_.back, ...), custom_call_target="tpu_custom_call" | custom-call | flops 33554432 | bytes 4194304 | tf_op jit(solution)/shard_map/backward_tiles/pallas_call | solution.py:286
  88.4 3.5 %collective-permute-start.16 = (bf16[9,128,128]{2,1,0:T(8,128)(2,1)S(1)}, bf16[9,128,128]{2,1,0:T(8,128)(2,1)S(1)}, u32[]{:S(2)}, u32[]{:S(2)}) collective-permute-start(bf16[9,128,128]{2,1,0:T(8,128)(2,1)S(1)} %get-tuple-element.63), channel_id=1, source_target_pairs={{0,48},{8,56},{16,0},{24,8},{32,16},{40,24},{48,32},{56,40},{64,11... | collective-permute-start | bytes 884744 | tf_op jit(solution)/shard_map/ppermute | solution.py:418
  91.9 1.4 %collective-permute-start.17 = (bf16[9,128,128]{2,1,0:T(8,128)(2,1)S(1)}, bf16[9,128,128]{2,1,0:T(8,128)(2,1)S(1)}, u32[]{:S(2)}, u32[]{:S(2)}) collective-permute-start(bf16[9,128,128]{2,1,0:T(8,128)(2,1)S(1)} %get-tuple-element.64), channel_id=1, source_target_pairs={{0,32},{8,40},{16,48},{24,56},{32,0},{40,8},{48,16},{56,24},{64,96... | collective-permute-start | bytes 884744 | tf_op jit(solution)/shard_map/ppermute | solution.py:418
  93.3 4.8 %backward_tiles.7 = (f32[64,16,128]{2,1,0:T(8,128)S(1)}, bf16[8,128,128]{2,1,0:T(8,128)(2,1)S(1)}, bf16[8,128,128]{2,1,0:T(8,128)(2,1)S(1)}, bf16[8,128,128]{2,1,0:T(8,128)(2,1)}) custom-call(s32[18,32]{1,0:T(8,128)S(1)} %add_add_fusion.meta, bf16[8,14,16,128]{3,2,1,0:T(8,128)(2,1)S(1)} %all_to_all.20.refs_0_.back, bf16[16,32,128,128]{3,2,1,0:T(8,128)(2,1)} %bitcast.36, ...), custom_call_target="tpu_custom_call" | custom-call | flops 33554432 | bytes 4194304 | tf_op jit(solution)/shard_map/backward_tiles/pallas_call | solution.py:286
  98.8 2.2 %collective-permute-start.18 = (bf16[8,128,128]{2,1,0:T(8,128)(2,1)}, bf16[8,128,128]{2,1,0:T(8,128)(2,1)S(1)}, u32[]{:S(2)}, u32[]{:S(2)}) collective-permute-start(bf16[8,128,128]{2,1,0:T(8,128)(2,1)} %get-tuple-element.65), channel_id=1, source_target_pairs={{0,32},{8,40},{16,48},{24,56},{32,0},{40,8},{48,16},{56,24},{64,96... | collective-permute-start | bytes 786440 | tf_op jit(solution)/shard_map/ppermute | solution.py:418
  100.9 3.5 %all-to-all-start.3 = ((bf16[8,8,32,128]{3,2,1,0:T(8,128)(2,1)}), bf16[8,8,32,128]{3,2,1,0:T(8,128)(2,1)S(1)}, u32[]{:S(2)}, u32[]{:S(2)}) async-start(bf16[8,8,32,128]{3,2,1,0:T(8,128)(2,1)} %get-tuple-element.59), calls=%async_computation.3 | async-start | bytes 1048576 | tf_op jit(solution)/shard_map/all_to_all | solution.py:487
  104.4 6.1 %collective-permute-done.16.up = bf16[9,128,128]{2,1,0:T(8,128)(2,1)S(1)} collective-permute-done((bf16[9,128,128]{2,1,0:T(8,128)(2,1)S(1)}, bf16[9,128,128]{2,1,0:T(8,128)(2,1)S(1)}, u32[]{:S(2)}, u32[]{:S(2)}) %collective-permute-start.16) | collective-permute-done | bytes 294944 | tf_op jit(solution)/shard_map/ppermute | solution.py:418
  110.5 2.0 %collective-permute-done.18.far = bf16[8,128,128]{2,1,0:T(8,128)(2,1)S(1)} collective-permute-done((bf16[8,128,128]{2,1,0:T(8,128)(2,1)}, bf16[8,128,128]{2,1,0:T(8,128)(2,1)S(1)}, u32[]{:S(2)}, u32[]{:S(2)}) %collective-permute-start.18) | collective-permute-done | bytes 262176 | tf_op jit(solution)/shard_map/ppermute | solution.py:418
  112.7 2.1 %collective-permute-start.19 = (bf16[9,128,128]{2,1,0:T(8,128)(2,1)S(1)}, bf16[9,128,128]{2,1,0:T(8,128)(2,1)S(1)}, u32[]{:S(2)}, u32[]{:S(2)}) collective-permute-start(bf16[9,128,128]{2,1,0:T(8,128)(2,1)S(1)} %cross.1.sent), channel_id=1, source_target_pairs={{0,64},{8,72},{16,80},{24,88},{32,96},{40,104},{48,112},{56,120},{... | collective-permute-start | bytes 884744 | tf_op jit(solution)/shard_map/ppermute | solution.py:418
  115.5 2.5 %collective-permute-start.14 = (bf16[8,128,128]{2,1,0:T(8,128)(2,1)S(1)}, bf16[8,128,128]{2,1,0:T(8,128)(2,1)S(1)}, u32[]{:S(2)}, u32[]{:S(2)}) collective-permute-start(bf16[8,128,128]{2,1,0:T(8,128)(2,1)S(1)} %get-tuple-element.62), channel_id=1, source_target_pairs={{0,48},{8,56},{16,0},{24,8},{32,16},{40,24},{48,32},{56,40},{64,11... | collective-permute-start | bytes 786440 | tf_op jit(solution)/shard_map/ppermute | solution.py:418
  118.9 5.4 %collective-permute-done.13.down = bf16[8,128,128]{2,1,0:T(8,128)(2,1)S(1)} collective-permute-done((bf16[8,128,128]{2,1,0:T(8,128)(2,1)}, bf16[8,128,128]{2,1,0:T(8,128)(2,1)S(1)}, u32[]{:S(2)}, u32[]{:S(2)}) %collective-permute-start.13) | collective-permute-done | bytes 262176 | tf_op jit(solution)/shard_map/ppermute | solution.py:418
  124.3 1.4 %finish.1 = (f32[16,8192]{1,0:T(8,128)}, f32[16,256]{1,0:T(8,128)}, f32[1,32]{1,0:T(1,128)}) custom-call(s32[1]{0:T(128)} %bitcast.place, f32[64,16,128]{2,1,0:T(8,128)S(1)} %get-tuple-element.61.kept, f32[64,128]{1,0:T(8,128)S(1)} %bitcast.29, bf16[8,128,128]{2,1,0:T(8,128)(2,1)S(1)} %collective-permute-done.13.down, ...), custom_call_target="tpu_custom_call" | custom-call | tf_op jit(solution)/shard_map/finish/pallas_call | solution.py:489
  (45 shorter events, 9.2 us)
Async XLA Ops:
  2.3 13.7 %collective-permute-start = (bf16[64,16,128]{2,1,0:T(8,128)(2,1)}, bf16[64,16,128]{2,1,0:T(8,128)(2,1)S(1)}, u32[]{:S(2)}, u32[]{:S(2)}) collective-permute-start(bf16[64,16,128]{2,1,0:T(8,128)(2,1)} %scale.1.refs_0_), channel_id=1, source_target_pairs={{0,64},{8,72},{16,80},{24,88},{32,96},{40,104},{48,112},{56,120},{... | collective-permute-start | bytes 786440 | tf_op jit(solution)/shard_map/ppermute | solution.py:418
  5.4 10.6 %collective-permute-start.1 = (bf16[64,16,128]{2,1,0:T(8,128)(2,1)}, bf16[64,16,128]{2,1,0:T(8,128)(2,1)S(1)}, u32[]{:S(2)}, u32[]{:S(2)}) collective-permute-start(bf16[64,16,128]{2,1,0:T(8,128)(2,1)} %scale.1.refs_0_), channel_id=1, source_target_pairs={{0,16},{8,24},{16,32},{24,40},{32,48},{40,56},{48,0},{56,8},{64,80... | collective-permute-start | bytes 786440 | tf_op jit(solution)/shard_map/ppermute | solution.py:418
  7.0 9.1 %collective-permute-start.2 = (bf16[64,16,128]{2,1,0:T(8,128)(2,1)}, bf16[64,16,128]{2,1,0:T(8,128)(2,1)S(1)}, u32[]{:S(2)}, u32[]{:S(2)}) collective-permute-start(bf16[64,16,128]{2,1,0:T(8,128)(2,1)} %scale.1.refs_0_), channel_id=1, source_target_pairs={{0,48},{8,56},{16,0},{24,8},{32,16},{40,24},{48,32},{56,40},{64,11... | collective-permute-start | bytes 786440 | tf_op jit(solution)/shard_map/ppermute | solution.py:418
  10.7 15.5 %all-to-all-start = ((bf16[8,10,32,128]{3,2,1,0:T(8,128)(2,1)}), bf16[8,10,32,128]{3,2,1,0:T(8,128)(2,1)S(1)}, u32[]{:S(2)}, u32[]{:S(2)}) async-start(bf16[8,10,32,128]{3,2,1,0:T(8,128)(2,1)} %payload.1), calls=%async_computation | async-start | bytes 1310720 | tf_op jit(solution)/shard_map/all_to_all | solution.py:435
  17.1 14.9 %collective-permute-start.8 = (bf16[3,64,16,128]{3,2,1,0:T(8,128)(2,1)}, bf16[3,64,16,128]{3,2,1,0:T(8,128)(2,1)S(1)}, u32[]{:S(2)}, u32[]{:S(2)}) collective-permute-start(bf16[3,64,16,128]{3,2,1,0:T(8,128)(2,1)} %pad_maximum_fusion.1), channel_id=1, source_target_pairs={{0,8},{8,0},{16,24},{24,16},{32,40},{40,32},{48,56},{56,48},{64,72... | collective-permute-start | bytes 2359304 | tf_op jit(solution)/shard_map/ppermute | solution.py:418
  17.1 11.0 %collective-permute-start.7 = (bf16[64,16,128]{2,1,0:T(8,128)(2,1)}, bf16[64,16,128]{2,1,0:T(8,128)(2,1)S(1)}, u32[]{:S(2)}, u32[]{:S(2)}) collective-permute-start(bf16[64,16,128]{2,1,0:T(8,128)(2,1)} %scale.1.refs_0_), channel_id=1, source_target_pairs={{0,8},{8,0},{16,24},{24,16},{32,40},{40,32},{48,56},{56,48},{64,72... | collective-permute-start | bytes 786440 | tf_op jit(solution)/shard_map/ppermute | solution.py:418
  17.6 22.0 %collective-permute-start.3 = (bf16[64,16,128]{2,1,0:T(8,128)(2,1)S(1)}, bf16[64,16,128]{2,1,0:T(8,128)(2,1)S(1)}, u32[]{:S(2)}, u32[]{:S(2)}) collective-permute-start(bf16[64,16,128]{2,1,0:T(8,128)(2,1)S(1)} %collective-permute-done.refs_2_), channel_id=1, source_target_pairs={{0,16},{8,24},{16,32},{24,40},{32,48},{40,56},{48,0},{56,8},{64,80... | collective-permute-start | bytes 786440 | tf_op jit(solution)/shard_map/ppermute | solution.py:418
  18.0 21.6 %collective-permute-start.4 = (bf16[64,16,128]{2,1,0:T(8,128)(2,1)S(1)}, bf16[64,16,128]{2,1,0:T(8,128)(2,1)S(1)}, u32[]{:S(2)}, u32[]{:S(2)}) collective-permute-start(bf16[64,16,128]{2,1,0:T(8,128)(2,1)S(1)} %collective-permute-done.refs_2_), channel_id=1, source_target_pairs={{0,48},{8,56},{16,0},{24,8},{32,16},{40,24},{48,32},{56,40},{64,11... | collective-permute-start | bytes 786440 | tf_op jit(solution)/shard_map/ppermute | solution.py:418
  26.2 13.4 %collective-permute-start.5 = (bf16[64,16,128]{2,1,0:T(8,128)(2,1)}, bf16[64,16,128]{2,1,0:T(8,128)(2,1)S(1)}, u32[]{:S(2)}, u32[]{:S(2)}) collective-permute-start(bf16[64,16,128]{2,1,0:T(8,128)(2,1)} %scale.1.refs_0_), channel_id=1, source_target_pairs={{0,32},{8,40},{16,48},{24,56},{32,0},{40,8},{48,16},{56,24},{64,96... | collective-permute-start | bytes 786440 | tf_op jit(solution)/shard_map/ppermute | solution.py:418
  28.1 0.7 copy-start.2
  28.8 10.8 %collective-permute-start.6 = (bf16[64,16,128]{2,1,0:T(8,128)(2,1)S(1)}, bf16[64,16,128]{2,1,0:T(8,128)(2,1)S(1)}, u32[]{:S(2)}, u32[]{:S(2)}) collective-permute-start(bf16[64,16,128]{2,1,0:T(8,128)(2,1)S(1)} %collective-permute-done.refs_2_), channel_id=1, source_target_pairs={{0,32},{8,40},{16,48},{24,56},{32,0},{40,8},{48,16},{56,24},{64,96... | collective-permute-start | bytes 786440 | tf_op jit(solution)/shard_map/ppermute | solution.py:418
  32.0 1.0 copy-start
  33.0 0.9 copy-start.3
  33.9 9.5 %copy-start.1 = (f32[8192]{0:T(1024)S(1)}, f32[8192]{0:T(1024)}, u32[]{:S(2)}) copy-start(f32[8192]{0:T(1024)} %param.14) | copy-start | bytes 98308
  39.8 3.6 %collective-permute-start.9 = (bf16[4,64,16,128]{3,2,1,0:T(8,128)(2,1)S(1)}, bf16[4,64,16,128]{3,2,1,0:T(8,128)(2,1)S(1)}, u32[]{:S(2)}, u32[]{:S(2)}) collective-permute-start(bf16[4,64,16,128]{3,2,1,0:T(8,128)(2,1)S(1)} %pad_maximum_fusion), channel_id=1, source_target_pairs={{0,8},{8,0},{16,24},{24,16},{32,40},{40,32},{48,56},{56,48},{64,72... | collective-permute-start | bytes 3145736 | tf_op jit(solution)/shard_map/ppermute | solution.py:418
  47.9 12.6 %all-to-all-start.1 = ((bf16[8,8,16,128]{3,2,1,0:T(8,128)(2,1)}), bf16[8,8,16,128]{3,2,1,0:T(8,128)(2,1)S(1)}, u32[]{:S(2)}, u32[]{:S(2)}) async-start(bf16[8,8,16,128]{3,2,1,0:T(8,128)(2,1)} %forward_tiles.5), calls=%async_computation.1 | async-start | bytes 524288 | tf_op jit(solution)/shard_map/all_to_all | solution.py:450
  79.0 4.7 %collective-permute-start.10 = (bf16[4,8,128,128]{3,2,1,0:T(8,128)(2,1)S(1)}, bf16[4,8,128,128]{3,2,1,0:T(8,128)(2,1)S(1)}, u32[]{:S(2)}, u32[]{:S(2)}) collective-permute-start(bf16[4,8,128,128]{3,2,1,0:T(8,128)(2,1)S(1)} %backward_tiles.4), channel_id=1, source_target_pairs={{0,8},{8,0},{16,24},{24,16},{32,40},{40,32},{48,56},{56,48},{64,72... | collective-permute-start | bytes 3145736 | tf_op jit(solution)/shard_map/ppermute | solution.py:418
  79.1 4.5 %collective-permute-start.11 = (f32[64,128]{1,0:T(8,128)S(1)}, f32[64,128]{1,0:T(8,128)S(1)}, u32[]{:S(2)}, u32[]{:S(2)}) collective-permute-start(f32[64,128]{1,0:T(8,128)S(1)} %weight_sums.1), channel_id=1, source_target_pairs={{0,8},{8,0},{16,24},{24,16},{32,40},{40,32},{48,56},{56,48},{64,72... | collective-permute-start | bytes 98312 | tf_op jit(solution)/shard_map/ppermute | solution.py:418
  83.7 9.6 %collective-permute-start.12 = (bf16[4,8,128,128]{3,2,1,0:T(8,128)(2,1)S(1)}, bf16[4,8,128,128]{3,2,1,0:T(8,128)(2,1)S(1)}, u32[]{:S(2)}, u32[]{:S(2)}) collective-permute-start(bf16[4,8,128,128]{3,2,1,0:T(8,128)(2,1)S(1)} %backward_tiles.5), channel_id=1, source_target_pairs={{0,8},{8,0},{16,24},{24,16},{32,40},{40,32},{48,56},{56,48},{64,72... | collective-permute-start | bytes 3145736 | tf_op jit(solution)/shard_map/ppermute | solution.py:418
  88.3 16.1 %collective-permute-start.15 = (bf16[9,128,128]{2,1,0:T(8,128)(2,1)}, bf16[9,128,128]{2,1,0:T(8,128)(2,1)S(1)}, u32[]{:S(2)}, u32[]{:S(2)}) collective-permute-start(bf16[9,128,128]{2,1,0:T(8,128)(2,1)} %get-tuple-element.56), channel_id=1, source_target_pairs={{0,16},{8,24},{16,32},{24,40},{32,48},{40,56},{48,0},{56,8},{64,80... | collective-permute-start | bytes 884744 | tf_op jit(solution)/shard_map/ppermute | solution.py:418
  88.4 22.1 %collective-permute-start.16 = (bf16[9,128,128]{2,1,0:T(8,128)(2,1)S(1)}, bf16[9,128,128]{2,1,0:T(8,128)(2,1)S(1)}, u32[]{:S(2)}, u32[]{:S(2)}) collective-permute-start(bf16[9,128,128]{2,1,0:T(8,128)(2,1)S(1)} %get-tuple-element.63), channel_id=1, source_target_pairs={{0,48},{8,56},{16,0},{24,8},{32,16},{40,24},{48,32},{56,40},{64,11... | collective-permute-start | bytes 884744 | tf_op jit(solution)/shard_map/ppermute | solution.py:418
  91.9 18.6 %collective-permute-start.17 = (bf16[9,128,128]{2,1,0:T(8,128)(2,1)S(1)}, bf16[9,128,128]{2,1,0:T(8,128)(2,1)S(1)}, u32[]{:S(2)}, u32[]{:S(2)}) collective-permute-start(bf16[9,128,128]{2,1,0:T(8,128)(2,1)S(1)} %get-tuple-element.64), channel_id=1, source_target_pairs={{0,32},{8,40},{16,48},{24,56},{32,0},{40,8},{48,16},{56,24},{64,96... | collective-permute-start | bytes 884744 | tf_op jit(solution)/shard_map/ppermute | solution.py:418
  98.1 0.7 copy-start.4
  98.8 13.8 %collective-permute-start.18 = (bf16[8,128,128]{2,1,0:T(8,128)(2,1)}, bf16[8,128,128]{2,1,0:T(8,128)(2,1)S(1)}, u32[]{:S(2)}, u32[]{:S(2)}) collective-permute-start(bf16[8,128,128]{2,1,0:T(8,128)(2,1)} %get-tuple-element.65), channel_id=1, source_target_pairs={{0,32},{8,40},{16,48},{24,56},{32,0},{40,8},{48,16},{56,24},{64,96... | collective-permute-start | bytes 786440 | tf_op jit(solution)/shard_map/ppermute | solution.py:418
  100.9 17.1 %all-to-all-start.3 = ((bf16[8,8,32,128]{3,2,1,0:T(8,128)(2,1)}), bf16[8,8,32,128]{3,2,1,0:T(8,128)(2,1)S(1)}, u32[]{:S(2)}, u32[]{:S(2)}) async-start(bf16[8,8,32,128]{3,2,1,0:T(8,128)(2,1)} %get-tuple-element.59), calls=%async_computation.3 | async-start | bytes 1048576 | tf_op jit(solution)/shard_map/all_to_all | solution.py:487
  112.7 11.6 %collective-permute-start.19 = (bf16[9,128,128]{2,1,0:T(8,128)(2,1)S(1)}, bf16[9,128,128]{2,1,0:T(8,128)(2,1)S(1)}, u32[]{:S(2)}, u32[]{:S(2)}) collective-permute-start(bf16[9,128,128]{2,1,0:T(8,128)(2,1)S(1)} %cross.1.sent), channel_id=1, source_target_pairs={{0,64},{8,72},{16,80},{24,88},{32,96},{40,104},{48,112},{56,120},{... | collective-permute-start | bytes 884744 | tf_op jit(solution)/shard_map/ppermute | solution.py:418
  114.8 9.5 %collective-permute-start.13 = (bf16[8,128,128]{2,1,0:T(8,128)(2,1)}, bf16[8,128,128]{2,1,0:T(8,128)(2,1)S(1)}, u32[]{:S(2)}, u32[]{:S(2)}) collective-permute-start(bf16[8,128,128]{2,1,0:T(8,128)(2,1)} %copy-done.4), channel_id=1, source_target_pairs={{0,16},{8,24},{16,32},{24,40},{32,48},{40,56},{48,0},{56,8},{64,80... | collective-permute-start | bytes 786440 | tf_op jit(solution)/shard_map/ppermute | solution.py:418
  115.5 8.8 %collective-permute-start.14 = (bf16[8,128,128]{2,1,0:T(8,128)(2,1)S(1)}, bf16[8,128,128]{2,1,0:T(8,128)(2,1)S(1)}, u32[]{:S(2)}, u32[]{:S(2)}) collective-permute-start(bf16[8,128,128]{2,1,0:T(8,128)(2,1)S(1)} %get-tuple-element.62), channel_id=1, source_target_pairs={{0,48},{8,56},{16,0},{24,8},{32,16},{40,24},{48,32},{56,40},{64,11... | collective-permute-start | bytes 786440 | tf_op jit(solution)/shard_map/ppermute | solution.py:418

commit v6 on v5

--- a/solution.py
+++ b/solution.py
@@ -455,7 +455,7 @@
             jax.ShapeDtypeStruct((peers, per_peer, hid_local, LANES), BF16),
         ),
         in_specs=[spec(SMEM), spec(VMEM), spec(VMEM), spec(VMEM)],
-        compiler_params=params(), name="dense",
+        compiler_params=params(48), name="dense",
     )(place, agg, received, norm_blocks)
     back = lax.all_to_all(back, "feat", 0, 0)
 
@@ -483,7 +483,7 @@
     hidden = pl.pallas_call(
         collect_kernel,
         out_shape=jax.ShapeDtypeStruct((hid_local, rows), BF16),
-        compiler_params=params(), name="collect",
+        compiler_params=params(48), name="collect",
     )(lax.all_to_all(after(sent, parts[1]), "feat", 0, 0))
     came = move(crossed, 1, 0, 0)
     grad_feats, grad_weight, grad_bias = pl.pallas_call(

time: 126 us -> 125 us (level)
  waiting for transfers between devices: 26.5 us -> 25.2 us
    ppermute x20, waiting for transfers between devices: 13.5 us -> 11.9 us  [move(): return lax.ppermute(value, 'nodes', pairs)]
  transfers between devices with their start and end apart: 23 -> 23, of which waited for: 5 -> 4; matrix products, arithmetic and copies ran while one was open for 2% -> 2% of each run, Pallas kernels for 20% -> 21%
where the time goes in v6:
time: 125 us
  starting transfers between devices  40.9 us (33%)
  Pallas kernels  39.7 us (32%)
  waiting for transfers between devices  25.2 us (20%)
  blocking collectives  12.4 us (10%)
  local copies, waits for them, and re-layouts  3.37 us (3%)
  other arithmetic  2.66 us (2%)
    ppermute x20, starting transfers between devices, move(): return lax.ppermute(value, 'nodes', pairs)  27.3 us
    pallas_call x4, Pallas kernels, backward_call(): pl.pallas_call(functools.partial(backward_kernel, hops, mode), out_shape=...  17.3 us
    pallas_call x3, Pallas kernels, forward_call(): pl.pallas_call(functools.partial(forward_kernel, hops, where, first, last...  13.9 us
    all_to_all x1, blocking collectives, on_device(): back = lax.all_to_all(back, 'feat', 0, 0)  12.4 us
    ppermute x20, waiting for transfers between devices, move(): return lax.ppermute(value, 'nodes', pairs)  11.9 us
    all_to_all x1, waiting for transfers between devices, on_device(): agg = lax.all_to_all(total, 'feat', 0, 0)  7.91 us
    all_to_all x1, waiting for transfers between devices, on_device(): received = lax.all_to_all(payload, 'feat', 0, 0)  5.35 us
    all_to_all x1, starting transfers between devices, on_device(): received = lax.all_to_all(payload, 'feat', 0, 0)  5.34 us
  transfers between devices with their start and end apart: 23, of which 4 were waited for; matrix products, arithmetic and copies ran while one was open for 2% of the time, Pallas kernels for 21%

profile of v6, /device:TPU:0, one launch (start us, length us, event | category | flops | bytes accessed | tf_op | source)
XLA Modules:
  0.0 125.1 jit_solution(10769866945389496987)
XLA Ops:
  0.6 1.7 %scale.1.refs_0_ = bf16[64,16,128]{2,1,0:T(8,128)(2,1)} custom-call(bf16[16,8192]{1,0:T(8,128)(2,1)} %bitcast.39, f32[64,128]{1,0:T(8,128)} %bitcast.26), custom_call_target="tpu_custom_call" | custom-call | tf_op jit(solution)/shard_map/scale/pallas_call | solution.py:420
  2.3 3.1 %collective-permute-start = (bf16[64,16,128]{2,1,0:T(8,128)(2,1)}, bf16[64,16,128]{2,1,0:T(8,128)(2,1)S(1)}, u32[]{:S(2)}, u32[]{:S(2)}) collective-permute-start(bf16[64,16,128]{2,1,0:T(8,128)(2,1)} %scale.1.refs_0_), channel_id=1, source_target_pairs={{0,64},{8,72},{16,80},{24,88},{32,96},{40,104},{48,112},{56,120},{... | collective-permute-start | bytes 786440 | tf_op jit(solution)/shard_map/ppermute | solution.py:418
  5.4 1.6 %collective-permute-start.1 = (bf16[64,16,128]{2,1,0:T(8,128)(2,1)}, bf16[64,16,128]{2,1,0:T(8,128)(2,1)S(1)}, u32[]{:S(2)}, u32[]{:S(2)}) collective-permute-start(bf16[64,16,128]{2,1,0:T(8,128)(2,1)} %scale.1.refs_0_), channel_id=1, source_target_pairs={{0,16},{8,24},{16,32},{24,40},{32,48},{40,56},{48,0},{56,8},{64,80... | collective-permute-start | bytes 786440 | tf_op jit(solution)/shard_map/ppermute | solution.py:418
  7.0 1.7 %collective-permute-start.2 = (bf16[64,16,128]{2,1,0:T(8,128)(2,1)}, bf16[64,16,128]{2,1,0:T(8,128)(2,1)S(1)}, u32[]{:S(2)}, u32[]{:S(2)}) collective-permute-start(bf16[64,16,128]{2,1,0:T(8,128)(2,1)} %scale.1.refs_0_), channel_id=1, source_target_pairs={{0,48},{8,56},{16,0},{24,8},{32,16},{40,24},{48,32},{56,40},{64,11... | collective-permute-start | bytes 786440 | tf_op jit(solution)/shard_map/ppermute | solution.py:418
  8.7 2.1 %payload.1 = bf16[8,10,32,128]{3,2,1,0:T(8,128)(2,1)} custom-call(bf16[32,8192]{1,0:T(8,128)(2,1)} %bitcast.37, bf16[16,256]{1,0:T(8,128)(2,1)} %weight.1, f32[1,32]{1,0:T(1,128)} %bitcast.40), custom_call_target="tpu_custom_call" | custom-call | tf_op jit(solution)/shard_map/payload/pallas_call | solution.py:425
  10.7 5.3 %all-to-all-start = ((bf16[8,10,32,128]{3,2,1,0:T(8,128)(2,1)}), bf16[8,10,32,128]{3,2,1,0:T(8,128)(2,1)S(1)}, u32[]{:S(2)}, u32[]{:S(2)}) async-start(bf16[8,10,32,128]{3,2,1,0:T(8,128)(2,1)} %payload.1), calls=%async_computation | async-start | bytes 1310720 | tf_op jit(solution)/shard_map/all_to_all | solution.py:435
  16.1 1.0 pad_maximum_fusion.1
  18.0 2.9 %collective-permute-start.4 = (bf16[64,16,128]{2,1,0:T(8,128)(2,1)S(1)}, bf16[64,16,128]{2,1,0:T(8,128)(2,1)S(1)}, u32[]{:S(2)}, u32[]{:S(2)}) collective-permute-start(bf16[64,16,128]{2,1,0:T(8,128)(2,1)S(1)} %collective-permute-done.refs_2_), channel_id=1, source_target_pairs={{0,48},{8,56},{16,0},{24,8},{32,16},{40,24},{48,32},{56,40},{64,11... | collective-permute-start | bytes 786440 | tf_op jit(solution)/shard_map/ppermute | solution.py:418
  20.8 5.4 %all-to-all-done.received = bf16[8,10,32,128]{3,2,1,0:T(8,128)(2,1)S(1)} async-done(((bf16[8,10,32,128]{3,2,1,0:T(8,128)(2,1)}), bf16[8,10,32,128]{3,2,1,0:T(8,128)(2,1)S(1)}, u32[]{:S(2)}, u32[]{:S(2)}) %all-to-all-start) | async-done | bytes 655392 | tf_op jit(solution)/shard_map/all_to_all | solution.py:435
  26.2 1.9 %collective-permute-start.5 = (bf16[64,16,128]{2,1,0:T(8,128)(2,1)}, bf16[64,16,128]{2,1,0:T(8,128)(2,1)S(1)}, u32[]{:S(2)}, u32[]{:S(2)}) collective-permute-start(bf16[64,16,128]{2,1,0:T(8,128)(2,1)} %scale.1.refs_0_), channel_id=1, source_target_pairs={{0,32},{8,40},{16,48},{24,56},{32,0},{40,8},{48,16},{56,24},{64,96... | collective-permute-start | bytes 786440 | tf_op jit(solution)/shard_map/ppermute | solution.py:418
  28.8 1.6 %collective-permute-start.6 = (bf16[64,16,128]{2,1,0:T(8,128)(2,1)S(1)}, bf16[64,16,128]{2,1,0:T(8,128)(2,1)S(1)}, u32[]{:S(2)}, u32[]{:S(2)}) collective-permute-start(bf16[64,16,128]{2,1,0:T(8,128)(2,1)S(1)} %collective-permute-done.refs_2_), channel_id=1, source_target_pairs={{0,32},{8,40},{16,48},{24,56},{32,0},{40,8},{48,16},{56,24},{64,96... | collective-permute-start | bytes 786440 | tf_op jit(solution)/shard_map/ppermute | solution.py:418
  33.0 0.9 copy-done.3
  33.9 5.9 %forward_tiles.3.refs_5_ = f32[64,16,128]{2,1,0:T(8,128)S(1)} custom-call(s32[18,32]{1,0:T(8,128)S(1)} %add_add_fusion.meta, bf16[64,16,128]{2,1,0:T(8,128)(2,1)S(1)} %copy-done, bf16[64,16,128]{2,1,0:T(8,128)(2,1)S(1)} %copy-done.3, bf16[64,16,128]{2,1,0:T(8,128)(2,1)S(1)} %collective-permute-done.refs_2_, ...), custom_call_target="tpu_custom_call" | custom-call | flops 67108864 | bytes 8388608 | tf_op jit(solution)/shard_map/forward_tiles/pallas_call | solution.py:171
  40.2 3.8 %forward_tiles.4.refs_2_ = f32[64,16,128]{2,1,0:T(8,128)S(1)} custom-call(s32[18,32]{1,0:T(8,128)S(1)} %add_add_fusion.meta, bf16[64,16,128]{2,1,0:T(8,128)(2,1)S(1)} %collective-permute-done.3.refs_0_, bf16[64,16,128]{2,1,0:T(8,128)(2,1)S(1)} %collective-permute-done.4.refs_1_, bf16[64,16,128]{2,1,0:T(8,128)(2,1)S(1)} %collective-permute-done.5.refs_2_, ...), custom_call_target="tpu_custom_call" | custom-call | flops 33554432 | bytes 4194304 | tf_op jit(solution)/shard_map/forward_tiles/pallas_call | solution.py:171
  44.0 4.2 %forward_tiles.5 = bf16[8,8,16,128]{3,2,1,0:T(8,128)(2,1)} custom-call(s32[18,32]{1,0:T(8,128)S(1)} %add_add_fusion.meta, bf16[4,64,16,128]{3,2,1,0:T(8,128)(2,1)S(1)} %collective-permute-done.9.refs_0_, bf16[16,32,128,128]{3,2,1,0:T(8,128)(2,1)} %bitcast.32, f32[64,16,128]{2,1,0:T(8,128)S(1)} %forward_tiles.4.refs_2_, f32[64,128]{1,0:T(8,128)S(1)} %bitcast.27), custom_call_target="tpu_custom_call" | custom-call | flops 33554432 | bytes 4194304 | tf_op jit(solution)/shard_map/forward_tiles/pallas_call | solution.py:171
  48.2 4.7 %all-to-all-start.1 = ((bf16[8,8,16,128]{3,2,1,0:T(8,128)(2,1)}), bf16[8,8,16,128]{3,2,1,0:T(8,128)(2,1)S(1)}, u32[]{:S(2)}, u32[]{:S(2)}) async-start(bf16[8,8,16,128]{3,2,1,0:T(8,128)(2,1)} %forward_tiles.5), calls=%async_computation.1 | async-start | bytes 524288 | tf_op jit(solution)/shard_map/all_to_all | solution.py:450
  52.9 7.9 %all-to-all-done.1.agg = bf16[8,8,16,128]{3,2,1,0:T(8,128)(2,1)S(1)} async-done(((bf16[8,8,16,128]{3,2,1,0:T(8,128)(2,1)}), bf16[8,8,16,128]{3,2,1,0:T(8,128)(2,1)S(1)}, u32[]{:S(2)}, u32[]{:S(2)}) %all-to-all-start.1) | async-done | bytes 262176 | tf_op jit(solution)/shard_map/all_to_all | solution.py:450
  60.8 2.2 %dense.1 = (bf16[8,14,16,128]{3,2,1,0:T(8,128)(2,1)S(1)}, bf16[8,8,32,128]{3,2,1,0:T(8,128)(2,1)}) custom-call(s32[1]{0:T(128)} %bitcast.place, bf16[8,8,16,128]{3,2,1,0:T(8,128)(2,1)S(1)} %all-to-all-done.1.agg, bf16[8,10,32,128]{3,2,1,0:T(8,128)(2,1)S(1)} %all-to-all-done.received, f32[64,128]{1,0:T(8,128)S(1)} %bitcast.28), custom_call_target="tpu_custom_call" | custom-call | tf_op jit(solution)/shard_map/dense/pallas_call | solution.py:451
  63.1 12.4 %all_to_all.20.refs_0_.back = bf16[8,14,16,128]{3,2,1,0:T(8,128)(2,1)S(1)} all-to-all(bf16[8,14,16,128]{3,2,1,0:T(8,128)(2,1)S(1)} %get-tuple-element.51), channel_id=1, replica_groups=mesh['nodes'=16,'feat'=8] {'feat'}, dimensions={0} | all-to-all | bytes 917504 | tf_op jit(solution)/shard_map/all_to_all | solution.py:460
  75.5 4.0 %backward_tiles.4 = bf16[4,8,128,128]{3,2,1,0:T(8,128)(2,1)S(1)} custom-call(s32[18,32]{1,0:T(8,128)S(1)} %add_add_fusion.meta, bf16[8,14,16,128]{3,2,1,0:T(8,128)(2,1)S(1)} %all_to_all.20.refs_0_.back, bf16[16,32,128,128]{3,2,1,0:T(8,128)(2,1)} %bitcast.33), custom_call_target="tpu_custom_call" | custom-call | flops 33554432 | bytes 4194304 | tf_op jit(solution)/shard_map/backward_tiles/pallas_call | solution.py:286
  80.3 4.2 %backward_tiles.5 = bf16[4,8,128,128]{3,2,1,0:T(8,128)(2,1)S(1)} custom-call(s32[18,32]{1,0:T(8,128)S(1)} %add_add_fusion.meta, bf16[8,14,16,128]{3,2,1,0:T(8,128)(2,1)S(1)} %all_to_all.20.refs_0_.back, bf16[16,32,128,128]{3,2,1,0:T(8,128)(2,1)} %bitcast.34), custom_call_target="tpu_custom_call" | custom-call | flops 33554432 | bytes 4194304 | tf_op jit(solution)/shard_map/backward_tiles/pallas_call | solution.py:286
  84.7 4.5 %backward_tiles.6 = (bf16[9,128,128]{2,1,0:T(8,128)(2,1)S(1)}, bf16[9,128,128]{2,1,0:T(8,128)(2,1)}, bf16[9,128,128]{2,1,0:T(8,128)(2,1)S(1)}, bf16[9,128,128]{2,1,0:T(8,128)(2,1)S(1)}) custom-call(s32[18,32]{1,0:T(8,128)S(1)} %add_add_fusion.meta, bf16[8,14,16,128]{3,2,1,0:T(8,128)(2,1)S(1)} %all_to_all.20.refs_0_.back, ...), custom_call_target="tpu_custom_call" | custom-call | flops 33554432 | bytes 4194304 | tf_op jit(solution)/shard_map/backward_tiles/pallas_call | solution.py:286
  89.3 3.2 %collective-permute-start.16 = (bf16[9,128,128]{2,1,0:T(8,128)(2,1)S(1)}, bf16[9,128,128]{2,1,0:T(8,128)(2,1)S(1)}, u32[]{:S(2)}, u32[]{:S(2)}) collective-permute-start(bf16[9,128,128]{2,1,0:T(8,128)(2,1)S(1)} %get-tuple-element.63), channel_id=1, source_target_pairs={{0,48},{8,56},{16,0},{24,8},{32,16},{40,24},{48,32},{56,40},{64,11... | collective-permute-start | bytes 884744 | tf_op jit(solution)/shard_map/ppermute | solution.py:418
  92.9 4.5 %backward_tiles.7 = (f32[64,16,128]{2,1,0:T(8,128)S(1)}, bf16[8,128,128]{2,1,0:T(8,128)(2,1)S(1)}, bf16[8,128,128]{2,1,0:T(8,128)(2,1)S(1)}, bf16[8,128,128]{2,1,0:T(8,128)(2,1)}) custom-call(s32[18,32]{1,0:T(8,128)S(1)} %add_add_fusion.meta, bf16[8,14,16,128]{3,2,1,0:T(8,128)(2,1)S(1)} %all_to_all.20.refs_0_.back, bf16[16,32,128,128]{3,2,1,0:T(8,128)(2,1)} %bitcast.36, ...), custom_call_target="tpu_custom_call" | custom-call | flops 33554432 | bytes 4194304 | tf_op jit(solution)/shard_map/backward_tiles/pallas_call | solution.py:286
  98.1 3.4 %collective-permute-start.18 = (bf16[8,128,128]{2,1,0:T(8,128)(2,1)}, bf16[8,128,128]{2,1,0:T(8,128)(2,1)S(1)}, u32[]{:S(2)}, u32[]{:S(2)}) collective-permute-start(bf16[8,128,128]{2,1,0:T(8,128)(2,1)} %get-tuple-element.65), channel_id=1, source_target_pairs={{0,32},{8,40},{16,48},{24,56},{32,0},{40,8},{48,16},{56,24},{64,96... | collective-permute-start | bytes 786440 | tf_op jit(solution)/shard_map/ppermute | solution.py:418
  101.5 3.5 %all-to-all-start.3 = ((bf16[8,8,32,128]{3,2,1,0:T(8,128)(2,1)}), bf16[8,8,32,128]{3,2,1,0:T(8,128)(2,1)S(1)}, u32[]{:S(2)}, u32[]{:S(2)}) async-start(bf16[8,8,32,128]{3,2,1,0:T(8,128)(2,1)} %get-tuple-element.59), calls=%async_computation.3 | async-start | bytes 1048576 | tf_op jit(solution)/shard_map/all_to_all | solution.py:487
  105.0 6.5 %collective-permute-done.15.down = bf16[9,128,128]{2,1,0:T(8,128)(2,1)S(1)} collective-permute-done((bf16[9,128,128]{2,1,0:T(8,128)(2,1)}, bf16[9,128,128]{2,1,0:T(8,128)(2,1)S(1)}, u32[]{:S(2)}, u32[]{:S(2)}) %collective-permute-start.15) | collective-permute-done | bytes 294944 | tf_op jit(solution)/shard_map/ppermute | solution.py:418
  111.7 2.5 %collective-permute-start.19 = (bf16[9,128,128]{2,1,0:T(8,128)(2,1)S(1)}, bf16[9,128,128]{2,1,0:T(8,128)(2,1)S(1)}, u32[]{:S(2)}, u32[]{:S(2)}) collective-permute-start(bf16[9,128,128]{2,1,0:T(8,128)(2,1)S(1)} %cross.1.sent), channel_id=1, source_target_pairs={{0,64},{8,72},{16,80},{24,88},{32,96},{40,104},{48,112},{56,120},{... | collective-permute-start | bytes 884744 | tf_op jit(solution)/shard_map/ppermute | solution.py:418
  114.1 1.0 collective-permute-start.13
  115.2 2.2 %collective-permute-start.14 = (bf16[8,128,128]{2,1,0:T(8,128)(2,1)S(1)}, bf16[8,128,128]{2,1,0:T(8,128)(2,1)S(1)}, u32[]{:S(2)}, u32[]{:S(2)}) collective-permute-start(bf16[8,128,128]{2,1,0:T(8,128)(2,1)S(1)} %get-tuple-element.62), channel_id=1, source_target_pairs={{0,48},{8,56},{16,0},{24,8},{32,16},{40,24},{48,32},{56,40},{64,11... | collective-permute-start | bytes 786440 | tf_op jit(solution)/shard_map/ppermute | solution.py:418
  118.3 5.4 %collective-permute-done.13.down = bf16[8,128,128]{2,1,0:T(8,128)(2,1)S(1)} collective-permute-done((bf16[8,128,128]{2,1,0:T(8,128)(2,1)}, bf16[8,128,128]{2,1,0:T(8,128)(2,1)S(1)}, u32[]{:S(2)}, u32[]{:S(2)}) %collective-permute-start.13) | collective-permute-done | bytes 262176 | tf_op jit(solution)/shard_map/ppermute | solution.py:418
  123.7 1.4 %finish.1 = (f32[16,8192]{1,0:T(8,128)}, f32[16,256]{1,0:T(8,128)}, f32[1,32]{1,0:T(1,128)}) custom-call(s32[1]{0:T(128)} %bitcast.place, f32[64,16,128]{2,1,0:T(8,128)S(1)} %get-tuple-element.61.kept, f32[64,128]{1,0:T(8,128)S(1)} %bitcast.29, bf16[8,128,128]{2,1,0:T(8,128)(2,1)S(1)} %collective-permute-done.13.down, ...), custom_call_target="tpu_custom_call" | custom-call | tf_op jit(solution)/shard_map/finish/pallas_call | solution.py:489
  (45 shorter events, 7.4 us)
Async XLA Ops:
  2.3 13.7 %collective-permute-start = (bf16[64,16,128]{2,1,0:T(8,128)(2,1)}, bf16[64,16,128]{2,1,0:T(8,128)(2,1)S(1)}, u32[]{:S(2)}, u32[]{:S(2)}) collective-permute-start(bf16[64,16,128]{2,1,0:T(8,128)(2,1)} %scale.1.refs_0_), channel_id=1, source_target_pairs={{0,64},{8,72},{16,80},{24,88},{32,96},{40,104},{48,112},{56,120},{... | collective-permute-start | bytes 786440 | tf_op jit(solution)/shard_map/ppermute | solution.py:418
  5.4 10.6 %collective-permute-start.1 = (bf16[64,16,128]{2,1,0:T(8,128)(2,1)}, bf16[64,16,128]{2,1,0:T(8,128)(2,1)S(1)}, u32[]{:S(2)}, u32[]{:S(2)}) collective-permute-start(bf16[64,16,128]{2,1,0:T(8,128)(2,1)} %scale.1.refs_0_), channel_id=1, source_target_pairs={{0,16},{8,24},{16,32},{24,40},{32,48},{40,56},{48,0},{56,8},{64,80... | collective-permute-start | bytes 786440 | tf_op jit(solution)/shard_map/ppermute | solution.py:418
  7.0 9.1 %collective-permute-start.2 = (bf16[64,16,128]{2,1,0:T(8,128)(2,1)}, bf16[64,16,128]{2,1,0:T(8,128)(2,1)S(1)}, u32[]{:S(2)}, u32[]{:S(2)}) collective-permute-start(bf16[64,16,128]{2,1,0:T(8,128)(2,1)} %scale.1.refs_0_), channel_id=1, source_target_pairs={{0,48},{8,56},{16,0},{24,8},{32,16},{40,24},{48,32},{56,40},{64,11... | collective-permute-start | bytes 786440 | tf_op jit(solution)/shard_map/ppermute | solution.py:418
  10.7 15.5 %all-to-all-start = ((bf16[8,10,32,128]{3,2,1,0:T(8,128)(2,1)}), bf16[8,10,32,128]{3,2,1,0:T(8,128)(2,1)S(1)}, u32[]{:S(2)}, u32[]{:S(2)}) async-start(bf16[8,10,32,128]{3,2,1,0:T(8,128)(2,1)} %payload.1), calls=%async_computation | async-start | bytes 1310720 | tf_op jit(solution)/shard_map/all_to_all | solution.py:435
  17.1 14.9 %collective-permute-start.8 = (bf16[3,64,16,128]{3,2,1,0:T(8,128)(2,1)}, bf16[3,64,16,128]{3,2,1,0:T(8,128)(2,1)S(1)}, u32[]{:S(2)}, u32[]{:S(2)}) collective-permute-start(bf16[3,64,16,128]{3,2,1,0:T(8,128)(2,1)} %pad_maximum_fusion.1), channel_id=1, source_target_pairs={{0,8},{8,0},{16,24},{24,16},{32,40},{40,32},{48,56},{56,48},{64,72... | collective-permute-start | bytes 2359304 | tf_op jit(solution)/shard_map/ppermute | solution.py:418
  17.1 11.0 %collective-permute-start.7 = (bf16[64,16,128]{2,1,0:T(8,128)(2,1)}, bf16[64,16,128]{2,1,0:T(8,128)(2,1)S(1)}, u32[]{:S(2)}, u32[]{:S(2)}) collective-permute-start(bf16[64,16,128]{2,1,0:T(8,128)(2,1)} %scale.1.refs_0_), channel_id=1, source_target_pairs={{0,8},{8,0},{16,24},{24,16},{32,40},{40,32},{48,56},{56,48},{64,72... | collective-permute-start | bytes 786440 | tf_op jit(solution)/shard_map/ppermute | solution.py:418
  17.6 22.3 %collective-permute-start.3 = (bf16[64,16,128]{2,1,0:T(8,128)(2,1)S(1)}, bf16[64,16,128]{2,1,0:T(8,128)(2,1)S(1)}, u32[]{:S(2)}, u32[]{:S(2)}) collective-permute-start(bf16[64,16,128]{2,1,0:T(8,128)(2,1)S(1)} %collective-permute-done.refs_2_), channel_id=1, source_target_pairs={{0,16},{8,24},{16,32},{24,40},{32,48},{40,56},{48,0},{56,8},{64,80... | collective-permute-start | bytes 786440 | tf_op jit(solution)/shard_map/ppermute | solution.py:418
  18.0 21.9 %collective-permute-start.4 = (bf16[64,16,128]{2,1,0:T(8,128)(2,1)S(1)}, bf16[64,16,128]{2,1,0:T(8,128)(2,1)S(1)}, u32[]{:S(2)}, u32[]{:S(2)}) collective-permute-start(bf16[64,16,128]{2,1,0:T(8,128)(2,1)S(1)} %collective-permute-done.refs_2_), channel_id=1, source_target_pairs={{0,48},{8,56},{16,0},{24,8},{32,16},{40,24},{48,32},{56,40},{64,11... | collective-permute-start | bytes 786440 | tf_op jit(solution)/shard_map/ppermute | solution.py:418
  26.2 13.7 %collective-permute-start.5 = (bf16[64,16,128]{2,1,0:T(8,128)(2,1)}, bf16[64,16,128]{2,1,0:T(8,128)(2,1)S(1)}, u32[]{:S(2)}, u32[]{:S(2)}) collective-permute-start(bf16[64,16,128]{2,1,0:T(8,128)(2,1)} %scale.1.refs_0_), channel_id=1, source_target_pairs={{0,32},{8,40},{16,48},{24,56},{32,0},{40,8},{48,16},{56,24},{64,96... | collective-permute-start | bytes 786440 | tf_op jit(solution)/shard_map/ppermute | solution.py:418
  28.1 0.7 copy-start.2
  28.8 11.1 %collective-permute-start.6 = (bf16[64,16,128]{2,1,0:T(8,128)(2,1)S(1)}, bf16[64,16,128]{2,1,0:T(8,128)(2,1)S(1)}, u32[]{:S(2)}, u32[]{:S(2)}) collective-permute-start(bf16[64,16,128]{2,1,0:T(8,128)(2,1)S(1)} %collective-permute-done.refs_2_), channel_id=1, source_target_pairs={{0,32},{8,40},{16,48},{24,56},{32,0},{40,8},{48,16},{56,24},{64,96... | collective-permute-start | bytes 786440 | tf_op jit(solution)/shard_map/ppermute | solution.py:418
  32.0 1.0 copy-start
  33.0 0.9 copy-start.3
  33.9 10.0 %copy-start.1 = (f32[8192]{0:T(1024)S(1)}, f32[8192]{0:T(1024)}, u32[]{:S(2)}) copy-start(f32[8192]{0:T(1024)} %param.14) | copy-start | bytes 98308
  40.1 3.9 %collective-permute-start.9 = (bf16[4,64,16,128]{3,2,1,0:T(8,128)(2,1)S(1)}, bf16[4,64,16,128]{3,2,1,0:T(8,128)(2,1)S(1)}, u32[]{:S(2)}, u32[]{:S(2)}) collective-permute-start(bf16[4,64,16,128]{3,2,1,0:T(8,128)(2,1)S(1)} %pad_maximum_fusion), channel_id=1, source_target_pairs={{0,8},{8,0},{16,24},{24,16},{32,40},{40,32},{48,56},{56,48},{64,72... | collective-permute-start | bytes 3145736 | tf_op jit(solution)/shard_map/ppermute | solution.py:418
  48.2 12.7 %all-to-all-start.1 = ((bf16[8,8,16,128]{3,2,1,0:T(8,128)(2,1)}), bf16[8,8,16,128]{3,2,1,0:T(8,128)(2,1)S(1)}, u32[]{:S(2)}, u32[]{:S(2)}) async-start(bf16[8,8,16,128]{3,2,1,0:T(8,128)(2,1)} %forward_tiles.5), calls=%async_computation.1 | async-start | bytes 524288 | tf_op jit(solution)/shard_map/all_to_all | solution.py:450
  79.6 4.9 %collective-permute-start.10 = (bf16[4,8,128,128]{3,2,1,0:T(8,128)(2,1)S(1)}, bf16[4,8,128,128]{3,2,1,0:T(8,128)(2,1)S(1)}, u32[]{:S(2)}, u32[]{:S(2)}) collective-permute-start(bf16[4,8,128,128]{3,2,1,0:T(8,128)(2,1)S(1)} %backward_tiles.4), channel_id=1, source_target_pairs={{0,8},{8,0},{16,24},{24,16},{32,40},{40,32},{48,56},{56,48},{64,72... | collective-permute-start | bytes 3145736 | tf_op jit(solution)/shard_map/ppermute | solution.py:418
  79.7 4.8 %collective-permute-start.11 = (f32[64,128]{1,0:T(8,128)S(1)}, f32[64,128]{1,0:T(8,128)S(1)}, u32[]{:S(2)}, u32[]{:S(2)}) collective-permute-start(f32[64,128]{1,0:T(8,128)S(1)} %weight_sums.1), channel_id=1, source_target_pairs={{0,8},{8,0},{16,24},{24,16},{32,40},{40,32},{48,56},{56,48},{64,72... | collective-permute-start | bytes 98312 | tf_op jit(solution)/shard_map/ppermute | solution.py:418
  84.5 8.3 %collective-permute-start.12 = (bf16[4,8,128,128]{3,2,1,0:T(8,128)(2,1)S(1)}, bf16[4,8,128,128]{3,2,1,0:T(8,128)(2,1)S(1)}, u32[]{:S(2)}, u32[]{:S(2)}) collective-permute-start(bf16[4,8,128,128]{3,2,1,0:T(8,128)(2,1)S(1)} %backward_tiles.5), channel_id=1, source_target_pairs={{0,8},{8,0},{16,24},{24,16},{32,40},{40,32},{48,56},{56,48},{64,72... | collective-permute-start | bytes 3145736 | tf_op jit(solution)/shard_map/ppermute | solution.py:418
  89.2 22.3 %collective-permute-start.15 = (bf16[9,128,128]{2,1,0:T(8,128)(2,1)}, bf16[9,128,128]{2,1,0:T(8,128)(2,1)S(1)}, u32[]{:S(2)}, u32[]{:S(2)}) collective-permute-start(bf16[9,128,128]{2,1,0:T(8,128)(2,1)} %get-tuple-element.56), channel_id=1, source_target_pairs={{0,16},{8,24},{16,32},{24,40},{32,48},{40,56},{48,0},{56,8},{64,80... | collective-permute-start | bytes 884744 | tf_op jit(solution)/shard_map/ppermute | solution.py:418
  89.3 22.2 %collective-permute-start.16 = (bf16[9,128,128]{2,1,0:T(8,128)(2,1)S(1)}, bf16[9,128,128]{2,1,0:T(8,128)(2,1)S(1)}, u32[]{:S(2)}, u32[]{:S(2)}) collective-permute-start(bf16[9,128,128]{2,1,0:T(8,128)(2,1)S(1)} %get-tuple-element.63), channel_id=1, source_target_pairs={{0,48},{8,56},{16,0},{24,8},{32,16},{40,24},{48,32},{56,40},{64,11... | collective-permute-start | bytes 884744 | tf_op jit(solution)/shard_map/ppermute | solution.py:418
  92.5 19.0 %collective-permute-start.17 = (bf16[9,128,128]{2,1,0:T(8,128)(2,1)S(1)}, bf16[9,128,128]{2,1,0:T(8,128)(2,1)S(1)}, u32[]{:S(2)}, u32[]{:S(2)}) collective-permute-start(bf16[9,128,128]{2,1,0:T(8,128)(2,1)S(1)} %get-tuple-element.64), channel_id=1, source_target_pairs={{0,32},{8,40},{16,48},{24,56},{32,0},{40,8},{48,16},{56,24},{64,96... | collective-permute-start | bytes 884744 | tf_op jit(solution)/shard_map/ppermute | solution.py:418
  97.4 0.7 copy-start.4
  98.1 13.4 %collective-permute-start.18 = (bf16[8,128,128]{2,1,0:T(8,128)(2,1)}, bf16[8,128,128]{2,1,0:T(8,128)(2,1)S(1)}, u32[]{:S(2)}, u32[]{:S(2)}) collective-permute-start(bf16[8,128,128]{2,1,0:T(8,128)(2,1)} %get-tuple-element.65), channel_id=1, source_target_pairs={{0,32},{8,40},{16,48},{24,56},{32,0},{40,8},{48,16},{56,24},{64,96... | collective-permute-start | bytes 786440 | tf_op jit(solution)/shard_map/ppermute | solution.py:418
  101.5 15.9 %all-to-all-start.3 = ((bf16[8,8,32,128]{3,2,1,0:T(8,128)(2,1)}), bf16[8,8,32,128]{3,2,1,0:T(8,128)(2,1)S(1)}, u32[]{:S(2)}, u32[]{:S(2)}) async-start(bf16[8,8,32,128]{3,2,1,0:T(8,128)(2,1)} %get-tuple-element.59), calls=%async_computation.3 | async-start | bytes 1048576 | tf_op jit(solution)/shard_map/all_to_all | solution.py:487
  111.7 12.0 %collective-permute-start.19 = (bf16[9,128,128]{2,1,0:T(8,128)(2,1)S(1)}, bf16[9,128,128]{2,1,0:T(8,128)(2,1)S(1)}, u32[]{:S(2)}, u32[]{:S(2)}) collective-permute-start(bf16[9,128,128]{2,1,0:T(8,128)(2,1)S(1)} %cross.1.sent), channel_id=1, source_target_pairs={{0,64},{8,72},{16,80},{24,88},{32,96},{40,104},{48,112},{56,120},{... | collective-permute-start | bytes 884744 | tf_op jit(solution)/shard_map/ppermute | solution.py:418
  114.1 9.5 %collective-permute-start.13 = (bf16[8,128,128]{2,1,0:T(8,128)(2,1)}, bf16[8,128,128]{2,1,0:T(8,128)(2,1)S(1)}, u32[]{:S(2)}, u32[]{:S(2)}) collective-permute-start(bf16[8,128,128]{2,1,0:T(8,128)(2,1)} %copy-done.4), channel_id=1, source_target_pairs={{0,16},{8,24},{16,32},{24,40},{32,48},{40,56},{48,0},{56,8},{64,80... | collective-permute-start | bytes 786440 | tf_op jit(solution)/shard_map/ppermute | solution.py:418
  115.2 8.5 %collective-permute-start.14 = (bf16[8,128,128]{2,1,0:T(8,128)(2,1)S(1)}, bf16[8,128,128]{2,1,0:T(8,128)(2,1)S(1)}, u32[]{:S(2)}, u32[]{:S(2)}) collective-permute-start(bf16[8,128,128]{2,1,0:T(8,128)(2,1)S(1)} %get-tuple-element.62), channel_id=1, source_target_pairs={{0,48},{8,56},{16,0},{24,8},{32,16},{40,24},{48,32},{56,40},{64,11... | collective-permute-start | bytes 786440 | tf_op jit(solution)/shard_map/ppermute | solution.py:418
